TPU v7x, 256 devices: a whole 4x4x8 slice. The times are simulated.
256 devices in a mesh: seq: 8 (over z), dp: 32 (over y, x, core).
Axes of the slice: x: 4, y: 4, z: 8, core: 2. Of those that a mesh axis runs over, the one named last changes fastest.
Arguments:
- frames: bfloat16 [32, 64, 8, 32, 128], P('dp', 'seq'), may hold values from -6 to 6
- clip_ids: int32 [32, 64], P('dp'), may hold values from 0 to 8, never falling along the last dimension, each value on 1 to 20 neighbouring positions
- cotangent: bfloat16 [32, 64, 8, 32, 128], P('dp', 'seq'), may hold values from -6 to 6
- conv1_weight: bfloat16 [3456, 128], replicated, may hold values from -0.109375 to 0.109375
- conv2_weight: bfloat16 [3456, 128], replicated, may hold values from -0.109375 to 0.109375
Outputs:
- block_out: bfloat16 [32, 64, 8, 32, 128], P('dp', 'seq')
- input_grad: bfloat16 [32, 64, 8, 32, 128], P('dp', 'seq')
- conv1_grad: float32 [3456, 128], P('dp')
- conv2_grad: float32 [3456, 128], P('dp')
Inputs may be any that keep to these rules, and one draw needn't show every extreme that they name: `clip_ids`: in each row the clip numbers never fall; each clip covers 1 to 20 consecutive frames, and one covers exactly that many.
All inputs are finite; a program needn't handle non-finite values.
Results may differ from a plain program's by a relative error of at most 0.0055.
Values may be sent and summed in bfloat16 or wider, within the bound.
No kernel may reach another device: no remote copies, remote signals or barrier semaphores. Data moves between devices by JAX's collectives and lax.ppermute only.
A program may use at most 128 MiB of HBM per device.

v0:
```python
import functools

import jax
import jax.numpy as jnp
from jax import lax
from jax.experimental import pallas as pl
from jax.experimental.pallas import tpu as pltpu
from jax.sharding import PartitionSpec as P

C = 128
GROUP = 4
F = 8
HT = 8
WT = 32
POS = HT * WT
NONE = F + 2
BF16 = jnp.bfloat16
F32 = jnp.float32
VMEM_LIMIT = 56 * 1024 * 1024


def column(rows):
    return lax.broadcasted_iota(jnp.int32, (rows, C), 0) % WT


def shift_down(value):
    return jnp.where(column(POS) == 0, 0.0, pltpu.roll(value, 1, 0))


def shift_up(value):
    return jnp.where(column(POS) == WT - 1, 0.0, pltpu.roll(value, POS - 1, 0))


def row_pieces(frame):
    edge = jnp.zeros((WT, C), frame.dtype)
    return [
        jnp.concatenate([edge, frame[: POS - WT]], axis=0),
        frame,
        jnp.concatenate([frame[WT:], edge], axis=0),
    ]


def conv_frame(window, slots, weight):
    pieces = []
    for slot in slots:
        pieces += row_pieces(window[slot])
    taps = jnp.dot(jnp.concatenate(pieces, axis=1), weight[...], preferred_element_type=F32)
    return shift_down(taps[:, :C]) + taps[:, C : 2 * C] + shift_up(taps[:, 2 * C :])


def forward_weight(weight_ref, out_ref):
    for outer in range(9):
        for b in range(3):
            out_ref[outer * C : (outer + 1) * C, b * C : (b + 1) * C] = weight_ref[
                (outer * 3 + b) * C : (outer * 3 + b + 1) * C, :
            ]


def adjoint_weight(weight_ref, out_ref):
    for outer in range(9):
        for b in range(3):
            tap = 26 - (outer * 3 + b)
            out_ref[outer * C : (outer + 1) * C, b * C : (b + 1) * C] = weight_ref[
                tap * C : (tap + 1) * C, :
            ].T


def group_mean(sums):
    lane = lax.broadcasted_iota(jnp.int32, sums.shape, 1)
    pairs = sums + jnp.where(lane % 2 == 0, pltpu.roll(sums, C - 1, 1), pltpu.roll(sums, 1, 1))
    quads = pairs + jnp.where(lane % 4 < 2, pltpu.roll(pairs, C - 2, 1), pltpu.roll(pairs, 2, 1))
    return quads * (1.0 / (GROUP * POS))


def main_kernel(
    core_ref,
    past_ref,
    next_ref,
    frames_ref,
    cache_ref,
    cot_ref,
    cot_next_ref,
    weight1_ref,
    weight2_ref,
    hidden_ref,
    act_grad_ref,
    keep_ref,
    send_ref,
    window,
    cot_window,
    conv_weight,
    back_weight,
    act,
    slope,
    cot_shifted,
    cot_taps,
    frame_t,
    frame_taps,
    hidden_t,
    grad_shifted,
    grads,
):
    zero = jnp.zeros((POS, C), BF16)
    for f in range(2):
        window[f] = cache_ref[f]
        cot_window[F + f] = cot_next_ref[f]
    for f in range(F):
        window[2 + f] = frames_ref[f]
        cot_window[f] = cot_ref[f]
    window[NONE] = zero
    cot_window[NONE] = zero
    forward_weight(weight1_ref, conv_weight)
    adjoint_weight(weight2_ref, back_weight)

    sums = []
    for t in range(F):
        out = conv_frame(window, [past_ref[t, k] for k in range(3)], conv_weight)
        act[t] = out
        sums.append(jnp.sum(out, axis=0, keepdims=True))
    center = group_mean(jnp.concatenate(sums, axis=0))
    sums = []
    for t in range(F):
        away = act[t] - center[t : t + 1]
        sums.append(jnp.sum(away * away, axis=0, keepdims=True))
    scale = lax.rsqrt(group_mean(jnp.concatenate(sums, axis=0)) + 1e-06)
    for t in range(F):
        normed = (act[t] - center[t : t + 1]) * scale[t : t + 1]
        gate = 1.0 / (1.0 + jnp.exp(-normed))
        hidden = (normed * gate).astype(BF16)
        hidden_ref[t] = hidden
        act[t] = normed
        slope[t] = gate * (1.0 + normed * (1.0 - gate))
        for a, piece in enumerate(row_pieces(hidden)):
            hidden_t[a * C : (a + 1) * C, t * POS : (t + 1) * POS] = piece.T

    first, second = [], []
    for t in range(F):
        grad = conv_frame(cot_window, [next_ref[t, q] for q in range(3)], back_weight) * slope[t]
        slope[t] = grad
        first.append(jnp.sum(grad, axis=0, keepdims=True))
        second.append(jnp.sum(grad * act[t], axis=0, keepdims=True))
    first = group_mean(jnp.concatenate(first, axis=0))
    second = group_mean(jnp.concatenate(second, axis=0))
    for t in range(F):
        grad = scale[t : t + 1] * (slope[t] - first[t : t + 1] - act[t] * second[t : t + 1])
        rounded = grad.astype(BF16)
        act_grad_ref[t] = rounded
        wide = rounded.astype(F32)
        grad_shifted[t * POS : (t + 1) * POS, :C] = shift_up(wide).astype(BF16)
        grad_shifted[t * POS : (t + 1) * POS, C : 2 * C] = rounded
        grad_shifted[t * POS : (t + 1) * POS, 2 * C :] = shift_down(wide).astype(BF16)

    for f in range(F + 2):
        wide = cot_window[f].astype(F32)
        cot_shifted[f, :, :C] = shift_up(wide).astype(BF16)
        cot_shifted[f, :, C : 2 * C] = cot_window[f]
        cot_shifted[f, :, 2 * C :] = shift_down(wide).astype(BF16)
    cot_shifted[NONE] = jnp.zeros((POS, 3 * C), BF16)
    for s in range(F):
        for k in range(3):
            cot_taps[s * POS : (s + 1) * POS, 3 * C * k : 3 * C * (k + 1)] = cot_shifted[
                next_ref[s, 2 - k]
            ]
    second_grad = jnp.dot(hidden_t[...], cot_taps[...], preferred_element_type=F32)
    for k in range(3):
        for a in range(3):
            for b in range(3):
                tap = (k * 3 + a) * 3 + b
                grads[1, tap * C : (tap + 1) * C] = second_grad[
                    a * C : (a + 1) * C, (k * 3 + b) * C : (k * 3 + b + 1) * C
                ]

    for f in range(F + 2):
        for a, piece in enumerate(row_pieces(window[f])):
            frame_t[f, a * C : (a + 1) * C, :] = piece.T
    frame_t[NONE] = jnp.zeros((3 * C, POS), BF16)
    for t in range(F):
        for k in range(3):
            frame_taps[3 * C * k : 3 * C * (k + 1), t * POS : (t + 1) * POS] = frame_t[
                past_ref[t, k]
            ]
    first_grad = jnp.dot(frame_taps[...], grad_shifted[...], preferred_element_type=F32)
    for outer in range(9):
        for b in range(3):
            tap = outer * 3 + b
            grads[0, tap * C : (tap + 1) * C] = first_grad[
                outer * C : (outer + 1) * C, b * C : (b + 1) * C
            ]

    own = core_ref[0] == 0
    for g in range(2):
        for m in range(16):
            low = grads[g, 216 * m : 216 * m + 108]
            high = grads[g, 216 * m + 108 : 216 * m + 216]
            keep_ref[g, m] = jnp.where(own, low, high)
            send_ref[g, m] = jnp.where(own, high, low).astype(BF16)


def conv_kernel(adjoint, slot_ref, frames_ref, cache_ref, weight_ref, base_ref, out_ref, window, weight):
    for f in range(2):
        window[F + f if adjoint else f] = cache_ref[f]
    for f in range(F):
        window[f if adjoint else 2 + f] = frames_ref[f]
    window[NONE] = jnp.zeros((POS, C), BF16)
    (adjoint_weight if adjoint else forward_weight)(weight_ref, weight)
    for t in range(F):
        out = conv_frame(window, [slot_ref[t, k] for k in range(3)], weight)
        out_ref[t] = (base_ref[t].astype(F32) + out).astype(BF16)


def add_kernel(own_ref, keep_ref, *refs):
    received, (kept_ref, *sent_refs) = refs[:-4], refs[-4:]
    own = own_ref[0]
    outer = keep_ref.shape[1]
    for g in range(2):
        for m in range(outer):
            for step in range(4):
                block = lax.rem(own + step, 4)
                total = keep_ref[g, m, block]
                for part in received:
                    total = total + part[g, m, block].astype(F32)
                if step == 0:
                    kept_ref[g, m] = total
                else:
                    sent_refs[step - 1][g, m] = total.astype(BF16)


SMEM = pl.BlockSpec(memory_space=pltpu.SMEM)
VMEM = pl.BlockSpec(memory_space=pltpu.VMEM)


def call(kernel, operands, scalars, outs, scratch=(), flops=0, moved=0):
    return pl.pallas_call(
        kernel,
        out_shape=[jax.ShapeDtypeStruct(shape, dtype) for shape, dtype in outs],
        in_specs=[SMEM] * scalars + [VMEM] * (len(operands) - scalars),
        out_specs=[VMEM] * len(outs),
        scratch_shapes=[pltpu.VMEM(shape, dtype) for shape, dtype in scratch],
        compiler_params=pltpu.CompilerParams(vmem_limit_bytes=VMEM_LIMIT),
        cost_estimate=pl.CostEstimate(flops=flops, bytes_accessed=moved, transcendentals=0),
    )(*operands)


CONV_FLOPS = 2 * F * POS * 27 * C * C


def main(core, past, following, frames, cache, cot, cot_next, weight1, weight2):
    return call(
        main_kernel,
        (core, past, following, frames, cache, cot, cot_next, weight1, weight2),
        3,
        [
            ((F, POS, C), BF16),
            ((F, POS, C), BF16),
            ((2, 16, 108, C), F32),
            ((2, 16, 108, C), BF16),
        ],
        [
            ((F + 3, POS, C), BF16),
            ((F + 3, POS, C), BF16),
            ((9 * C, 3 * C), BF16),
            ((9 * C, 3 * C), BF16),
            ((F, POS, C), F32),
            ((F, POS, C), F32),
            ((F + 3, POS, 3 * C), BF16),
            ((F * POS, 9 * C), BF16),
            ((F + 3, 3 * C, POS), BF16),
            ((9 * C, F * POS), BF16),
            ((3 * C, F * POS), BF16),
            ((F * POS, 3 * C), BF16),
            ((2, 27 * C, C), F32),
        ],
        flops=4 * CONV_FLOPS,
        moved=9 << 20,
    )


def conv(adjoint, slots, frames, cache, weight, base):
    return call(
        functools.partial(conv_kernel, adjoint),
        (slots, frames, cache, weight, base),
        1,
        [((F, POS, C), BF16)],
        [((F + 3, POS, C), BF16), ((9 * C, 3 * C), BF16)],
        flops=CONV_FLOPS,
        moved=3 << 20,
    )[0]


def add_stage(own, keep, received, outer):
    return call(
        add_kernel,
        (own, keep, *received),
        1,
        [((2, outer, 108, C), F32)] + [((2, outer, 108, C), BF16)] * 3,
        flops=0,
        moved=2 << 20,
    )


def shifted(value, steps):
    count = lax.axis_size("seq")
    first, last = (max(0, -steps), min(count, count - steps))
    return lax.ppermute(value, "seq", [(source, source + steps) for source in range(first, last)])


def dp_permute(value, target):
    return lax.ppermute(value, "dp", [(source, target(source)) for source in range(32)])


def slot_tables(clips, first_frame):
    padded = jnp.concatenate(
        [jnp.full((2,), -1, jnp.int32), clips, jnp.full((2,), -1, jnp.int32)]
    )
    near = lax.dynamic_slice_in_dim(padded, first_frame, F + 4)
    frame = jnp.arange(F, dtype=jnp.int32)
    current = near[2 : 2 + F]
    past = jnp.stack(
        [jnp.where(near[k : k + F] == current, frame + k, NONE) for k in range(3)], axis=1
    )
    following = jnp.stack(
        [jnp.where(near[2 + q : 2 + q + F] == current, frame + q, NONE) for q in range(3)], axis=1
    )
    return past, following


def per_device(frames, clip_ids, cotangent, conv1_weight, conv2_weight):
    own_frames = frames.reshape(F, POS, C)
    own_cot = cotangent.reshape(F, POS, C)
    index = lax.axis_index("dp")
    core, x, y = index % 2, (index // 2) % 4, index // 8
    past, following = slot_tables(clip_ids[0], lax.axis_index("seq") * F)
    cache = shifted(own_frames[F - 2 :], 1)
    cot_next = shifted(own_cot[:2], -1)
    hidden, act_grad, keep, send = main(
        core[None], past, following, own_frames, cache, own_cot, cot_next, conv1_weight, conv2_weight
    )
    hidden_cache = shifted(hidden[F - 2 :], 1)
    act_grad_next = shifted(act_grad[:2], -1)
    recv = dp_permute(send, lambda d: d ^ 1)
    block_out = conv(False, past, hidden, hidden_cache, conv2_weight, own_frames)
    input_grad = conv(True, following, act_grad, act_grad_next, conv1_weight, own_cot)

    keep, *sent = add_stage(
        x[None], keep.reshape(2, 4, 4, 108, C), [recv.reshape(2, 4, 4, 108, C)], 4
    )
    recv = [
        dp_permute(part, lambda d, s=s: (d // 8) * 8 + (d % 8 + 2 * s) % 8)
        for s, part in zip((1, 2, 3), sent)
    ]
    keep, *sent = add_stage(
        y[None], keep.reshape(2, 1, 4, 108, C), [part.reshape(2, 1, 4, 108, C) for part in recv], 1
    )
    recv = [dp_permute(part, lambda d, s=s: (d + 8 * s) % 32) for s, part in zip((1, 2, 3), sent)]
    total = keep + recv[0].astype(F32) + recv[1].astype(F32) + recv[2].astype(F32)
    near = [
        lax.ppermute(total, "seq", [(z, (z // 4) * 4 + (z + s) % 4) for z in range(8)])
        for s in (1, 2, 3)
    ]
    total = (total + near[1]) + (near[0] + near[2])
    total = total + lax.ppermute(total, "seq", [(z, z ^ 4) for z in range(8)])
    rows = lax.axis_size("dp") * lax.axis_size("seq") * F * POS
    total = total.reshape(2, 108, C) * (F32(1.0) / jnp.sqrt(F32(rows)))
    return (
        block_out.reshape(frames.shape),
        input_grad.reshape(frames.shape),
        total[0],
        total[1],
    )


def solution(mesh):
    return jax.shard_map(
        per_device,
        mesh=mesh,
        in_specs=(
            P("dp", "seq", None, None, None),
            P("dp", None),
            P("dp", "seq", None, None, None),
            P(),
            P(),
        ),
        out_specs=(
            P("dp", "seq", None, None, None),
            P("dp", "seq", None, None, None),
            P("dp", None),
            P("dp", None),
        ),
        check_vma=False,
    )
```

profile of v0, /device:TPU:2, one launch (start us, length us, event | category | flops | bytes accessed | tf_op | source)
XLA Modules:
  0.0 94.0 jit_solution(11951805125674558678)
XLA Ops:
  0.6 0.9 slice.50
  1.5 1.3 %collective-permute-start.1 = (bf16[2,256,128]{2,1,0:T(8,128)(2,1)S(1)}, bf16[2,256,128]{2,1,0:T(8,128)(2,1)S(1)}, u32[]{:S(2)}, u32[]{:S(2)}) collective-permute-start(bf16[2,256,128]{2,1,0:T(8,128)(2,1)S(1)} %bitcast.34), channel_id=1, source_target_pairs={{32,0},{64,32},{96,64},{128,96},{160,128},{192,160},{224,192},{33,... | collective-permute-start | bytes 393224 | tf_op jit(solution)/shard_map/ppermute | solution.py:304
  2.8 0.9 slice.48
  3.8 4.6 %collective-permute-start = (bf16[2,256,128]{2,1,0:T(8,128)(2,1)S(1)}, bf16[2,256,128]{2,1,0:T(8,128)(2,1)S(1)}, u32[]{:S(2)}, u32[]{:S(2)}) collective-permute-start(bf16[2,256,128]{2,1,0:T(8,128)(2,1)S(1)} %bitcast.35), channel_id=1, source_target_pairs={{0,32},{32,64},{64,96},{96,128},{128,160},{160,192},{192,224},{1,3... | collective-permute-start | bytes 393224 | tf_op jit(solution)/shard_map/ppermute | solution.py:304
  8.3 0.7 pad_add_fusion.2
  9.1 0.1 dynamic_slice.3
  9.2 0.1 fusion.2
  9.2 0.1 copy.15
  9.3 0.1 copy.14
  9.4 0.1 copy.16
  9.5 0.1 copy.13
  9.6 0.7 pad_add_fusion
  10.2 0.0 collective-permute-done.1.cot_next_ref
  10.2 0.0 copy-start.3
  10.2 0.7 collective-permute-done.cache_ref
  11.0 0.0 copy-start.4
  11.0 0.0 copy-done.3
  11.0 0.7 copy-done.4
  11.6 15.3 %shard_map.84 = (bf16[8,256,128]{2,1,0:T(8,128)(2,1)}, bf16[8,256,128]{2,1,0:T(8,128)(2,1)}, f32[2,16,108,128]{3,2,1,0:T(8,128)}, bf16[2,16,108,128]{3,2,1,0:T(8,128)(2,1)}) custom-call(s32[1]{0:T(128)} %bitcast.3.core_ref, s32[8,3]{1,0:T(8,128)} %get-tuple-element.34.past_ref.slot_ref, s32[8,3]{1,0:T(8,128)} %get-tuple-element.35.next_ref.slot_ref, ...), custom_call_target="tpu_custom_call" | custom-call | flops 7247757312 | bytes 9437184 | tf_op jit(solution)/shard_map/pallas_call | solution.py:233
  26.9 1.4 %copy.17 = bf16[2,16,108,128]{3,1,2,0:T(8,128)(2,1)S(1)} copy(bf16[2,16,108,128]{3,2,1,0:T(8,128)(2,1)} %get-tuple-element.19) | data formatting | bytes 1769472 | tf_op jit(solution)/shard_map/pallas_call | solution.py:233
  28.4 0.3 collective-permute-start.4
  28.7 2.4 %collective-permute-done.4 = bf16[2,16,108,128]{3,1,2,0:T(8,128)(2,1)S(1)} collective-permute-done((bf16[2,16,108,128]{3,1,2,0:T(8,128)(2,1)S(1)}, bf16[2,16,108,128]{3,1,2,0:T(8,128)(2,1)S(1)}, u32[]{:S(2)}, u32[]{:S(2)}) %collective-permute-start.4) | collective-permute-done | bytes 884768 | tf_op jit(solution)/shard_map/ppermute | solution.py:308
  31.1 1.2 %copy.18 = bf16[2,16,108,128]{3,2,1,0:T(8,128)(2,1)} copy(bf16[2,16,108,128]{3,1,2,0:T(8,128)(2,1)S(1)} %collective-permute-done.4) | data formatting | bytes 1769472 | tf_op jit(solution)/shard_map/ppermute | solution.py:308
  32.2 2.9 %shard_map.87 = (f32[2,4,108,128]{3,2,1,0:T(8,128)}, bf16[2,4,108,128]{3,2,1,0:T(8,128)(2,1)}, bf16[2,4,108,128]{3,2,1,0:T(8,128)(2,1)}, bf16[2,4,108,128]{3,2,1,0:T(8,128)(2,1)}) custom-call(s32[1]{0:T(128)} %bitcast.13.own_ref, f32[2,4,4,108,128]{4,3,2,1,0:T(8,128)} %bitcast.29, bf16[2,4,4,108,128]{4,3,2,1,0:T(8,128)(2,1)} %bitcast.28), custom_call_target="tpu_custom_call" | custom-call | bytes 2097152 | tf_op jit(solution)/shard_map/pallas_call | solution.py:233
  35.1 1.5 %collective-permute-start.5 = (bf16[2,4,108,128]{3,2,1,0:T(8,128)(2,1)}, bf16[2,4,108,128]{3,2,1,0:T(8,128)(2,1)S(1)}, u32[]{:S(2)}, u32[]{:S(2)}) collective-permute-start(bf16[2,4,108,128]{3,2,1,0:T(8,128)(2,1)} %get-tuple-element.21), channel_id=1, source_target_pairs={{0,2},{1,3},{2,4},{3,5},{4,6},{5,7},{6,0},{7,1},{8,10},{9,11},{10,... | collective-permute-start | bytes 663560 | tf_op jit(solution)/shard_map/ppermute | solution.py:308
  36.6 2.7 %collective-permute-start.6 = (bf16[2,4,108,128]{3,2,1,0:T(8,128)(2,1)}, bf16[2,4,108,128]{3,2,1,0:T(8,128)(2,1)S(1)}, u32[]{:S(2)}, u32[]{:S(2)}) collective-permute-start(bf16[2,4,108,128]{3,2,1,0:T(8,128)(2,1)} %get-tuple-element.22), channel_id=1, source_target_pairs={{0,4},{1,5},{2,6},{3,7},{4,0},{5,1},{6,2},{7,3},{8,12},{9,13},{10,... | collective-permute-start | bytes 663560 | tf_op jit(solution)/shard_map/ppermute | solution.py:308
  39.3 0.6 collective-permute-start.7
  39.9 4.0 %collective-permute-done.5 = bf16[2,4,108,128]{3,2,1,0:T(8,128)(2,1)S(1)} collective-permute-done((bf16[2,4,108,128]{3,2,1,0:T(8,128)(2,1)}, bf16[2,4,108,128]{3,2,1,0:T(8,128)(2,1)S(1)}, u32[]{:S(2)}, u32[]{:S(2)}) %collective-permute-start.5) | collective-permute-done | bytes 221216 | tf_op jit(solution)/shard_map/ppermute | solution.py:308
  43.8 0.0 copy-start
  43.8 3.0 %collective-permute-done.6 = bf16[2,4,108,128]{3,2,1,0:T(8,128)(2,1)S(1)} collective-permute-done((bf16[2,4,108,128]{3,2,1,0:T(8,128)(2,1)}, bf16[2,4,108,128]{3,2,1,0:T(8,128)(2,1)S(1)}, u32[]{:S(2)}, u32[]{:S(2)}) %collective-permute-start.6) | collective-permute-done | bytes 221216 | tf_op jit(solution)/shard_map/ppermute | solution.py:308
  46.8 0.0 copy-start.1
  46.9 3.7 %collective-permute-done.7 = bf16[2,4,108,128]{3,2,1,0:T(8,128)(2,1)S(1)} collective-permute-done((bf16[2,4,108,128]{3,2,1,0:T(8,128)(2,1)}, bf16[2,4,108,128]{3,2,1,0:T(8,128)(2,1)S(1)}, u32[]{:S(2)}, u32[]{:S(2)}) %collective-permute-start.7) | collective-permute-done | bytes 221216 | tf_op jit(solution)/shard_map/ppermute | solution.py:308
  50.6 0.0 copy-start.2
  50.6 0.0 copy-done
  50.6 0.0 copy-done.1
  50.6 0.7 copy-done.2
  51.3 2.0 %shard_map.88 = (f32[2,1,108,128]{3,2,1,0:T(8,128)}, bf16[2,1,108,128]{3,2,1,0:T(8,128)(2,1)}, bf16[2,1,108,128]{3,2,1,0:T(8,128)(2,1)}, bf16[2,1,108,128]{3,2,1,0:T(8,128)(2,1)}) custom-call(s32[1]{0:T(128)} %bitcast.12.own_ref, f32[2,1,4,108,128]{4,3,2,1,0:T(8,128)} %bitcast.30, bf16[2,1,4,108,128]{4,3,2,1,0:T(8,128)(2,1)} %bitcast.31, ...), custom_call_target="tpu_custom_call" | custom-call | bytes 2097152 | tf_op jit(solution)/shard_map/pallas_call | solution.py:233
  53.3 0.9 collective-permute-start.8
  54.2 2.9 %collective-permute-start.9 = (bf16[2,1,108,128]{3,2,1,0:T(8,128)(2,1)}, bf16[2,1,108,128]{3,2,1,0:T(8,128)(2,1)S(1)}, u32[]{:S(2)}, u32[]{:S(2)}) collective-permute-start(bf16[2,1,108,128]{3,2,1,0:T(8,128)(2,1)} %get-tuple-element.26), channel_id=1, source_target_pairs={{0,16},{1,17},{2,18},{3,19},{4,20},{5,21},{6,22},{7,23},{8,24},{9,... | collective-permute-start | bytes 165896 | tf_op jit(solution)/shard_map/ppermute | solution.py:308
  57.1 1.4 %collective-permute-start.10 = (bf16[2,1,108,128]{3,2,1,0:T(8,128)(2,1)}, bf16[2,1,108,128]{3,2,1,0:T(8,128)(2,1)S(1)}, u32[]{:S(2)}, u32[]{:S(2)}) collective-permute-start(bf16[2,1,108,128]{3,2,1,0:T(8,128)(2,1)} %get-tuple-element.27), channel_id=1, source_target_pairs={{0,24},{1,25},{2,26},{3,27},{4,28},{5,29},{6,30},{7,31},{8,0},{9,1... | collective-permute-start | bytes 165896 | tf_op jit(solution)/shard_map/ppermute | solution.py:308
  58.5 0.9 slice.52
  59.4 0.9 slice.53
  60.3 1.3 %collective-permute-start.3 = (bf16[2,256,128]{2,1,0:T(8,128)(2,1)S(1)}, bf16[2,256,128]{2,1,0:T(8,128)(2,1)S(1)}, u32[]{:S(2)}, u32[]{:S(2)}) collective-permute-start(bf16[2,256,128]{2,1,0:T(8,128)(2,1)S(1)} %slice.53), channel_id=1, source_target_pairs={{32,0},{64,32},{96,64},{128,96},{160,128},{192,160},{224,192},{33,... | collective-permute-start | bytes 393224 | tf_op jit(solution)/shard_map/ppermute | solution.py:304
  61.6 5.0 %collective-permute-start.2 = (bf16[2,256,128]{2,1,0:T(8,128)(2,1)S(1)}, bf16[2,256,128]{2,1,0:T(8,128)(2,1)S(1)}, u32[]{:S(2)}, u32[]{:S(2)}) collective-permute-start(bf16[2,256,128]{2,1,0:T(8,128)(2,1)S(1)} %slice.52), channel_id=1, source_target_pairs={{0,32},{32,64},{64,96},{96,128},{128,160},{160,192},{192,224},{1,3... | collective-permute-start | bytes 393224 | tf_op jit(solution)/shard_map/ppermute | solution.py:304
  66.6 0.0 collective-permute-done.8
  66.6 0.0 collective-permute-done.9
  66.7 0.0 collective-permute-done.10
  66.7 0.9 convert_add_fusion
  67.6 7.1 %collective-permute-start.13 = (f32[2,1,108,128]{3,2,1,0:T(8,128)S(1)}, f32[2,1,108,128]{3,2,1,0:T(8,128)S(1)}, u32[]{:S(2)}, u32[]{:S(2)}) collective-permute-start(f32[2,1,108,128]{3,2,1,0:T(8,128)S(1)} %convert_add_fusion), channel_id=1, source_target_pairs={{0,96},{32,0},{64,32},{96,64},{128,224},{160,128},{192,160},{224,1... | collective-permute-start | bytes 331784 | tf_op jit(solution)/shard_map/ppermute | solution.py:357
  74.7 0.0 collective-permute-start.12
  74.7 0.7 collective-permute-start.11
  75.4 0.0 collective-permute-done.3.cache_ref
  75.4 0.0 copy-start.6
  75.4 0.6 copy-done.6
  76.0 5.3 %shard_map.86 = bf16[8,256,128]{2,1,0:T(8,128)(2,1)} custom-call(s32[8,3]{1,0:T(8,128)} %get-tuple-element.35.next_ref.slot_ref, bf16[8,256,128]{2,1,0:T(8,128)(2,1)} %get-tuple-element.17.frames_ref, bf16[2,256,128]{2,1,0:T(8,128)(2,1)} %copy-done.6, bf16[3456,128]{1,0:T(8,128)(2,1)} %weight_ref.3, bf16[8,256,128]{2,1,0:T(8,128)(2,1)} %bitcast.37), custom_call_target="tpu_custom_call" | custom-call | flops 1811939328 | bytes 3145728 | tf_op jit(solution)/shard_map/pallas_call | solution.py:233
  81.3 0.0 collective-permute-done.13
  81.3 0.0 collective-permute-done.12
  81.3 2.3 %collective-permute-done.11 = f32[2,1,108,128]{3,2,1,0:T(8,128)S(1)} collective-permute-done((f32[2,1,108,128]{3,2,1,0:T(8,128)S(1)}, f32[2,1,108,128]{3,2,1,0:T(8,128)S(1)}, u32[]{:S(2)}, u32[]{:S(2)}) %collective-permute-start.11) | collective-permute-done | bytes 110624 | tf_op jit(solution)/shard_map/ppermute | solution.py:357
  83.7 3.8 %collective-permute-start.14 = (f32[2,1,108,128]{3,2,1,0:T(8,128)S(1)}, f32[2,1,108,128]{3,2,1,0:T(8,128)S(1)}, u32[]{:S(2)}, u32[]{:S(2)}) collective-permute-start(f32[2,1,108,128]{3,2,1,0:T(8,128)S(1)} %add_add_fusion), channel_id=1, source_target_pairs={{0,128},{32,160},{64,192},{96,224},{128,0},{160,32},{192,64},{224,... | collective-permute-start | bytes 331784 | tf_op jit(solution)/shard_map/ppermute | solution.py:361
  87.5 0.0 collective-permute-done.2.cache_ref
  87.5 0.6 copy-done.5
  88.1 5.2 %shard_map.85 = bf16[8,256,128]{2,1,0:T(8,128)(2,1)} custom-call(s32[8,3]{1,0:T(8,128)} %get-tuple-element.34.past_ref.slot_ref, bf16[8,256,128]{2,1,0:T(8,128)(2,1)} %get-tuple-element.16.frames_ref, bf16[2,256,128]{2,1,0:T(8,128)(2,1)} %copy-done.5, bf16[3456,128]{1,0:T(8,128)(2,1)} %weight_ref.2, bf16[8,256,128]{2,1,0:T(8,128)(2,1)} %bitcast.39), custom_call_target="tpu_custom_call" | custom-call | flops 1811939328 | bytes 3145728 | tf_op jit(solution)/shard_map/pallas_call | solution.py:233
  93.3 0.0 collective-permute-done.14
  93.3 0.6 slice_bitcast_fusion
  (6 shorter events, 0.1 us)
Async XLA Ops:
  1.5 8.7 %collective-permute-start.1 = (bf16[2,256,128]{2,1,0:T(8,128)(2,1)S(1)}, bf16[2,256,128]{2,1,0:T(8,128)(2,1)S(1)}, u32[]{:S(2)}, u32[]{:S(2)}) collective-permute-start(bf16[2,256,128]{2,1,0:T(8,128)(2,1)S(1)} %bitcast.34), channel_id=1, source_target_pairs={{32,0},{64,32},{96,64},{128,96},{160,128},{192,160},{224,192},{33,... | collective-permute-start | bytes 393224 | tf_op jit(solution)/shard_map/ppermute | solution.py:304
  3.8 7.2 %collective-permute-start = (bf16[2,256,128]{2,1,0:T(8,128)(2,1)S(1)}, bf16[2,256,128]{2,1,0:T(8,128)(2,1)S(1)}, u32[]{:S(2)}, u32[]{:S(2)}) collective-permute-start(bf16[2,256,128]{2,1,0:T(8,128)(2,1)S(1)} %bitcast.35), channel_id=1, source_target_pairs={{0,32},{32,64},{64,96},{96,128},{128,160},{160,192},{192,224},{1,3... | collective-permute-start | bytes 393224 | tf_op jit(solution)/shard_map/ppermute | solution.py:304
  10.2 0.7 copy-start.3
  11.0 0.7 copy-start.4
  28.4 2.7 %collective-permute-start.4 = (bf16[2,16,108,128]{3,1,2,0:T(8,128)(2,1)S(1)}, bf16[2,16,108,128]{3,1,2,0:T(8,128)(2,1)S(1)}, u32[]{:S(2)}, u32[]{:S(2)}) collective-permute-start(bf16[2,16,108,128]{3,1,2,0:T(8,128)(2,1)S(1)} %copy.17), channel_id=1, source_target_pairs={{0,1},{1,0},{2,3},{3,2},{4,5},{5,4},{6,7},{7,6},{8,9},{9,8},{10,11... | collective-permute-start | bytes 2654216 | tf_op jit(solution)/shard_map/ppermute | solution.py:308
  35.1 8.7 %collective-permute-start.5 = (bf16[2,4,108,128]{3,2,1,0:T(8,128)(2,1)}, bf16[2,4,108,128]{3,2,1,0:T(8,128)(2,1)S(1)}, u32[]{:S(2)}, u32[]{:S(2)}) collective-permute-start(bf16[2,4,108,128]{3,2,1,0:T(8,128)(2,1)} %get-tuple-element.21), channel_id=1, source_target_pairs={{0,2},{1,3},{2,4},{3,5},{4,6},{5,7},{6,0},{7,1},{8,10},{9,11},{10,... | collective-permute-start | bytes 663560 | tf_op jit(solution)/shard_map/ppermute | solution.py:308
  36.6 10.2 %collective-permute-start.6 = (bf16[2,4,108,128]{3,2,1,0:T(8,128)(2,1)}, bf16[2,4,108,128]{3,2,1,0:T(8,128)(2,1)S(1)}, u32[]{:S(2)}, u32[]{:S(2)}) collective-permute-start(bf16[2,4,108,128]{3,2,1,0:T(8,128)(2,1)} %get-tuple-element.22), channel_id=1, source_target_pairs={{0,4},{1,5},{2,6},{3,7},{4,0},{5,1},{6,2},{7,3},{8,12},{9,13},{10,... | collective-permute-start | bytes 663560 | tf_op jit(solution)/shard_map/ppermute | solution.py:308
  39.3 11.3 %collective-permute-start.7 = (bf16[2,4,108,128]{3,2,1,0:T(8,128)(2,1)}, bf16[2,4,108,128]{3,2,1,0:T(8,128)(2,1)S(1)}, u32[]{:S(2)}, u32[]{:S(2)}) collective-permute-start(bf16[2,4,108,128]{3,2,1,0:T(8,128)(2,1)} %get-tuple-element.23), channel_id=1, source_target_pairs={{0,6},{1,7},{2,0},{3,1},{4,2},{5,3},{6,4},{7,5},{8,14},{9,15},{10,... | collective-permute-start | bytes 663560 | tf_op jit(solution)/shard_map/ppermute | solution.py:308
  43.8 6.8 %copy-start = (bf16[2,4,108,128]{3,2,1,0:T(8,128)(2,1)}, bf16[2,4,108,128]{3,2,1,0:T(8,128)(2,1)S(1)}, u32[]{:S(2)}) copy-start(bf16[2,4,108,128]{3,2,1,0:T(8,128)(2,1)S(1)} %collective-permute-done.5) | copy-start | bytes 663556
  46.8 3.8 %copy-start.1 = (bf16[2,4,108,128]{3,2,1,0:T(8,128)(2,1)}, bf16[2,4,108,128]{3,2,1,0:T(8,128)(2,1)S(1)}, u32[]{:S(2)}) copy-start(bf16[2,4,108,128]{3,2,1,0:T(8,128)(2,1)S(1)} %collective-permute-done.6) | copy-start | bytes 663556
  50.6 0.7 copy-start.2
  53.3 13.3 %collective-permute-start.8 = (bf16[2,1,108,128]{3,2,1,0:T(8,128)(2,1)}, bf16[2,1,108,128]{3,2,1,0:T(8,128)(2,1)S(1)}, u32[]{:S(2)}, u32[]{:S(2)}) collective-permute-start(bf16[2,1,108,128]{3,2,1,0:T(8,128)(2,1)} %get-tuple-element.25), channel_id=1, source_target_pairs={{0,8},{1,9},{2,10},{3,11},{4,12},{5,13},{6,14},{7,15},{8,16},{9,17... | collective-permute-start | bytes 165896 | tf_op jit(solution)/shard_map/ppermute | solution.py:308
  54.2 12.4 %collective-permute-start.9 = (bf16[2,1,108,128]{3,2,1,0:T(8,128)(2,1)}, bf16[2,1,108,128]{3,2,1,0:T(8,128)(2,1)S(1)}, u32[]{:S(2)}, u32[]{:S(2)}) collective-permute-start(bf16[2,1,108,128]{3,2,1,0:T(8,128)(2,1)} %get-tuple-element.26), channel_id=1, source_target_pairs={{0,16},{1,17},{2,18},{3,19},{4,20},{5,21},{6,22},{7,23},{8,24},{9,... | collective-permute-start | bytes 165896 | tf_op jit(solution)/shard_map/ppermute | solution.py:308
  57.1 9.5 %collective-permute-start.10 = (bf16[2,1,108,128]{3,2,1,0:T(8,128)(2,1)}, bf16[2,1,108,128]{3,2,1,0:T(8,128)(2,1)S(1)}, u32[]{:S(2)}, u32[]{:S(2)}) collective-permute-start(bf16[2,1,108,128]{3,2,1,0:T(8,128)(2,1)} %get-tuple-element.27), channel_id=1, source_target_pairs={{0,24},{1,25},{2,26},{3,27},{4,28},{5,29},{6,30},{7,31},{8,0},{9,1... | collective-permute-start | bytes 165896 | tf_op jit(solution)/shard_map/ppermute | solution.py:308
  60.3 15.1 %collective-permute-start.3 = (bf16[2,256,128]{2,1,0:T(8,128)(2,1)S(1)}, bf16[2,256,128]{2,1,0:T(8,128)(2,1)S(1)}, u32[]{:S(2)}, u32[]{:S(2)}) collective-permute-start(bf16[2,256,128]{2,1,0:T(8,128)(2,1)S(1)} %slice.53), channel_id=1, source_target_pairs={{32,0},{64,32},{96,64},{128,96},{160,128},{192,160},{224,192},{33,... | collective-permute-start | bytes 393224 | tf_op jit(solution)/shard_map/ppermute | solution.py:304
  61.6 25.9 %collective-permute-start.2 = (bf16[2,256,128]{2,1,0:T(8,128)(2,1)S(1)}, bf16[2,256,128]{2,1,0:T(8,128)(2,1)S(1)}, u32[]{:S(2)}, u32[]{:S(2)}) collective-permute-start(bf16[2,256,128]{2,1,0:T(8,128)(2,1)S(1)} %slice.52), channel_id=1, source_target_pairs={{0,32},{32,64},{64,96},{96,128},{128,160},{160,192},{192,224},{1,3... | collective-permute-start | bytes 393224 | tf_op jit(solution)/shard_map/ppermute | solution.py:304
  67.6 13.7 %collective-permute-start.13 = (f32[2,1,108,128]{3,2,1,0:T(8,128)S(1)}, f32[2,1,108,128]{3,2,1,0:T(8,128)S(1)}, u32[]{:S(2)}, u32[]{:S(2)}) collective-permute-start(f32[2,1,108,128]{3,2,1,0:T(8,128)S(1)} %convert_add_fusion), channel_id=1, source_target_pairs={{0,96},{32,0},{64,32},{96,64},{128,224},{160,128},{192,160},{224,1... | collective-permute-start | bytes 331784 | tf_op jit(solution)/shard_map/ppermute | solution.py:357
  74.7 6.6 %collective-permute-start.12 = (f32[2,1,108,128]{3,2,1,0:T(8,128)S(1)}, f32[2,1,108,128]{3,2,1,0:T(8,128)S(1)}, u32[]{:S(2)}, u32[]{:S(2)}) collective-permute-start(f32[2,1,108,128]{3,2,1,0:T(8,128)S(1)} %convert_add_fusion), channel_id=1, source_target_pairs={{0,32},{32,64},{64,96},{96,0},{128,160},{160,192},{192,224},{224,1... | collective-permute-start | bytes 331784 | tf_op jit(solution)/shard_map/ppermute | solution.py:357
  74.7 8.9 %collective-permute-start.11 = (f32[2,1,108,128]{3,2,1,0:T(8,128)S(1)}, f32[2,1,108,128]{3,2,1,0:T(8,128)S(1)}, u32[]{:S(2)}, u32[]{:S(2)}) collective-permute-start(f32[2,1,108,128]{3,2,1,0:T(8,128)S(1)} %convert_add_fusion), channel_id=1, source_target_pairs={{0,64},{32,96},{64,0},{96,32},{128,192},{160,224},{192,128},{224,1... | collective-permute-start | bytes 331784 | tf_op jit(solution)/shard_map/ppermute | solution.py:357
  75.4 0.6 copy-start.6
  83.7 9.7 %collective-permute-start.14 = (f32[2,1,108,128]{3,2,1,0:T(8,128)S(1)}, f32[2,1,108,128]{3,2,1,0:T(8,128)S(1)}, u32[]{:S(2)}, u32[]{:S(2)}) collective-permute-start(f32[2,1,108,128]{3,2,1,0:T(8,128)S(1)} %add_add_fusion), channel_id=1, source_target_pairs={{0,128},{32,160},{64,192},{96,224},{128,0},{160,32},{192,64},{224,... | collective-permute-start | bytes 331784 | tf_op jit(solution)/shard_map/ppermute | solution.py:361
  87.5 0.6 copy-start.5
where the time goes:
time: 94.9 us; the launch traced here: 94 us
  starting transfers between devices  33.9 us (36%)
  Pallas kernels  30.7 us (32%)
  waiting for transfers between devices  16.2 us (17%)
  local copies, waits for them, and re-layouts  9.95 us (10%)
  other arithmetic  2.46 us (3%)
    pallas_call x5, Pallas kernels, call(): pl.pallas_call(kernel, out_shape=[jax.ShapeDtypeStruct(shape, dtype) for...  30.7 us
    ppermute x7, waiting for transfers between devices, dp_permute(): lax.ppermute(value, 'dp', [(source, target(source)) for source in range(3...  13.1 us
    ppermute x4, starting transfers between devices, shifted(): lax.ppermute(value, 'seq', [(source, source + steps) for source in range(...  12.2 us
    ppermute x7, starting transfers between devices, dp_permute(): lax.ppermute(value, 'dp', [(source, target(source)) for source in range(3...  10.2 us
    ppermute x3, starting transfers between devices, per_device(): lax.ppermute(total, 'seq', [(z, z // 4 * 4 + (z + s) % 4) for z in range(...  7.77 us
    ppermute x1, starting transfers between devices, per_device(): total = total + lax.ppermute(total, 'seq', [(z, z ^ 4) for z in range(8)])  3.81 us
    unnamed x14, local copies, waits for them, and re-layouts  2.65 us
    ppermute x3, waiting for transfers between devices, per_device(): lax.ppermute(total, 'seq', [(z, z // 4 * 4 + (z + s) % 4) for z in range(...  2.35 us
  transfers between devices with their start and end apart: 15, of which 6 were waited for; matrix products, arithmetic and copies ran while one was open for 6% of the time, Pallas kernels for 11%

commit v1 on v0

--- a/solution.py
+++ b/solution.py
@@ -16,7 +16,27 @@
 NONE = F + 2
 BF16 = jnp.bfloat16
 F32 = jnp.float32
-VMEM_LIMIT = 56 * 1024 * 1024
+BLOCK = 108
+PADDED = 112
+
+
+def past_slots(clips, first, t):
+    slots = []
+    for k in range(3):
+        frame = first + t + k - 2
+        same = clips[0, jnp.maximum(frame, 0)] == clips[0, first + t]
+        slots.append(jnp.where(same & (frame >= 0), t + k, NONE))
+    return slots
+
+
+def next_slots(clips, first, t):
+    last = clips.shape[1] - 1
+    slots = []
+    for q in range(3):
+        frame = first + t + q
+        same = clips[0, jnp.minimum(frame, last)] == clips[0, first + t]
+        slots.append(jnp.where(same & (frame <= last), t + q, NONE))
+    return slots
 
 
 def column(rows):
@@ -73,9 +93,7 @@
 
 
 def main_kernel(
-    core_ref,
-    past_ref,
-    next_ref,
+    clips,
     frames_ref,
     cache_ref,
     cot_ref,
@@ -84,6 +102,8 @@
     weight2_ref,
     hidden_ref,
     act_grad_ref,
+    hidden_tail_ref,
+    act_grad_head_ref,
     keep_ref,
     send_ref,
     window,
@@ -100,6 +120,9 @@
     grad_shifted,
     grads,
 ):
+    first_frame = lax.axis_index("seq") * F
+    past = [past_slots(clips, first_frame, t) for t in range(F)]
+    following = [next_slots(clips, first_frame, t) for t in range(F)]
     zero = jnp.zeros((POS, C), BF16)
     for f in range(2):
         window[f] = cache_ref[f]
@@ -114,7 +137,7 @@
 
     sums = []
     for t in range(F):
-        out = conv_frame(window, [past_ref[t, k] for k in range(3)], conv_weight)
+        out = conv_frame(window, past[t], conv_weight)
         act[t] = out
         sums.append(jnp.sum(out, axis=0, keepdims=True))
     center = group_mean(jnp.concatenate(sums, axis=0))
@@ -128,6 +151,8 @@
         gate = 1.0 / (1.0 + jnp.exp(-normed))
         hidden = (normed * gate).astype(BF16)
         hidden_ref[t] = hidden
+        if t >= F - 2:
+            hidden_tail_ref[t - F + 2] = hidden
         act[t] = normed
         slope[t] = gate * (1.0 + normed * (1.0 - gate))
         for a, piece in enumerate(row_pieces(hidden)):
@@ -135,7 +160,7 @@
 
     first, second = [], []
     for t in range(F):
-        grad = conv_frame(cot_window, [next_ref[t, q] for q in range(3)], back_weight) * slope[t]
+        grad = conv_frame(cot_window, following[t], back_weight) * slope[t]
         slope[t] = grad
         first.append(jnp.sum(grad, axis=0, keepdims=True))
         second.append(jnp.sum(grad * act[t], axis=0, keepdims=True))
@@ -145,6 +170,8 @@
         grad = scale[t : t + 1] * (slope[t] - first[t : t + 1] - act[t] * second[t : t + 1])
         rounded = grad.astype(BF16)
         act_grad_ref[t] = rounded
+        if t < 2:
+            act_grad_head_ref[t] = rounded
         wide = rounded.astype(F32)
         grad_shifted[t * POS : (t + 1) * POS, :C] = shift_up(wide).astype(BF16)
         grad_shifted[t * POS : (t + 1) * POS, C : 2 * C] = rounded
@@ -159,7 +186,7 @@
     for s in range(F):
         for k in range(3):
             cot_taps[s * POS : (s + 1) * POS, 3 * C * k : 3 * C * (k + 1)] = cot_shifted[
-                next_ref[s, 2 - k]
+                following[s][2 - k]
             ]
     second_grad = jnp.dot(hidden_t[...], cot_taps[...], preferred_element_type=F32)
     for k in range(3):
@@ -177,7 +204,7 @@
     for t in range(F):
         for k in range(3):
             frame_taps[3 * C * k : 3 * C * (k + 1), t * POS : (t + 1) * POS] = frame_t[
-                past_ref[t, k]
+                past[t][k]
             ]
     first_grad = jnp.dot(frame_taps[...], grad_shifted[...], preferred_element_type=F32)
     for outer in range(9):
@@ -187,33 +214,42 @@
                 outer * C : (outer + 1) * C, b * C : (b + 1) * C
             ]
 
-    own = core_ref[0] == 0
+    own = lax.rem(lax.axis_index("dp"), 2) == 0
     for g in range(2):
         for m in range(16):
-            low = grads[g, 216 * m : 216 * m + 108]
-            high = grads[g, 216 * m + 108 : 216 * m + 216]
-            keep_ref[g, m] = jnp.where(own, low, high)
-            send_ref[g, m] = jnp.where(own, high, low).astype(BF16)
-
-
-def conv_kernel(adjoint, slot_ref, frames_ref, cache_ref, weight_ref, base_ref, out_ref, window, weight):
+            low = grads[g, 2 * BLOCK * m : 2 * BLOCK * m + BLOCK]
+            high = grads[g, 2 * BLOCK * m + BLOCK : 2 * BLOCK * (m + 1)]
+            keep_ref[g, m, :BLOCK] = jnp.where(own, low, high)
+            keep_ref[g, m, BLOCK:] = jnp.zeros((PADDED - BLOCK, C), F32)
+            send_ref[g, m, :BLOCK] = jnp.where(own, high, low).astype(BF16)
+            send_ref[g, m, BLOCK:] = jnp.zeros((PADDED - BLOCK, C), BF16)
+
+
+def head_kernel(frames_ref, cot_ref, tail_ref, head_ref):
+    tail_ref[...] = frames_ref[...]
+    head_ref[...] = cot_ref[...]
+
+
+def conv_kernel(adjoint, clips, frames_ref, cache_ref, weight_ref, base_ref, out_ref, window, weight):
     for f in range(2):
         window[F + f if adjoint else f] = cache_ref[f]
     for f in range(F):
         window[f if adjoint else 2 + f] = frames_ref[f]
     window[NONE] = jnp.zeros((POS, C), BF16)
+    first_frame = lax.axis_index("seq") * F
     (adjoint_weight if adjoint else forward_weight)(weight_ref, weight)
     for t in range(F):
-        out = conv_frame(window, [slot_ref[t, k] for k in range(3)], weight)
+        slots = (next_slots if adjoint else past_slots)(clips, first_frame, t)
+        out = conv_frame(window, slots, weight)
         out_ref[t] = (base_ref[t].astype(F32) + out).astype(BF16)
 
 
-def add_kernel(own_ref, keep_ref, *refs):
+def add_kernel(axis, keep_ref, *refs):
     received, (kept_ref, *sent_refs) = refs[:-4], refs[-4:]
-    own = own_ref[0]
-    outer = keep_ref.shape[1]
+    index = lax.axis_index("dp")
+    own = lax.rem(lax.div(index, 2), 4) if axis == "x" else lax.div(index, 8)
     for g in range(2):
-        for m in range(outer):
+        for m in range(keep_ref.shape[1]):
             for step in range(4):
                 block = lax.rem(own + step, 4)
                 total = keep_ref[g, m, block]
@@ -229,14 +265,14 @@
 VMEM = pl.BlockSpec(memory_space=pltpu.VMEM)
 
 
-def call(kernel, operands, scalars, outs, scratch=(), flops=0, moved=0):
+def call(kernel, operands, scalars, outs, scratch=(), flops=0, moved=0, limit=16):
     return pl.pallas_call(
         kernel,
         out_shape=[jax.ShapeDtypeStruct(shape, dtype) for shape, dtype in outs],
         in_specs=[SMEM] * scalars + [VMEM] * (len(operands) - scalars),
         out_specs=[VMEM] * len(outs),
         scratch_shapes=[pltpu.VMEM(shape, dtype) for shape, dtype in scratch],
-        compiler_params=pltpu.CompilerParams(vmem_limit_bytes=VMEM_LIMIT),
+        compiler_params=pltpu.CompilerParams(vmem_limit_bytes=limit << 20),
         cost_estimate=pl.CostEstimate(flops=flops, bytes_accessed=moved, transcendentals=0),
     )(*operands)
 
@@ -244,16 +280,18 @@
 CONV_FLOPS = 2 * F * POS * 27 * C * C
 
 
-def main(core, past, following, frames, cache, cot, cot_next, weight1, weight2):
+def main(clips, frames, cache, cot, cot_next, weight1, weight2):
     return call(
         main_kernel,
-        (core, past, following, frames, cache, cot, cot_next, weight1, weight2),
-        3,
+        (clips, frames, cache, cot, cot_next, weight1, weight2),
+        1,
         [
             ((F, POS, C), BF16),
             ((F, POS, C), BF16),
-            ((2, 16, 108, C), F32),
-            ((2, 16, 108, C), BF16),
+            ((2, POS, C), BF16),
+            ((2, POS, C), BF16),
+            ((2, 16, PADDED, C), F32),
+            ((2, 16, PADDED, C), BF16),
         ],
         [
             ((F + 3, POS, C), BF16),
@@ -272,13 +310,14 @@
         ],
         flops=4 * CONV_FLOPS,
         moved=9 << 20,
-    )
-
-
-def conv(adjoint, slots, frames, cache, weight, base):
+        limit=44,
+    )
+
+
+def conv(adjoint, clips, frames, cache, weight, base):
     return call(
         functools.partial(conv_kernel, adjoint),
-        (slots, frames, cache, weight, base),
+        (clips, frames, cache, weight, base),
         1,
         [((F, POS, C), BF16)],
         [((F + 3, POS, C), BF16), ((9 * C, 3 * C), BF16)],
@@ -287,15 +326,26 @@
     )[0]
 
 
-def add_stage(own, keep, received, outer):
+def add_stage(axis, keep, received, outer):
     return call(
-        add_kernel,
-        (own, keep, *received),
-        1,
-        [((2, outer, 108, C), F32)] + [((2, outer, 108, C), BF16)] * 3,
-        flops=0,
-        moved=2 << 20,
-    )
+        functools.partial(add_kernel, axis),
+        (keep, *received),
+        0,
+        [((2, outer, PADDED, C), F32)] + [((2, outer, PADDED, C), BF16)] * 3,
+        moved=1 << 20,
+    )
+
+
+def halos(frames, cot):
+    pair = (2, POS, C)
+    return pl.pallas_call(
+        head_kernel,
+        grid=(1,),
+        out_shape=[jax.ShapeDtypeStruct(pair, BF16)] * 2,
+        in_specs=[pl.BlockSpec(pair, lambda i: (F // 2 - 1, 0, 0)), pl.BlockSpec(pair, lambda i: (0, 0, 0))],
+        out_specs=[pl.BlockSpec(pair, lambda i: (0, 0, 0))] * 2,
+        compiler_params=pltpu.CompilerParams(vmem_limit_bytes=4 << 20),
+    )(frames, cot)
 
 
 def shifted(value, steps):
@@ -308,48 +358,34 @@
     return lax.ppermute(value, "dp", [(source, target(source)) for source in range(32)])
 
 
-def slot_tables(clips, first_frame):
-    padded = jnp.concatenate(
-        [jnp.full((2,), -1, jnp.int32), clips, jnp.full((2,), -1, jnp.int32)]
-    )
-    near = lax.dynamic_slice_in_dim(padded, first_frame, F + 4)
-    frame = jnp.arange(F, dtype=jnp.int32)
-    current = near[2 : 2 + F]
-    past = jnp.stack(
-        [jnp.where(near[k : k + F] == current, frame + k, NONE) for k in range(3)], axis=1
-    )
-    following = jnp.stack(
-        [jnp.where(near[2 + q : 2 + q + F] == current, frame + q, NONE) for q in range(3)], axis=1
-    )
-    return past, following
-
-
 def per_device(frames, clip_ids, cotangent, conv1_weight, conv2_weight):
     own_frames = frames.reshape(F, POS, C)
     own_cot = cotangent.reshape(F, POS, C)
-    index = lax.axis_index("dp")
-    core, x, y = index % 2, (index // 2) % 4, index // 8
-    past, following = slot_tables(clip_ids[0], lax.axis_index("seq") * F)
-    cache = shifted(own_frames[F - 2 :], 1)
-    cot_next = shifted(own_cot[:2], -1)
-    hidden, act_grad, keep, send = main(
-        core[None], past, following, own_frames, cache, own_cot, cot_next, conv1_weight, conv2_weight
-    )
-    hidden_cache = shifted(hidden[F - 2 :], 1)
-    act_grad_next = shifted(act_grad[:2], -1)
+    tail, head = halos(own_frames, own_cot)
+    cache = shifted(tail, 1)
+    cot_next = shifted(head, -1)
+    hidden, act_grad, tail, head, keep, send = main(
+        clip_ids, own_frames, cache, own_cot, cot_next, conv1_weight, conv2_weight
+    )
     recv = dp_permute(send, lambda d: d ^ 1)
-    block_out = conv(False, past, hidden, hidden_cache, conv2_weight, own_frames)
-    input_grad = conv(True, following, act_grad, act_grad_next, conv1_weight, own_cot)
-
+    hidden_cache = shifted(tail, 1)
+    act_grad_next = shifted(head, -1)
     keep, *sent = add_stage(
-        x[None], keep.reshape(2, 4, 4, 108, C), [recv.reshape(2, 4, 4, 108, C)], 4
-    )
+        "x", keep.reshape(2, 4, 4, PADDED, C), [recv.reshape(2, 4, 4, PADDED, C)], 4
+    )
+    sent, hidden, act_grad = lax.optimization_barrier((sent, hidden, act_grad))
     recv = [
         dp_permute(part, lambda d, s=s: (d // 8) * 8 + (d % 8 + 2 * s) % 8)
         for s, part in zip((1, 2, 3), sent)
     ]
+    block_out = conv(False, clip_ids, hidden, hidden_cache, conv2_weight, own_frames)
+    input_grad = conv(True, clip_ids, act_grad, act_grad_next, conv1_weight, own_cot)
+    recv, block_out, input_grad = lax.optimization_barrier((recv, block_out, input_grad))
     keep, *sent = add_stage(
-        y[None], keep.reshape(2, 1, 4, 108, C), [part.reshape(2, 1, 4, 108, C) for part in recv], 1
+        "y",
+        keep.reshape(2, 1, 4, PADDED, C),
+        [part.reshape(2, 1, 4, PADDED, C) for part in recv],
+        1,
     )
     recv = [dp_permute(part, lambda d, s=s: (d + 8 * s) % 32) for s, part in zip((1, 2, 3), sent)]
     total = keep + recv[0].astype(F32) + recv[1].astype(F32) + recv[2].astype(F32)
@@ -360,7 +396,7 @@
     total = (total + near[1]) + (near[0] + near[2])
     total = total + lax.ppermute(total, "seq", [(z, z ^ 4) for z in range(8)])
     rows = lax.axis_size("dp") * lax.axis_size("seq") * F * POS
-    total = total.reshape(2, 108, C) * (F32(1.0) / jnp.sqrt(F32(rows)))
+    total = total.reshape(2, PADDED, C)[:, :BLOCK] * (F32(1.0) / jnp.sqrt(F32(rows)))
     return (
         block_out.reshape(frames.shape),
         input_grad.reshape(frames.shape),

time: 94.9 us -> 88.1 us (0.928)
  Pallas kernels: 30.7 us -> 21.6 us
  waiting for transfers between devices: 16.2 us -> 25.1 us
  other arithmetic: 2.46 us -> 0.08 us
  local copies, waits for them, and re-layouts: 9.95 us -> 7.8 us
  starting transfers between devices: 33.9 us -> 32.3 us
    pallas_call x5, Pallas kernels: 30.7 us -> 21.6 us  [call(): pl.pallas_call(kernel, out_shape=[jax.ShapeDtypeStruct(shape, dtype) for...]
    ppermute x7, waiting for transfers between devices: 13.1 us -> 4.29 us  [dp_permute(): lax.ppermute(value, 'dp', [(source, target(source)) for source in range(3...]
    ppermute x1, waiting for transfers between devices: 0.01 us -> 6.76 us  [per_device(): total = total + lax.ppermute(total, 'seq', [(z, z ^ 4) for z in range(8)])]
    ppermute x3, waiting for transfers between devices: 2.35 us -> 8.34 us  [per_device(): lax.ppermute(total, 'seq', [(z, z // 4 * 4 + (z + s) % 4) for z in range(...]
    ppermute x4, waiting for transfers between devices: 0.73 us -> 5.74 us  [shifted(): lax.ppermute(value, 'seq', [(source, source + steps) for source in range(...]
    unnamed x14 -> x16, local copies, waits for them, and re-layouts: 2.65 us -> 7.16 us
    slice x4 -> x0, local copies, waits for them, and re-layouts: 3.66 us -> none  [the longest x1 0.92 us: per_device(): cache = shifted(own_frames[F - 2:], 1)]
    ppermute x4, starting transfers between devices: 12.2 us -> 10.4 us  [shifted(): lax.ppermute(value, 'seq', [(source, source + steps) for source in range(...]
  transfers between devices with their start and end apart: 15 -> 15, of which waited for: 6 -> 10; matrix products, arithmetic and copies ran while one was open for 6% -> 0% of each run, Pallas kernels for 11% -> 10%
where the time goes in v1:
time: 88.1 us; the launch traced here: 87.6 us
  starting transfers between devices  32.3 us (37%)
  waiting for transfers between devices  25.1 us (28%)
  Pallas kernels  21.6 us (25%)
  local copies, waits for them, and re-layouts  7.8 us (9%)
    pallas_call x5, Pallas kernels, call(): pl.pallas_call(kernel, out_shape=[jax.ShapeDtypeStruct(shape, dtype) for...  21.6 us
    ppermute x7, starting transfers between devices, dp_permute(): lax.ppermute(value, 'dp', [(source, target(source)) for source in range(3...  10.9 us
    ppermute x4, starting transfers between devices, shifted(): lax.ppermute(value, 'seq', [(source, source + steps) for source in range(...  10.4 us
    ppermute x3, waiting for transfers between devices, per_device(): lax.ppermute(total, 'seq', [(z, z // 4 * 4 + (z + s) % 4) for z in range(...  8.34 us
    ppermute x3, starting transfers between devices, per_device(): lax.ppermute(total, 'seq', [(z, z // 4 * 4 + (z + s) % 4) for z in range(...  8.25 us
    unnamed x16, local copies, waits for them, and re-layouts  7.16 us
    ppermute x1, waiting for transfers between devices, per_device(): total = total + lax.ppermute(total, 'seq', [(z, z ^ 4) for z in range(8)])  6.76 us
    ppermute x4, waiting for transfers between devices, shifted(): lax.ppermute(value, 'seq', [(source, source + steps) for source in range(...  5.74 us
  transfers between devices with their start and end apart: 15, of which 10 were waited for; matrix products, arithmetic and copies ran while one was open for 0% of the time, Pallas kernels for 10%

profile of v1, /device:TPU:2, one launch (start us, length us, event | category | flops | bytes accessed | tf_op | source)
XLA Modules:
  0.0 87.6 jit_solution(16881983881255495448)
XLA Ops:
  0.6 0.0 copy-start
  0.6 1.0 %copy-done = bf16[1,8,8,32,128]{4,3,2,1,0:T(8,128)(2,1)S(1)} copy-done((bf16[1,8,8,32,128]{4,3,2,1,0:T(8,128)(2,1)S(1)}, bf16[1,8,8,32,128]{4,3,2,1,0:T(8,128)(2,1)}, u32[]{:S(2)}) %copy-start) | copy-done | bytes 524312
  1.7 0.0 copy-start.2
  1.7 1.0 %copy-done.2 = bf16[1,8,8,32,128]{4,3,2,1,0:T(8,128)(2,1)S(1)} copy-done((bf16[1,8,8,32,128]{4,3,2,1,0:T(8,128)(2,1)S(1)}, bf16[1,8,8,32,128]{4,3,2,1,0:T(8,128)(2,1)}, u32[]{:S(2)}) %copy-start.2) | copy-done | bytes 524312
  2.7 3.8 %collective-permute-start = (bf16[2,256,128]{2,1,0:T(8,128)(2,1)S(1)}, bf16[2,256,128]{2,1,0:T(8,128)(2,1)S(1)}, u32[]{:S(2)}, u32[]{:S(2)}) collective-permute-start(bf16[2,256,128]{2,1,0:T(8,128)(2,1)S(1)} %get-tuple-element.30), channel_id=1, source_target_pairs={{0,32},{32,64},{64,96},{96,128},{128,160},{160,192},{192,224},{1,3... | collective-permute-start | bytes 393224 | tf_op jit(solution)/shard_map/ppermute | solution.py:354
  6.6 1.3 %collective-permute-start.1 = (bf16[2,256,128]{2,1,0:T(8,128)(2,1)S(1)}, bf16[2,256,128]{2,1,0:T(8,128)(2,1)S(1)}, u32[]{:S(2)}, u32[]{:S(2)}) collective-permute-start(bf16[2,256,128]{2,1,0:T(8,128)(2,1)S(1)} %get-tuple-element.31), channel_id=1, source_target_pairs={{32,0},{64,32},{96,64},{128,96},{160,128},{192,160},{224,192},{33,... | collective-permute-start | bytes 393224 | tf_op jit(solution)/shard_map/ppermute | solution.py:354
  7.9 1.4 %collective-permute-done.cache_ref = bf16[2,256,128]{2,1,0:T(8,128)(2,1)S(1)} collective-permute-done((bf16[2,256,128]{2,1,0:T(8,128)(2,1)S(1)}, bf16[2,256,128]{2,1,0:T(8,128)(2,1)S(1)}, u32[]{:S(2)}, u32[]{:S(2)}) %collective-permute-start) | collective-permute-done | bytes 131104 | tf_op jit(solution)/shard_map/ppermute | solution.py:354
  9.3 4.3 %collective-permute-done.1.cot_next_ref = bf16[2,256,128]{2,1,0:T(8,128)(2,1)S(1)} collective-permute-done((bf16[2,256,128]{2,1,0:T(8,128)(2,1)S(1)}, bf16[2,256,128]{2,1,0:T(8,128)(2,1)S(1)}, u32[]{:S(2)}, u32[]{:S(2)}) %collective-permute-start.1) | collective-permute-done | bytes 131104 | tf_op jit(solution)/shard_map/ppermute | solution.py:354
  13.6 0.0 copy-start.1
  13.6 1.0 %copy-done.1 = bf16[1,8,8,32,128]{4,3,2,1,0:T(8,128)(2,1)S(1)} copy-done((bf16[1,8,8,32,128]{4,3,2,1,0:T(8,128)(2,1)S(1)}, bf16[1,8,8,32,128]{4,3,2,1,0:T(8,128)(2,1)}, u32[]{:S(2)}) %copy-start.1) | copy-done | bytes 524312
  14.6 0.0 copy-start.3
  14.7 1.0 %copy-done.3 = bf16[1,8,8,32,128]{4,3,2,1,0:T(8,128)(2,1)S(1)} copy-done((bf16[1,8,8,32,128]{4,3,2,1,0:T(8,128)(2,1)S(1)}, bf16[1,8,8,32,128]{4,3,2,1,0:T(8,128)(2,1)}, u32[]{:S(2)}) %copy-start.3) | copy-done | bytes 524312
  15.7 0.0 copy-start.4
  15.7 1.2 %copy-done.4 = bf16[3456,128]{1,0:T(8,128)(2,1)S(1)} copy-done((bf16[3456,128]{1,0:T(8,128)(2,1)S(1)}, bf16[3456,128]{1,0:T(8,128)(2,1)}, u32[]{:S(2)}) %copy-start.4) | copy-done | bytes 884760
  16.9 0.0 copy-start.5
  16.9 1.2 %copy-done.5 = bf16[3456,128]{1,0:T(8,128)(2,1)S(1)} copy-done((bf16[3456,128]{1,0:T(8,128)(2,1)S(1)}, bf16[3456,128]{1,0:T(8,128)(2,1)}, u32[]{:S(2)}) %copy-start.5) | copy-done | bytes 884760
  18.0 0.0 copy-start.6
  18.0 0.7 copy-done.6
  18.7 12.8 %shard_map.85 = (bf16[8,256,128]{2,1,0:T(8,128)(2,1)S(1)}, bf16[8,256,128]{2,1,0:T(8,128)(2,1)S(1)}, bf16[2,256,128]{2,1,0:T(8,128)(2,1)S(1)}, bf16[2,256,128]{2...) custom-call(s32[1,64]{1,0:T(1,128)S(1)} %copy-done.6, ...), custom_call_target="tpu_custom_call" | custom-call | flops 7247757312 | bytes 9437184 | tf_op jit(solution)/shard_map/pallas_call | solution.py:269
  31.5 0.0 copy-start.7
  31.5 0.1 collective-permute-start.2
  31.6 3.8 %collective-permute-start.6 = (bf16[2,256,128]{2,1,0:T(8,128)(2,1)S(1)}, bf16[2,256,128]{2,1,0:T(8,128)(2,1)S(1)}, u32[]{:S(2)}, u32[]{:S(2)}) collective-permute-start(bf16[2,256,128]{2,1,0:T(8,128)(2,1)S(1)} %get-tuple-element.43), channel_id=1, source_target_pairs={{0,32},{32,64},{64,96},{96,128},{128,160},{160,192},{192,224},{1,3... | collective-permute-start | bytes 393224 | tf_op jit(solution)/shard_map/ppermute | solution.py:354
  35.5 1.5 %collective-permute-start.7 = (bf16[2,256,128]{2,1,0:T(8,128)(2,1)S(1)}, bf16[2,256,128]{2,1,0:T(8,128)(2,1)S(1)}, u32[]{:S(2)}, u32[]{:S(2)}) collective-permute-start(bf16[2,256,128]{2,1,0:T(8,128)(2,1)S(1)} %get-tuple-element.45), channel_id=1, source_target_pairs={{32,0},{64,32},{96,64},{128,96},{160,128},{192,160},{224,192},{33,... | collective-permute-start | bytes 393224 | tf_op jit(solution)/shard_map/ppermute | solution.py:354
  36.9 0.0 collective-permute-done.2
  37.0 0.2 shard_map.86
  37.2 1.6 %collective-permute-start.3 = (bf16[2,4,112,128]{3,2,1,0:T(8,128)(2,1)S(1)}, bf16[2,4,112,128]{3,2,1,0:T(8,128)(2,1)S(1)}, u32[]{:S(2)}, u32[]{:S(2)}) collective-permute-start(bf16[2,4,112,128]{3,2,1,0:T(8,128)(2,1)S(1)} %get-tuple-element.39), channel_id=1, source_target_pairs={{0,2},{1,3},{2,4},{3,5},{4,6},{5,7},{6,0},{7,1},{8,10},{9,11},{10,... | collective-permute-start | bytes 688136 | tf_op jit(solution)/shard_map/ppermute | solution.py:358
  38.7 1.1 %collective-permute-start.4 = (bf16[2,4,112,128]{3,2,1,0:T(8,128)(2,1)S(1)}, bf16[2,4,112,128]{3,2,1,0:T(8,128)(2,1)S(1)}, u32[]{:S(2)}, u32[]{:S(2)}) collective-permute-start(bf16[2,4,112,128]{3,2,1,0:T(8,128)(2,1)S(1)} %get-tuple-element.40), channel_id=1, source_target_pairs={{0,4},{1,5},{2,6},{3,7},{4,0},{5,1},{6,2},{7,3},{8,12},{9,13},{10,... | collective-permute-start | bytes 688136 | tf_op jit(solution)/shard_map/ppermute | solution.py:358
  39.8 2.2 %collective-permute-start.5 = (bf16[2,4,112,128]{3,2,1,0:T(8,128)(2,1)S(1)}, bf16[2,4,112,128]{3,2,1,0:T(8,128)(2,1)S(1)}, u32[]{:S(2)}, u32[]{:S(2)}) collective-permute-start(bf16[2,4,112,128]{3,2,1,0:T(8,128)(2,1)S(1)} %get-tuple-element.41), channel_id=1, source_target_pairs={{0,6},{1,7},{2,0},{3,1},{4,2},{5,3},{6,4},{7,5},{8,14},{9,15},{10,... | collective-permute-start | bytes 688136 | tf_op jit(solution)/shard_map/ppermute | solution.py:358
  42.0 0.0 collective-permute-done.6.cache_ref
  42.0 0.0 copy-done.7
  42.0 4.2 %shard_map.87 = bf16[8,256,128]{2,1,0:T(8,128)(2,1)} custom-call(s32[1,64]{1,0:T(1,128)S(1)} %copy-done.7, bf16[8,256,128]{2,1,0:T(8,128)(2,1)S(1)} %get-tuple-element.42.frames_ref, bf16[2,256,128]{2,1,0:T(8,128)(2,1)S(1)} %collective-permute-done.6.cache_ref, bf16[3456,128]{1,0:T(8,128)(2,1)S(1)} %copy-done.4, bf16[8,256,128]{2,1,0:T(8,128)(2,1)S(1)} %bitcast.20), custom_call_target="tpu_custom_call" | custom-call | flops 1811939328 | bytes 3145728 | tf_op jit(solution)/shard_map/pallas_call | solution.py:269
  46.2 0.0 collective-permute-done.7.cache_ref
  46.2 4.3 %shard_map.88 = bf16[8,256,128]{2,1,0:T(8,128)(2,1)} custom-call(s32[1,64]{1,0:T(1,128)S(1)} %copy-done.7, bf16[8,256,128]{2,1,0:T(8,128)(2,1)S(1)} %get-tuple-element.44.frames_ref, bf16[2,256,128]{2,1,0:T(8,128)(2,1)S(1)} %collective-permute-done.7.cache_ref, bf16[3456,128]{1,0:T(8,128)(2,1)S(1)} %copy-done.5, bf16[8,256,128]{2,1,0:T(8,128)(2,1)S(1)} %bitcast.23), custom_call_target="tpu_custom_call" | custom-call | flops 1811939328 | bytes 3145728 | tf_op jit(solution)/shard_map/pallas_call | solution.py:269
  50.4 0.0 collective-permute-done.3
  50.4 0.0 collective-permute-done.4
  50.4 1.5 %collective-permute-done.5 = bf16[2,4,112,128]{3,2,1,0:T(8,128)(2,1)S(1)} collective-permute-done((bf16[2,4,112,128]{3,2,1,0:T(8,128)(2,1)S(1)}, bf16[2,4,112,128]{3,2,1,0:T(8,128)(2,1)S(1)}, u32[]{:S(2)}, u32[]{:S(2)}) %collective-permute-start.5) | collective-permute-done | bytes 229408 | tf_op jit(solution)/shard_map/ppermute | solution.py:358
  51.9 0.1 shard_map.89
  52.0 1.7 %collective-permute-start.8 = (bf16[2,1,112,128]{3,2,1,0:T(8,128)(2,1)S(1)}, bf16[2,1,112,128]{3,2,1,0:T(8,128)(2,1)S(1)}, u32[]{:S(2)}, u32[]{:S(2)}) collective-permute-start(bf16[2,1,112,128]{3,2,1,0:T(8,128)(2,1)S(1)} %get-tuple-element.53), channel_id=1, source_target_pairs={{0,8},{1,9},{2,10},{3,11},{4,12},{5,13},{6,14},{7,15},{8,16},{9,17... | collective-permute-start | bytes 172040 | tf_op jit(solution)/shard_map/ppermute | solution.py:358
  53.7 2.9 %collective-permute-start.9 = (bf16[2,1,112,128]{3,2,1,0:T(8,128)(2,1)S(1)}, bf16[2,1,112,128]{3,2,1,0:T(8,128)(2,1)S(1)}, u32[]{:S(2)}, u32[]{:S(2)}) collective-permute-start(bf16[2,1,112,128]{3,2,1,0:T(8,128)(2,1)S(1)} %get-tuple-element.54), channel_id=1, source_target_pairs={{0,16},{1,17},{2,18},{3,19},{4,20},{5,21},{6,22},{7,23},{8,24},{9,... | collective-permute-start | bytes 172040 | tf_op jit(solution)/shard_map/ppermute | solution.py:358
  56.6 1.4 %collective-permute-start.10 = (bf16[2,1,112,128]{3,2,1,0:T(8,128)(2,1)S(1)}, bf16[2,1,112,128]{3,2,1,0:T(8,128)(2,1)S(1)}, u32[]{:S(2)}, u32[]{:S(2)}) collective-permute-start(bf16[2,1,112,128]{3,2,1,0:T(8,128)(2,1)S(1)} %get-tuple-element.55), channel_id=1, source_target_pairs={{0,24},{1,25},{2,26},{3,27},{4,28},{5,29},{6,30},{7,31},{8,0},{9,1... | collective-permute-start | bytes 172040 | tf_op jit(solution)/shard_map/ppermute | solution.py:358
  57.9 0.2 collective-permute-done.8
  58.1 1.3 %collective-permute-done.9 = bf16[2,1,112,128]{3,2,1,0:T(8,128)(2,1)S(1)} collective-permute-done((bf16[2,1,112,128]{3,2,1,0:T(8,128)(2,1)S(1)}, bf16[2,1,112,128]{3,2,1,0:T(8,128)(2,1)S(1)}, u32[]{:S(2)}, u32[]{:S(2)}) %collective-permute-start.9) | collective-permute-done | bytes 57376 | tf_op jit(solution)/shard_map/ppermute | solution.py:358
  59.4 1.4 %collective-permute-done.10 = bf16[2,1,112,128]{3,2,1,0:T(8,128)(2,1)S(1)} collective-permute-done((bf16[2,1,112,128]{3,2,1,0:T(8,128)(2,1)S(1)}, bf16[2,1,112,128]{3,2,1,0:T(8,128)(2,1)S(1)}, u32[]{:S(2)}, u32[]{:S(2)}) %collective-permute-start.10) | collective-permute-done | bytes 57376 | tf_op jit(solution)/shard_map/ppermute | solution.py:358
  60.8 7.4 %collective-permute-start.13 = (f32[2,1,112,128]{3,2,1,0:T(8,128)S(1)}, f32[2,1,112,128]{3,2,1,0:T(8,128)S(1)}, u32[]{:S(2)}, u32[]{:S(2)}) collective-permute-start(f32[2,1,112,128]{3,2,1,0:T(8,128)S(1)} %convert_add_fusion), channel_id=1, source_target_pairs={{0,96},{32,0},{64,32},{96,64},{128,224},{160,128},{192,160},{224,1... | collective-permute-start | bytes 344072 | tf_op jit(solution)/shard_map/ppermute | solution.py:393
  68.2 0.0 collective-permute-start.12
  68.2 0.9 collective-permute-start.11
  69.1 2.5 %collective-permute-done.13 = f32[2,1,112,128]{3,2,1,0:T(8,128)S(1)} collective-permute-done((f32[2,1,112,128]{3,2,1,0:T(8,128)S(1)}, f32[2,1,112,128]{3,2,1,0:T(8,128)S(1)}, u32[]{:S(2)}, u32[]{:S(2)}) %collective-permute-start.13) | collective-permute-done | bytes 114720 | tf_op jit(solution)/shard_map/ppermute | solution.py:393
  71.6 3.3 %collective-permute-done.12 = f32[2,1,112,128]{3,2,1,0:T(8,128)S(1)} collective-permute-done((f32[2,1,112,128]{3,2,1,0:T(8,128)S(1)}, f32[2,1,112,128]{3,2,1,0:T(8,128)S(1)}, u32[]{:S(2)}, u32[]{:S(2)}) %collective-permute-start.12) | collective-permute-done | bytes 114720 | tf_op jit(solution)/shard_map/ppermute | solution.py:393
  74.9 2.5 %collective-permute-done.11 = f32[2,1,112,128]{3,2,1,0:T(8,128)S(1)} collective-permute-done((f32[2,1,112,128]{3,2,1,0:T(8,128)S(1)}, f32[2,1,112,128]{3,2,1,0:T(8,128)S(1)}, u32[]{:S(2)}, u32[]{:S(2)}) %collective-permute-start.11) | collective-permute-done | bytes 114720 | tf_op jit(solution)/shard_map/ppermute | solution.py:393
  77.4 2.8 %collective-permute-start.14 = (f32[2,1,112,128]{3,2,1,0:T(8,128)S(1)}, f32[2,1,112,128]{3,2,1,0:T(8,128)S(1)}, u32[]{:S(2)}, u32[]{:S(2)}) collective-permute-start(f32[2,1,112,128]{3,2,1,0:T(8,128)S(1)} %add_add_fusion), channel_id=1, source_target_pairs={{0,128},{32,160},{64,192},{96,224},{128,0},{160,32},{192,64},{224,... | collective-permute-start | bytes 344072 | tf_op jit(solution)/shard_map/ppermute | solution.py:397
  80.2 6.8 %collective-permute-done.14 = f32[2,1,112,128]{3,2,1,0:T(8,128)S(1)} collective-permute-done((f32[2,1,112,128]{3,2,1,0:T(8,128)S(1)}, f32[2,1,112,128]{3,2,1,0:T(8,128)S(1)}, u32[]{:S(2)}, u32[]{:S(2)}) %collective-permute-start.14) | collective-permute-done | bytes 114720 | tf_op jit(solution)/shard_map/ppermute | solution.py:397
  87.0 0.6 slice_bitcast_fusion
  (5 shorter events, 0.1 us)
Async XLA Ops:
  0.6 1.0 %copy-start = (bf16[1,8,8,32,128]{4,3,2,1,0:T(8,128)(2,1)S(1)}, bf16[1,8,8,32,128]{4,3,2,1,0:T(8,128)(2,1)}, u32[]{:S(2)}) copy-start(bf16[1,8,8,32,128]{4,3,2,1,0:T(8,128)(2,1)} %param.5) | copy-start | bytes 1572868
  1.7 1.0 %copy-start.2 = (bf16[1,8,8,32,128]{4,3,2,1,0:T(8,128)(2,1)S(1)}, bf16[1,8,8,32,128]{4,3,2,1,0:T(8,128)(2,1)}, u32[]{:S(2)}) copy-start(bf16[1,8,8,32,128]{4,3,2,1,0:T(8,128)(2,1)} %param.7) | copy-start | bytes 1572868
  2.7 6.6 %collective-permute-start = (bf16[2,256,128]{2,1,0:T(8,128)(2,1)S(1)}, bf16[2,256,128]{2,1,0:T(8,128)(2,1)S(1)}, u32[]{:S(2)}, u32[]{:S(2)}) collective-permute-start(bf16[2,256,128]{2,1,0:T(8,128)(2,1)S(1)} %get-tuple-element.30), channel_id=1, source_target_pairs={{0,32},{32,64},{64,96},{96,128},{128,160},{160,192},{192,224},{1,3... | collective-permute-start | bytes 393224 | tf_op jit(solution)/shard_map/ppermute | solution.py:354
  6.6 7.0 %collective-permute-start.1 = (bf16[2,256,128]{2,1,0:T(8,128)(2,1)S(1)}, bf16[2,256,128]{2,1,0:T(8,128)(2,1)S(1)}, u32[]{:S(2)}, u32[]{:S(2)}) collective-permute-start(bf16[2,256,128]{2,1,0:T(8,128)(2,1)S(1)} %get-tuple-element.31), channel_id=1, source_target_pairs={{32,0},{64,32},{96,64},{128,96},{160,128},{192,160},{224,192},{33,... | collective-permute-start | bytes 393224 | tf_op jit(solution)/shard_map/ppermute | solution.py:354
  13.6 1.0 %copy-start.1 = (bf16[1,8,8,32,128]{4,3,2,1,0:T(8,128)(2,1)S(1)}, bf16[1,8,8,32,128]{4,3,2,1,0:T(8,128)(2,1)}, u32[]{:S(2)}) copy-start(bf16[1,8,8,32,128]{4,3,2,1,0:T(8,128)(2,1)} %param.5) | copy-start | bytes 1572868
  14.6 1.0 %copy-start.3 = (bf16[1,8,8,32,128]{4,3,2,1,0:T(8,128)(2,1)S(1)}, bf16[1,8,8,32,128]{4,3,2,1,0:T(8,128)(2,1)}, u32[]{:S(2)}) copy-start(bf16[1,8,8,32,128]{4,3,2,1,0:T(8,128)(2,1)} %param.7) | copy-start | bytes 1572868
  15.7 1.2 %copy-start.4 = (bf16[3456,128]{1,0:T(8,128)(2,1)S(1)}, bf16[3456,128]{1,0:T(8,128)(2,1)}, u32[]{:S(2)}) copy-start(bf16[3456,128]{1,0:T(8,128)(2,1)} %weight_ref.2) | copy-start | bytes 2654212
  16.9 1.2 %copy-start.5 = (bf16[3456,128]{1,0:T(8,128)(2,1)S(1)}, bf16[3456,128]{1,0:T(8,128)(2,1)}, u32[]{:S(2)}) copy-start(bf16[3456,128]{1,0:T(8,128)(2,1)} %weight_ref.3) | copy-start | bytes 2654212
  18.0 0.7 copy-start.6
  31.5 10.5 %copy-start.7 = (s32[1,64]{1,0:T(1,128)S(1)}, s32[1,64]{1,0:T(1,128)}, u32[]{:S(2)}) copy-start(s32[1,64]{1,0:T(1,128)} %clips.5) | copy-start | bytes 772
  31.5 5.4 %collective-permute-start.2 = (bf16[2,16,112,128]{3,2,1,0:T(8,128)(2,1)S(1)}, bf16[2,16,112,128]{3,2,1,0:T(8,128)(2,1)S(1)}, u32[]{:S(2)}, u32[]{:S(2)}) collective-permute-start(bf16[2,16,112,128]{3,2,1,0:T(8,128)(2,1)S(1)} %get-tuple-element.33), channel_id=1, source_target_pairs={{0,1},{1,0},{2,3},{3,2},{4,5},{5,4},{6,7},{7,6},{8,9},{9,8},{10,11... | collective-permute-start | bytes 2752520 | tf_op jit(solution)/shard_map/ppermute | solution.py:358
  31.6 10.4 %collective-permute-start.6 = (bf16[2,256,128]{2,1,0:T(8,128)(2,1)S(1)}, bf16[2,256,128]{2,1,0:T(8,128)(2,1)S(1)}, u32[]{:S(2)}, u32[]{:S(2)}) collective-permute-start(bf16[2,256,128]{2,1,0:T(8,128)(2,1)S(1)} %get-tuple-element.43), channel_id=1, source_target_pairs={{0,32},{32,64},{64,96},{96,128},{128,160},{160,192},{192,224},{1,3... | collective-permute-start | bytes 393224 | tf_op jit(solution)/shard_map/ppermute | solution.py:354
  35.5 10.7 %collective-permute-start.7 = (bf16[2,256,128]{2,1,0:T(8,128)(2,1)S(1)}, bf16[2,256,128]{2,1,0:T(8,128)(2,1)S(1)}, u32[]{:S(2)}, u32[]{:S(2)}) collective-permute-start(bf16[2,256,128]{2,1,0:T(8,128)(2,1)S(1)} %get-tuple-element.45), channel_id=1, source_target_pairs={{32,0},{64,32},{96,64},{128,96},{160,128},{192,160},{224,192},{33,... | collective-permute-start | bytes 393224 | tf_op jit(solution)/shard_map/ppermute | solution.py:354
  37.2 13.3 %collective-permute-start.3 = (bf16[2,4,112,128]{3,2,1,0:T(8,128)(2,1)S(1)}, bf16[2,4,112,128]{3,2,1,0:T(8,128)(2,1)S(1)}, u32[]{:S(2)}, u32[]{:S(2)}) collective-permute-start(bf16[2,4,112,128]{3,2,1,0:T(8,128)(2,1)S(1)} %get-tuple-element.39), channel_id=1, source_target_pairs={{0,2},{1,3},{2,4},{3,5},{4,6},{5,7},{6,0},{7,1},{8,10},{9,11},{10,... | collective-permute-start | bytes 688136 | tf_op jit(solution)/shard_map/ppermute | solution.py:358
  38.7 11.7 %collective-permute-start.4 = (bf16[2,4,112,128]{3,2,1,0:T(8,128)(2,1)S(1)}, bf16[2,4,112,128]{3,2,1,0:T(8,128)(2,1)S(1)}, u32[]{:S(2)}, u32[]{:S(2)}) collective-permute-start(bf16[2,4,112,128]{3,2,1,0:T(8,128)(2,1)S(1)} %get-tuple-element.40), channel_id=1, source_target_pairs={{0,4},{1,5},{2,6},{3,7},{4,0},{5,1},{6,2},{7,3},{8,12},{9,13},{10,... | collective-permute-start | bytes 688136 | tf_op jit(solution)/shard_map/ppermute | solution.py:358
  39.8 12.1 %collective-permute-start.5 = (bf16[2,4,112,128]{3,2,1,0:T(8,128)(2,1)S(1)}, bf16[2,4,112,128]{3,2,1,0:T(8,128)(2,1)S(1)}, u32[]{:S(2)}, u32[]{:S(2)}) collective-permute-start(bf16[2,4,112,128]{3,2,1,0:T(8,128)(2,1)S(1)} %get-tuple-element.41), channel_id=1, source_target_pairs={{0,6},{1,7},{2,0},{3,1},{4,2},{5,3},{6,4},{7,5},{8,14},{9,15},{10,... | collective-permute-start | bytes 688136 | tf_op jit(solution)/shard_map/ppermute | solution.py:358
  52.0 6.1 %collective-permute-start.8 = (bf16[2,1,112,128]{3,2,1,0:T(8,128)(2,1)S(1)}, bf16[2,1,112,128]{3,2,1,0:T(8,128)(2,1)S(1)}, u32[]{:S(2)}, u32[]{:S(2)}) collective-permute-start(bf16[2,1,112,128]{3,2,1,0:T(8,128)(2,1)S(1)} %get-tuple-element.53), channel_id=1, source_target_pairs={{0,8},{1,9},{2,10},{3,11},{4,12},{5,13},{6,14},{7,15},{8,16},{9,17... | collective-permute-start | bytes 172040 | tf_op jit(solution)/shard_map/ppermute | solution.py:358
  53.7 5.7 %collective-permute-start.9 = (bf16[2,1,112,128]{3,2,1,0:T(8,128)(2,1)S(1)}, bf16[2,1,112,128]{3,2,1,0:T(8,128)(2,1)S(1)}, u32[]{:S(2)}, u32[]{:S(2)}) collective-permute-start(bf16[2,1,112,128]{3,2,1,0:T(8,128)(2,1)S(1)} %get-tuple-element.54), channel_id=1, source_target_pairs={{0,16},{1,17},{2,18},{3,19},{4,20},{5,21},{6,22},{7,23},{8,24},{9,... | collective-permute-start | bytes 172040 | tf_op jit(solution)/shard_map/ppermute | solution.py:358
  56.6 4.2 %collective-permute-start.10 = (bf16[2,1,112,128]{3,2,1,0:T(8,128)(2,1)S(1)}, bf16[2,1,112,128]{3,2,1,0:T(8,128)(2,1)S(1)}, u32[]{:S(2)}, u32[]{:S(2)}) collective-permute-start(bf16[2,1,112,128]{3,2,1,0:T(8,128)(2,1)S(1)} %get-tuple-element.55), channel_id=1, source_target_pairs={{0,24},{1,25},{2,26},{3,27},{4,28},{5,29},{6,30},{7,31},{8,0},{9,1... | collective-permute-start | bytes 172040 | tf_op jit(solution)/shard_map/ppermute | solution.py:358
  60.8 10.8 %collective-permute-start.13 = (f32[2,1,112,128]{3,2,1,0:T(8,128)S(1)}, f32[2,1,112,128]{3,2,1,0:T(8,128)S(1)}, u32[]{:S(2)}, u32[]{:S(2)}) collective-permute-start(f32[2,1,112,128]{3,2,1,0:T(8,128)S(1)} %convert_add_fusion), channel_id=1, source_target_pairs={{0,96},{32,0},{64,32},{96,64},{128,224},{160,128},{192,160},{224,1... | collective-permute-start | bytes 344072 | tf_op jit(solution)/shard_map/ppermute | solution.py:393
  68.2 6.7 %collective-permute-start.12 = (f32[2,1,112,128]{3,2,1,0:T(8,128)S(1)}, f32[2,1,112,128]{3,2,1,0:T(8,128)S(1)}, u32[]{:S(2)}, u32[]{:S(2)}) collective-permute-start(f32[2,1,112,128]{3,2,1,0:T(8,128)S(1)} %convert_add_fusion), channel_id=1, source_target_pairs={{0,32},{32,64},{64,96},{96,0},{128,160},{160,192},{192,224},{224,1... | collective-permute-start | bytes 344072 | tf_op jit(solution)/shard_map/ppermute | solution.py:393
  68.2 9.2 %collective-permute-start.11 = (f32[2,1,112,128]{3,2,1,0:T(8,128)S(1)}, f32[2,1,112,128]{3,2,1,0:T(8,128)S(1)}, u32[]{:S(2)}, u32[]{:S(2)}) collective-permute-start(f32[2,1,112,128]{3,2,1,0:T(8,128)S(1)} %convert_add_fusion), channel_id=1, source_target_pairs={{0,64},{32,96},{64,0},{96,32},{128,192},{160,224},{192,128},{224,1... | collective-permute-start | bytes 344072 | tf_op jit(solution)/shard_map/ppermute | solution.py:393
  77.4 9.5 %collective-permute-start.14 = (f32[2,1,112,128]{3,2,1,0:T(8,128)S(1)}, f32[2,1,112,128]{3,2,1,0:T(8,128)S(1)}, u32[]{:S(2)}, u32[]{:S(2)}) collective-permute-start(f32[2,1,112,128]{3,2,1,0:T(8,128)S(1)} %add_add_fusion), channel_id=1, source_target_pairs={{0,128},{32,160},{64,192},{96,224},{128,0},{160,32},{192,64},{224,... | collective-permute-start | bytes 344072 | tf_op jit(solution)/shard_map/ppermute | solution.py:397

commit v2 on v1

v2 whole, which is shorter than its diff:
```python
import jax
import jax.numpy as jnp
from jax import lax
from jax.experimental import pallas as pl
from jax.experimental.pallas import tpu as pltpu
from jax.sharding import PartitionSpec as P

C = 128
GROUP = 4
F = 8
HT = 8
WT = 32
POS = HT * WT
BLOCK = 108
PADDED = 112
BF16 = jnp.bfloat16
F32 = jnp.float32


def clip_at(clips, frame):
    return clips[0, jnp.clip(frame, 0, clips.shape[1] - 1)]


def past_slots(clips, first, t, base, none):
    slots = []
    for k in range(3):
        frame = first + t + k - 2
        same = clip_at(clips, frame) == clip_at(clips, first + t)
        slots.append(jnp.where(same & (frame >= 0), t + k - 2 + base, none))
    return slots


def next_slots(clips, first, t, base, none):
    slots = []
    for q in range(3):
        frame = first + t + q
        same = clip_at(clips, frame) == clip_at(clips, first + t)
        slots.append(jnp.where(same & (frame < clips.shape[1]), t + q + base, none))
    return slots


def column(rows):
    return lax.broadcasted_iota(jnp.int32, (rows, C), 0) % WT


def shift_down(value):
    return jnp.where(column(POS) == 0, 0.0, pltpu.roll(value, 1, 0))


def shift_up(value):
    return jnp.where(column(POS) == WT - 1, 0.0, pltpu.roll(value, POS - 1, 0))


def row_pieces(frame):
    edge = jnp.zeros((WT, C), frame.dtype)
    return [
        jnp.concatenate([edge, frame[: POS - WT]], axis=0),
        frame,
        jnp.concatenate([frame[WT:], edge], axis=0),
    ]


def column_pieces(frame):
    wide = frame.astype(F32)
    return jnp.concatenate([shift_up(wide).astype(BF16), frame, shift_down(wide).astype(BF16)], axis=1)


def conv_frame(window, slots, weight):
    pieces = []
    for slot in slots:
        pieces += row_pieces(window[slot])
    taps = jnp.dot(jnp.concatenate(pieces, axis=1), weight[...], preferred_element_type=F32)
    return shift_down(taps[:, :C]) + taps[:, C : 2 * C] + shift_up(taps[:, 2 * C :])


def forward_weight(weight_ref, out_ref):
    for outer in range(9):
        for b in range(3):
            out_ref[outer * C : (outer + 1) * C, b * C : (b + 1) * C] = weight_ref[
                (outer * 3 + b) * C : (outer * 3 + b + 1) * C, :
            ]


def adjoint_weight(weight_ref, out_ref):
    for outer in range(9):
        for b in range(3):
            tap = 26 - (outer * 3 + b)
            out_ref[outer * C : (outer + 1) * C, b * C : (b + 1) * C] = weight_ref[
                tap * C : (tap + 1) * C, :
            ].T


def group_mean(sums):
    count = len(sums)
    sums = jnp.concatenate(sums + [jnp.zeros_like(sums[0])] * (F - count), axis=0)
    lane = lax.broadcasted_iota(jnp.int32, sums.shape, 1)
    pairs = sums + jnp.where(lane % 2 == 0, pltpu.roll(sums, C - 1, 1), pltpu.roll(sums, 1, 1))
    quads = pairs + jnp.where(lane % 4 < 2, pltpu.roll(pairs, C - 2, 1), pltpu.roll(pairs, 2, 1))
    mean = quads * (1.0 / (GROUP * POS))
    return [mean[t : t + 1] for t in range(count)]


def tile_sum(value):
    return jnp.sum(value, axis=0, keepdims=True)


def normalize(act, count):
    center = group_mean([tile_sum(act[t]) for t in range(count)])
    sums = []
    for t in range(count):
        away = act[t] - center[t]
        act[t] = away
        sums.append(tile_sum(away * away))
    scale = [lax.rsqrt(mean + 1e-06) for mean in group_mean(sums)]
    for t in range(count):
        act[t] = act[t] * scale[t]
    return scale


def gate_of(normed):
    return 1.0 / (1.0 + jnp.exp(-normed))


def norm_adjoint(act, back, scale, count):
    first, second = [], []
    for t in range(count):
        gate = gate_of(act[t])
        grad = back[t] * (gate * (1.0 + act[t] * (1.0 - gate)))
        back[t] = grad
        first.append(tile_sum(grad))
        second.append(tile_sum(grad * act[t]))
    first, second = group_mean(first), group_mean(second)
    return [
        (scale[t] * (back[t] - first[t] - act[t] * second[t])).astype(BF16) for t in range(count)
    ]


def first_frame():
    return lax.axis_index("seq") * F


def halo_kernel(frames, cot, tail, head, sems):
    copies = [
        pltpu.make_async_copy(frames.at[F - 4 :], tail, sems.at[0]),
        pltpu.make_async_copy(frames.at[:2], head.at[:2], sems.at[1]),
        pltpu.make_async_copy(cot.at[:4], head.at[2:], sems.at[2]),
    ]
    for copy in copies:
        copy.start()
    for copy in copies:
        copy.wait()


def local_kernel(
    clips,
    frames,
    cot,
    weight1,
    weight2,
    window,
    cot_window,
    weight1_copy,
    weight2_copy,
    conv_weight,
    back_weight,
    act,
    back,
    sems,
):
    copies = [
        pltpu.make_async_copy(weight1, weight1_copy, sems.at[0]),
        pltpu.make_async_copy(frames, window.at[:F], sems.at[1]),
        pltpu.make_async_copy(weight2, weight2_copy, sems.at[2]),
        pltpu.make_async_copy(cot, cot_window.at[:F], sems.at[3]),
    ]
    for copy in copies:
        copy.start()
    window[F] = jnp.zeros((POS, C), BF16)
    cot_window[F] = jnp.zeros((POS, C), BF16)
    first = first_frame()
    copies[0].wait()
    forward_weight(weight1_copy, conv_weight)
    copies[1].wait()
    for t in range(2, F):
        act[t] = conv_frame(window, past_slots(clips, first, t, 0, F), conv_weight)
    copies[2].wait()
    adjoint_weight(weight2_copy, back_weight)
    copies[3].wait()
    for t in range(F - 2):
        back[t] = conv_frame(cot_window, next_slots(clips, first, t, 0, F), back_weight)


def main_kernel(
    clips,
    frames,
    cot,
    tail,
    head,
    conv_weight,
    back_weight,
    act_in,
    back_in,
    hidden_ref,
    act_grad_ref,
    keep_ref,
    send_ref,
    window,
    cot_window,
    act,
    back,
    cot_shifted,
    cot_taps,
    frame_t,
    frame_taps,
    hidden_t,
    grad_shifted,
    grads,
):
    none = F + 2
    first = first_frame()
    past = [past_slots(clips, first, t, 2, none) for t in range(F)]
    following = [next_slots(clips, first, t, 0, none) for t in range(F)]
    for f in range(2):
        window[f] = tail[2 + f]
        cot_window[F + f] = head[2 + f]
    for f in range(F):
        window[2 + f] = frames[f]
        cot_window[f] = cot[f]
    window[none] = jnp.zeros((POS, C), BF16)
    cot_window[none] = jnp.zeros((POS, C), BF16)

    for t in range(F):
        act[t] = conv_frame(window, past[t], conv_weight) if t < 2 else act_in[t]
        back[t] = back_in[t] if t < F - 2 else conv_frame(cot_window, following[t], back_weight)
    scale = normalize(act, F)
    for t in range(F):
        hidden = (act[t] * gate_of(act[t])).astype(BF16)
        hidden_ref[t] = hidden
        for a, piece in enumerate(row_pieces(hidden)):
            hidden_t[a * C : (a + 1) * C, t * POS : (t + 1) * POS] = piece.T
    for t, rounded in enumerate(norm_adjoint(act, back, scale, F)):
        act_grad_ref[t] = rounded
        grad_shifted[t * POS : (t + 1) * POS] = column_pieces(rounded)

    for f in range(F + 2):
        cot_shifted[f] = column_pieces(cot_window[f])
    cot_shifted[none] = jnp.zeros((POS, 3 * C), BF16)
    for s in range(F):
        for k in range(3):
            cot_taps[s * POS : (s + 1) * POS, 3 * C * k : 3 * C * (k + 1)] = cot_shifted[
                following[s][2 - k]
            ]
    second_grad = jnp.dot(hidden_t[...], cot_taps[...], preferred_element_type=F32)
    for k in range(3):
        for a in range(3):
            for b in range(3):
                tap = (k * 3 + a) * 3 + b
                grads[1, tap * C : (tap + 1) * C] = second_grad[
                    a * C : (a + 1) * C, (k * 3 + b) * C : (k * 3 + b + 1) * C
                ]

    for f in range(F + 2):
        for a, piece in enumerate(row_pieces(window[f])):
            frame_t[f, a * C : (a + 1) * C, :] = piece.T
    frame_t[none] = jnp.zeros((3 * C, POS), BF16)
    for t in range(F):
        for k in range(3):
            frame_taps[3 * C * k : 3 * C * (k + 1), t * POS : (t + 1) * POS] = frame_t[past[t][k]]
    first_grad = jnp.dot(frame_taps[...], grad_shifted[...], preferred_element_type=F32)
    for outer in range(9):
        for b in range(3):
            tap = outer * 3 + b
            grads[0, tap * C : (tap + 1) * C] = first_grad[
                outer * C : (outer + 1) * C, b * C : (b + 1) * C
            ]

    own = lax.rem(lax.axis_index("dp"), 2) == 0
    for g in range(2):
        for m in range(16):
            low = grads[g, 2 * BLOCK * m : 2 * BLOCK * m + BLOCK]
            high = grads[g, 2 * BLOCK * m + BLOCK : 2 * BLOCK * (m + 1)]
            keep_ref[g, m, :BLOCK] = jnp.where(own, low, high)
            keep_ref[g, m, BLOCK:] = jnp.zeros((PADDED - BLOCK, C), F32)
            send_ref[g, m, :BLOCK] = jnp.where(own, high, low).astype(BF16)
            send_ref[g, m, BLOCK:] = jnp.zeros((PADDED - BLOCK, C), BF16)


def forward_kernel(
    clips, hidden_in, frames, tail, conv_weight, weight2, out_ref, window, act, hidden, weight
):
    first = first_frame()
    for f in range(4):
        window[f] = tail[f]
    window[4] = jnp.zeros((POS, C), BF16)
    for t in range(2):
        act[t] = conv_frame(window, past_slots(clips, first, t - 2, 4, 4), conv_weight)
    normalize(act, 2)
    for t in range(2):
        hidden[t] = (act[t] * gate_of(act[t])).astype(BF16)
    for f in range(F):
        hidden[2 + f] = hidden_in[f]
    hidden[F + 2] = jnp.zeros((POS, C), BF16)
    forward_weight(weight2, weight)
    for t in range(F):
        out = conv_frame(hidden, past_slots(clips, first, t, 2, F + 2), weight)
        out_ref[t] = (frames[t].astype(F32) + out).astype(BF16)


def backward_kernel(
    clips,
    act_grad_in,
    frames,
    cot,
    head,
    conv_weight,
    back_weight,
    weight1,
    out_ref,
    window,
    cot_window,
    act,
    back,
    act_grad,
    weight,
):
    first = first_frame()
    zero = jnp.zeros((POS, C), BF16)
    for f in range(2):
        window[f] = frames[F - 2 + f]
        window[2 + f] = head[f]
    for f in range(4):
        cot_window[f] = head[2 + f]
    window[4] = zero
    cot_window[4] = zero
    for t in range(2):
        act[t] = conv_frame(window, past_slots(clips, first, F + t, 2 - F, 4), conv_weight)
        back[t] = conv_frame(cot_window, next_slots(clips, first, F + t, -F, 4), back_weight)
    scale = normalize(act, 2)
    for t, rounded in enumerate(norm_adjoint(act, back, scale, 2)):
        act_grad[F + t] = rounded
    for f in range(F):
        act_grad[f] = act_grad_in[f]
    act_grad[F + 2] = zero
    adjoint_weight(weight1, weight)
    for t in range(F):
        out = conv_frame(act_grad, next_slots(clips, first, t, 0, F + 2), weight)
        out_ref[t] = (cot[t].astype(F32) + out).astype(BF16)


def x_kernel(keep_ref, part, kept_ref, *sent_refs):
    own = lax.rem(lax.div(lax.axis_index("dp"), 2), 4)
    for g in range(2):
        for y in range(4):
            for step in range(4):
                block = lax.rem(own + step, 4)
                total = keep_ref[g, y, block] + part[g, y, block].astype(F32)
                if step == 0:
                    kept_ref[g, y] = total
                else:
                    sent_refs[step - 1][g, y] = total.astype(BF16)


def y_kernel(keep_ref, *refs):
    received, (kept_ref, *sent_refs) = refs[:3], refs[3:]
    own = lax.div(lax.axis_index("dp"), 8)
    for g in range(2):
        for step in range(4):
            block = lax.rem(own + step, 4)
            total = keep_ref[g, block]
            for part in received:
                total = total + part[g, block].astype(F32)
            if step == 0:
                kept_ref[g] = total
            else:
                sent_refs[step - 1][g] = total.astype(BF16)


def sum_kernel(keep_ref, *refs):
    received, out_ref = refs[:-1], refs[-1]
    total = keep_ref[...].astype(F32)
    for part in received:
        total = total + part[...].astype(F32)
    out_ref[...] = total.astype(BF16)


def last_kernel(scale, own, near, next_near, far, first_ref, second_ref):
    for g, out_ref in enumerate((first_ref, second_ref)):
        total = (own[g].astype(F32) + far[g].astype(F32)) + (
            near[g].astype(F32) + next_near[g].astype(F32)
        )
        out_ref[...] = (total * scale)[:BLOCK]


VMEM = pl.BlockSpec(memory_space=pltpu.VMEM)
SMEM = pl.BlockSpec(memory_space=pltpu.SMEM)
HBM = pl.BlockSpec(memory_space=pltpu.HBM)


def call(kernel, operands, in_specs, outs, scratch=(), flops=0, moved=1 << 20, limit=4):
    return pl.pallas_call(
        kernel,
        out_shape=[jax.ShapeDtypeStruct(shape, dtype) for shape, dtype in outs],
        in_specs=in_specs,
        out_specs=[VMEM] * len(outs),
        scratch_shapes=[
            pltpu.VMEM(*one) if isinstance(one, tuple) else one for one in scratch
        ],
        compiler_params=pltpu.CompilerParams(vmem_limit_bytes=limit << 20),
        cost_estimate=pl.CostEstimate(flops=flops, bytes_accessed=moved, transcendentals=0),
    )(*operands)


CONV_FLOPS = 2 * F * POS * 27 * C * C
WIDE = ((9 * C, 3 * C), BF16)


def frame_shape(count, dtype=BF16):
    return ((count, POS, C), dtype)


def shifted(value, steps):
    count = lax.axis_size("seq")
    first, last = (max(0, -steps), min(count, count - steps))
    return lax.ppermute(value, "seq", [(source, source + steps) for source in range(first, last)])


def dp_permute(value, target):
    return lax.ppermute(value, "dp", [(source, target(source)) for source in range(32)])


def seq_permute(value, target):
    return lax.ppermute(value, "seq", [(source, target(source) % 8) for source in range(8)])


def per_device(frames, clip_ids, cotangent, conv1_weight, conv2_weight):
    own_frames = frames.reshape(F, POS, C)
    own_cot = cotangent.reshape(F, POS, C)
    own_frames, own_cot, conv1_weight, conv2_weight = (
        pltpu.with_memory_space_constraint(value, pltpu.HBM)
        for value in (own_frames, own_cot, conv1_weight, conv2_weight)
    )
    tail, head = call(
        halo_kernel,
        (own_frames, own_cot),
        [HBM, HBM],
        [frame_shape(4), frame_shape(6)],
        [pltpu.SemaphoreType.DMA((3,))],
    )
    head = shifted(head, -1)
    tail = shifted(tail, 1)
    local = call(
        local_kernel,
        (clip_ids, own_frames, own_cot, conv1_weight, conv2_weight),
        [SMEM, HBM, HBM, HBM, HBM],
        [
            frame_shape(F + 1),
            frame_shape(F + 1),
            ((27 * C, C), BF16),
            ((27 * C, C), BF16),
            WIDE,
            WIDE,
            frame_shape(F, F32),
            frame_shape(F, F32),
        ],
        [pltpu.SemaphoreType.DMA((4,))],
        flops=CONV_FLOPS * 3 // 2,
        limit=16,
    )
    tail, head, local = lax.optimization_barrier((tail, head, local))
    frame_copy, cot_copy, weight1, weight2, conv_weight, back_weight, act, back = local
    block = ((2, 16, PADDED, C), F32)
    hidden, act_grad, keep, send = call(
        main_kernel,
        (clip_ids, frame_copy, cot_copy, tail, head, conv_weight, back_weight, act, back),
        [SMEM] + [VMEM] * 8,
        [frame_shape(F), frame_shape(F), block, (block[0], BF16)],
        [
            frame_shape(F + 3),
            frame_shape(F + 3),
            frame_shape(F, F32),
            frame_shape(F, F32),
            ((F + 3, POS, 3 * C), BF16),
            ((F * POS, 9 * C), BF16),
            ((F + 3, 3 * C, POS), BF16),
            ((9 * C, F * POS), BF16),
            ((3 * C, F * POS), BF16),
            ((F * POS, 3 * C), BF16),
            ((2, 27 * C, C), F32),
        ],
        flops=CONV_FLOPS * 5 // 2,
        limit=40,
    )
    recv = dp_permute(send, lambda d: d ^ 1)
    keep, *sent = call(
        x_kernel,
        (keep.reshape(2, 4, 4, PADDED, C), recv.reshape(2, 4, 4, PADDED, C)),
        [VMEM] * 2,
        [((2, 4, PADDED, C), F32)] + [((2, 4, PADDED, C), BF16)] * 3,
    )
    sent, hidden, act_grad = lax.optimization_barrier((sent, hidden, act_grad))
    recv = [
        dp_permute(part, lambda d, s=s: (d // 8) * 8 + (d % 8 + 2 * s) % 8)
        for s, part in zip((1, 2, 3), sent)
    ]
    (block_out,) = call(
        forward_kernel,
        (clip_ids, hidden, frame_copy, tail, conv_weight, weight2),
        [SMEM] + [VMEM] * 5,
        [frame_shape(F)],
        [frame_shape(5), frame_shape(2, F32), frame_shape(F + 3), WIDE],
        flops=CONV_FLOPS * 5 // 4,
        limit=12,
    )
    (input_grad,) = call(
        backward_kernel,
        (clip_ids, act_grad, frame_copy, cot_copy, head, conv_weight, back_weight, weight1),
        [SMEM] + [VMEM] * 7,
        [frame_shape(F)],
        [
            frame_shape(5),
            frame_shape(5),
            frame_shape(2, F32),
            frame_shape(2, F32),
            frame_shape(F + 3),
            WIDE,
        ],
        flops=CONV_FLOPS * 3 // 2,
        limit=12,
    )
    recv, block_out, input_grad = lax.optimization_barrier((recv, block_out, input_grad))
    pair = (2, PADDED, C)
    keep, *sent = call(y_kernel, (keep, *recv), [VMEM] * 4, [(pair, F32)] + [(pair, BF16)] * 3)
    recv = [dp_permute(part, lambda d, s=s: (d + 8 * s) % 32) for s, part in zip((1, 2, 3), sent)]
    (total,) = call(sum_kernel, (keep, *recv), [VMEM] * 4, [(pair, BF16)])
    other = seq_permute(total, lambda z: z ^ 1)
    (total,) = call(sum_kernel, (total, other), [VMEM] * 2, [(pair, BF16)])
    others = [
        seq_permute(total, lambda z, s=s: z + s if z % 2 else z - s) for s in (1, 2, 3)
    ]
    rows = lax.axis_size("dp") * lax.axis_size("seq") * F * POS
    first_grad, second_grad = call(
        lambda *refs: last_kernel(rows**-0.5, *refs),
        (total, *others),
        [VMEM] * 4,
        [((BLOCK, C), F32)] * 2,
    )
    return (
        block_out.reshape(frames.shape),
        input_grad.reshape(frames.shape),
        first_grad,
        second_grad,
    )


def solution(mesh):
    return jax.shard_map(
        per_device,
        mesh=mesh,
        in_specs=(
            P("dp", "seq", None, None, None),
            P("dp", None),
            P("dp", "seq", None, None, None),
            P(),
            P(),
        ),
        out_specs=(
            P("dp", "seq", None, None, None),
            P("dp", "seq", None, None, None),
            P("dp", None),
            P("dp", None),
        ),
        check_vma=False,
    )
```

time: 88.1 us -> 71.2 us (0.81)
  waiting for transfers between devices: 25.1 us -> 10.9 us
  local copies, waits for them, and re-layouts: 7.8 us -> 0.65 us
  Pallas kernels: 21.6 us -> 28.7 us
  starting transfers between devices: 32.3 us -> 29.6 us
    ppermute x4, waiting for transfers between devices: 15.1 us -> 5.57 us  [seq_permute(): lax.ppermute(value, 'seq', [(source, target(source) % 8) for source in ra...]
    pallas_call x5 -> x10, Pallas kernels: 21.6 us -> 28.7 us  [call(): pl.pallas_call(kernel, out_shape=[jax.ShapeDtypeStruct(shape, dtype) for...]
    unnamed x16 -> x4, local copies, waits for them, and re-layouts: 7.16 us -> 0.65 us
    ppermute x4 -> x2, waiting for transfers between devices: 5.74 us -> 0.01 us  [shifted(): lax.ppermute(value, 'seq', [(source, source + steps) for source in range(...]
    ppermute x4 -> x2, starting transfers between devices: 10.4 us -> 5.85 us  [shifted(): lax.ppermute(value, 'seq', [(source, source + steps) for source in range(...]
    ppermute x4, starting transfers between devices: 11 us -> 12.7 us  [seq_permute(): lax.ppermute(value, 'seq', [(source, target(source) % 8) for source in ra...]
    ppermute x7, waiting for transfers between devices: 4.29 us -> 5.28 us  [dp_permute(): lax.ppermute(value, 'dp', [(source, target(source)) for source in range(3...]
  transfers between devices with their start and end apart: 15 -> 13, of which waited for: 10 -> 7; matrix products, arithmetic and copies ran while one was open for 0% -> 0% of each run, Pallas kernels for 10% -> 25%
where the time goes in v2:
time: 71.2 us; the launch traced here: 70.5 us
  starting transfers between devices  29.6 us (42%)
  Pallas kernels  28.7 us (40%)
  waiting for transfers between devices  10.9 us (15%)
  between operations  0.73 us (1%)
    pallas_call x10, Pallas kernels, call(): pl.pallas_call(kernel, out_shape=[jax.ShapeDtypeStruct(shape, dtype) for...  28.7 us
    ppermute x4, starting transfers between devices, seq_permute(): lax.ppermute(value, 'seq', [(source, target(source) % 8) for source in ra...  12.7 us
    ppermute x7, starting transfers between devices, dp_permute(): lax.ppermute(value, 'dp', [(source, target(source)) for source in range(3...  11 us
    ppermute x2, starting transfers between devices, shifted(): lax.ppermute(value, 'seq', [(source, source + steps) for source in range(...  5.85 us
    ppermute x4, waiting for transfers between devices, seq_permute(): lax.ppermute(value, 'seq', [(source, target(source) % 8) for source in ra...  5.57 us
    ppermute x7, waiting for transfers between devices, dp_permute(): lax.ppermute(value, 'dp', [(source, target(source)) for source in range(3...  5.28 us
  transfers between devices with their start and end apart: 13, of which 7 were waited for; matrix products, arithmetic and copies ran while one was open for 0% of the time, Pallas kernels for 25%

profile of v2, /device:TPU:2, one launch (start us, length us, event | category | flops | bytes accessed | tf_op | source)
XLA Modules:
  0.0 70.5 jit_solution(2185485429769577432)
XLA Ops:
  0.6 1.1 %shard_map.84 = (bf16[4,256,128]{2,1,0:T(8,128)(2,1)S(1)}, bf16[6,256,128]{2,1,0:T(8,128)(2,1)S(1)}) custom-call(bf16[8,256,128]{2,1,0:T(8,128)(2,1)} %bitcast.8, bf16[8,256,128]{2,1,0:T(8,128)(2,1)} %bitcast.10), custom_call_target="tpu_custom_call" | custom-call | bytes 1048576 | tf_op jit(solution)/shard_map/pallas_call | solution.py:400
  1.8 1.3 %collective-permute-start.1 = (bf16[6,256,128]{2,1,0:T(8,128)(2,1)S(1)}, bf16[6,256,128]{2,1,0:T(8,128)(2,1)S(1)}, u32[]{:S(2)}, u32[]{:S(2)}) collective-permute-start(bf16[6,256,128]{2,1,0:T(8,128)(2,1)S(1)} %get-tuple-element.49), channel_id=1, source_target_pairs={{32,0},{64,32},{96,64},{128,96},{160,128},{192,160},{224,192},{33,... | collective-permute-start | bytes 1179656 | tf_op jit(solution)/shard_map/ppermute | solution.py:424
  3.1 4.6 %collective-permute-start = (bf16[4,256,128]{2,1,0:T(8,128)(2,1)S(1)}, bf16[4,256,128]{2,1,0:T(8,128)(2,1)S(1)}, u32[]{:S(2)}, u32[]{:S(2)}) collective-permute-start(bf16[4,256,128]{2,1,0:T(8,128)(2,1)S(1)} %get-tuple-element.48), channel_id=1, source_target_pairs={{0,32},{32,64},{64,96},{96,128},{128,160},{160,192},{192,224},{1,3... | collective-permute-start | bytes 786440 | tf_op jit(solution)/shard_map/ppermute | solution.py:424
  7.6 0.0 copy-start
  7.6 0.6 copy-done
  8.3 0.0 copy-start.1
  8.3 6.4 %shard_map.85 = (bf16[9,256,128]{2,1,0:T(8,128)(2,1)S(1)}, bf16[9,256,128]{2,1,0:T(8,128)(2,1)S(1)}, bf16[3456,128]{1,0:T(8,128)(2,1)S(1)}, bf16[3456,128]{1,0:T...) custom-call(s32[1,64]{1,0:T(1,128)S(1)} %copy-done, ...), custom_call_target="tpu_custom_call" | custom-call | flops 2717908992 | bytes 1048576 | tf_op jit(solution)/shard_map/pallas_call | solution.py:400
  14.7 0.0 collective-permute-done.tail
  14.7 0.0 collective-permute-done.1.head
  14.7 0.0 copy-done.1
  14.7 9.1 %shard_map.86 = (bf16[8,256,128]{2,1,0:T(8,128)(2,1)S(1)}, bf16[8,256,128]{2,1,0:T(8,128)(2,1)S(1)}, f32[2,16,112,128]{3,2,1,0:T(8,128)S(1)}, bf16[2,16,112,128]{3,2,1,0:T(8,128)(2,1)S(1)}) custom-call(s32[1,64]{1,0:T(1,128)S(1)} %copy-done.1, bf16[9,256,128]{2,1,0:T(8,128)(2,1)S(1)} %get-tuple-element.58.frames, ...), custom_call_target="tpu_custom_call" | custom-call | flops 4529848320 | bytes 1048576 | tf_op jit(solution)/shard_map/pallas_call | solution.py:400
  23.8 0.3 collective-permute-start.2
  24.1 2.5 %collective-permute-done.2 = bf16[2,16,112,128]{3,2,1,0:T(8,128)(2,1)S(1)} collective-permute-done((bf16[2,16,112,128]{3,2,1,0:T(8,128)(2,1)S(1)}, bf16[2,16,112,128]{3,2,1,0:T(8,128)(2,1)S(1)}, u32[]{:S(2)}, u32[]{:S(2)}) %collective-permute-start.2) | collective-permute-done | bytes 917536 | tf_op jit(solution)/shard_map/ppermute | solution.py:428
  26.6 0.2 shard_map.87
  26.8 1.6 %collective-permute-start.3 = (bf16[2,4,112,128]{3,2,1,0:T(8,128)(2,1)S(1)}, bf16[2,4,112,128]{3,2,1,0:T(8,128)(2,1)S(1)}, u32[]{:S(2)}, u32[]{:S(2)}) collective-permute-start(bf16[2,4,112,128]{3,2,1,0:T(8,128)(2,1)S(1)} %get-tuple-element.73), channel_id=1, source_target_pairs={{0,2},{1,3},{2,4},{3,5},{4,6},{5,7},{6,0},{7,1},{8,10},{9,11},{10,... | collective-permute-start | bytes 688136 | tf_op jit(solution)/shard_map/ppermute | solution.py:428
  28.4 2.8 %collective-permute-start.4 = (bf16[2,4,112,128]{3,2,1,0:T(8,128)(2,1)S(1)}, bf16[2,4,112,128]{3,2,1,0:T(8,128)(2,1)S(1)}, u32[]{:S(2)}, u32[]{:S(2)}) collective-permute-start(bf16[2,4,112,128]{3,2,1,0:T(8,128)(2,1)S(1)} %get-tuple-element.74), channel_id=1, source_target_pairs={{0,4},{1,5},{2,6},{3,7},{4,0},{5,1},{6,2},{7,3},{8,12},{9,13},{10,... | collective-permute-start | bytes 688136 | tf_op jit(solution)/shard_map/ppermute | solution.py:428
  31.2 0.4 collective-permute-start.5
  31.6 5.7 %shard_map.89 = bf16[8,256,128]{2,1,0:T(8,128)(2,1)} custom-call(s32[1,64]{1,0:T(1,128)S(1)} %copy-done.1, bf16[8,256,128]{2,1,0:T(8,128)(2,1)S(1)} %get-tuple-element.78.act_grad_in, bf16[9,256,128]{2,1,0:T(8,128)(2,1)S(1)} %get-tuple-element.58.frames, bf16[9,256,128]{2,1,0:T(8,128)(2,1)S(1)} %get-tuple-element.59.cot, ...), custom_call_target="tpu_custom_call" | custom-call | flops 2717908992 | bytes 1048576 | tf_op jit(solution)/shard_map/pallas_call | solution.py:400
  37.3 5.4 %shard_map.88 = bf16[8,256,128]{2,1,0:T(8,128)(2,1)} custom-call(s32[1,64]{1,0:T(1,128)S(1)} %copy-done.1, bf16[8,256,128]{2,1,0:T(8,128)(2,1)S(1)} %get-tuple-element.76.hidden_in, bf16[9,256,128]{2,1,0:T(8,128)(2,1)S(1)} %get-tuple-element.58.frames, bf16[4,256,128]{2,1,0:T(8,128)(2,1)S(1)} %collective-permute-done.tail, ...), custom_call_target="tpu_custom_call" | custom-call | flops 2264924160 | bytes 1048576 | tf_op jit(solution)/shard_map/pallas_call | solution.py:400
  42.7 0.0 collective-permute-done.3.refs_0_
  42.7 0.0 collective-permute-done.4.refs_1_
  42.7 0.0 collective-permute-done.5.refs_2_
  42.7 0.1 shard_map.90
  42.9 1.6 %collective-permute-start.6 = (bf16[2,112,128]{2,1,0:T(8,128)(2,1)S(1)}, bf16[2,112,128]{2,1,0:T(8,128)(2,1)S(1)}, u32[]{:S(2)}, u32[]{:S(2)}) collective-permute-start(bf16[2,112,128]{2,1,0:T(8,128)(2,1)S(1)} %get-tuple-element.87), channel_id=1, source_target_pairs={{0,8},{1,9},{2,10},{3,11},{4,12},{5,13},{6,14},{7,15},{8,16},{9,17... | collective-permute-start | bytes 172040 | tf_op jit(solution)/shard_map/ppermute | solution.py:428
  44.5 2.9 %collective-permute-start.7 = (bf16[2,112,128]{2,1,0:T(8,128)(2,1)S(1)}, bf16[2,112,128]{2,1,0:T(8,128)(2,1)S(1)}, u32[]{:S(2)}, u32[]{:S(2)}) collective-permute-start(bf16[2,112,128]{2,1,0:T(8,128)(2,1)S(1)} %get-tuple-element.88), channel_id=1, source_target_pairs={{0,16},{1,17},{2,18},{3,19},{4,20},{5,21},{6,22},{7,23},{8,24},{9,... | collective-permute-start | bytes 172040 | tf_op jit(solution)/shard_map/ppermute | solution.py:428
  47.4 1.4 %collective-permute-start.8 = (bf16[2,112,128]{2,1,0:T(8,128)(2,1)S(1)}, bf16[2,112,128]{2,1,0:T(8,128)(2,1)S(1)}, u32[]{:S(2)}, u32[]{:S(2)}) collective-permute-start(bf16[2,112,128]{2,1,0:T(8,128)(2,1)S(1)} %get-tuple-element.89), channel_id=1, source_target_pairs={{0,24},{1,25},{2,26},{3,27},{4,28},{5,29},{6,30},{7,31},{8,0},{9,1... | collective-permute-start | bytes 172040 | tf_op jit(solution)/shard_map/ppermute | solution.py:428
  48.8 0.2 collective-permute-done.6.refs_0_
  48.9 1.2 %collective-permute-done.7.refs_1_ = bf16[2,112,128]{2,1,0:T(8,128)(2,1)S(1)} collective-permute-done((bf16[2,112,128]{2,1,0:T(8,128)(2,1)S(1)}, bf16[2,112,128]{2,1,0:T(8,128)(2,1)S(1)}, u32[]{:S(2)}, u32[]{:S(2)}) %collective-permute-start.7) | collective-permute-done | bytes 57376 | tf_op jit(solution)/shard_map/ppermute | solution.py:428
  50.2 1.4 %collective-permute-done.8.refs_2_ = bf16[2,112,128]{2,1,0:T(8,128)(2,1)S(1)} collective-permute-done((bf16[2,112,128]{2,1,0:T(8,128)(2,1)S(1)}, bf16[2,112,128]{2,1,0:T(8,128)(2,1)S(1)}, u32[]{:S(2)}, u32[]{:S(2)}) %collective-permute-start.8) | collective-permute-done | bytes 57376 | tf_op jit(solution)/shard_map/ppermute | solution.py:428
  51.6 2.0 %collective-permute-start.9 = (bf16[2,112,128]{2,1,0:T(8,128)(2,1)S(1)}, bf16[2,112,128]{2,1,0:T(8,128)(2,1)S(1)}, u32[]{:S(2)}, u32[]{:S(2)}) collective-permute-start(bf16[2,112,128]{2,1,0:T(8,128)(2,1)S(1)} %shard_map.91.keep_ref), channel_id=1, source_target_pairs={{0,32},{32,0},{64,96},{96,64},{128,160},{160,128},{192,224},{224,1... | collective-permute-start | bytes 172040 | tf_op jit(solution)/shard_map/ppermute | solution.py:432
  53.6 2.2 %collective-permute-done.9.refs_0_ = bf16[2,112,128]{2,1,0:T(8,128)(2,1)S(1)} collective-permute-done((bf16[2,112,128]{2,1,0:T(8,128)(2,1)S(1)}, bf16[2,112,128]{2,1,0:T(8,128)(2,1)S(1)}, u32[]{:S(2)}, u32[]{:S(2)}) %collective-permute-start.9) | collective-permute-done | bytes 57376 | tf_op jit(solution)/shard_map/ppermute | solution.py:432
  55.9 6.8 %collective-permute-start.12 = (bf16[2,112,128]{2,1,0:T(8,128)(2,1)S(1)}, bf16[2,112,128]{2,1,0:T(8,128)(2,1)S(1)}, u32[]{:S(2)}, u32[]{:S(2)}) collective-permute-start(bf16[2,112,128]{2,1,0:T(8,128)(2,1)S(1)} %shard_map.92.refs_0_), channel_id=1, source_target_pairs={{0,160},{32,128},{64,224},{96,192},{128,32},{160,0},{192,96},{224,... | collective-permute-start | bytes 172040 | tf_op jit(solution)/shard_map/ppermute | solution.py:432
  62.7 1.8 %collective-permute-start.11 = (bf16[2,112,128]{2,1,0:T(8,128)(2,1)S(1)}, bf16[2,112,128]{2,1,0:T(8,128)(2,1)S(1)}, u32[]{:S(2)}, u32[]{:S(2)}) collective-permute-start(bf16[2,112,128]{2,1,0:T(8,128)(2,1)S(1)} %shard_map.92.refs_0_), channel_id=1, source_target_pairs={{0,192},{32,96},{64,0},{96,160},{128,64},{160,224},{192,128},{224,... | collective-permute-start | bytes 172040 | tf_op jit(solution)/shard_map/ppermute | solution.py:432
  64.5 2.1 %collective-permute-start.10 = (bf16[2,112,128]{2,1,0:T(8,128)(2,1)S(1)}, bf16[2,112,128]{2,1,0:T(8,128)(2,1)S(1)}, u32[]{:S(2)}, u32[]{:S(2)}) collective-permute-start(bf16[2,112,128]{2,1,0:T(8,128)(2,1)S(1)} %shard_map.92.refs_0_), channel_id=1, source_target_pairs={{0,224},{32,64},{64,32},{96,128},{128,96},{160,192},{192,160},{224... | collective-permute-start | bytes 172040 | tf_op jit(solution)/shard_map/ppermute | solution.py:432
  66.5 0.0 collective-permute-done.12.refs_3_
  66.5 1.3 %collective-permute-done.11.refs_2_ = bf16[2,112,128]{2,1,0:T(8,128)(2,1)S(1)} collective-permute-done((bf16[2,112,128]{2,1,0:T(8,128)(2,1)S(1)}, bf16[2,112,128]{2,1,0:T(8,128)(2,1)S(1)}, u32[]{:S(2)}, u32[]{:S(2)}) %collective-permute-start.11) | collective-permute-done | bytes 57376 | tf_op jit(solution)/shard_map/ppermute | solution.py:432
  67.8 2.1 %collective-permute-done.10.refs_1_ = bf16[2,112,128]{2,1,0:T(8,128)(2,1)S(1)} collective-permute-done((bf16[2,112,128]{2,1,0:T(8,128)(2,1)S(1)}, bf16[2,112,128]{2,1,0:T(8,128)(2,1)S(1)}, u32[]{:S(2)}, u32[]{:S(2)}) %collective-permute-start.10) | collective-permute-done | bytes 57376 | tf_op jit(solution)/shard_map/ppermute | solution.py:432
  69.9 0.7 shard_map.93
  (2 shorter events, 0.0 us)
Async XLA Ops:
  1.8 13.0 %collective-permute-start.1 = (bf16[6,256,128]{2,1,0:T(8,128)(2,1)S(1)}, bf16[6,256,128]{2,1,0:T(8,128)(2,1)S(1)}, u32[]{:S(2)}, u32[]{:S(2)}) collective-permute-start(bf16[6,256,128]{2,1,0:T(8,128)(2,1)S(1)} %get-tuple-element.49), channel_id=1, source_target_pairs={{32,0},{64,32},{96,64},{128,96},{160,128},{192,160},{224,192},{33,... | collective-permute-start | bytes 1179656 | tf_op jit(solution)/shard_map/ppermute | solution.py:424
  3.1 11.7 %collective-permute-start = (bf16[4,256,128]{2,1,0:T(8,128)(2,1)S(1)}, bf16[4,256,128]{2,1,0:T(8,128)(2,1)S(1)}, u32[]{:S(2)}, u32[]{:S(2)}) collective-permute-start(bf16[4,256,128]{2,1,0:T(8,128)(2,1)S(1)} %get-tuple-element.48), channel_id=1, source_target_pairs={{0,32},{32,64},{64,96},{96,128},{128,160},{160,192},{192,224},{1,3... | collective-permute-start | bytes 786440 | tf_op jit(solution)/shard_map/ppermute | solution.py:424
  7.6 0.7 copy-start
  8.3 6.5 %copy-start.1 = (s32[1,64]{1,0:T(1,128)S(1)}, s32[1,64]{1,0:T(1,128)}, u32[]{:S(2)}) copy-start(s32[1,64]{1,0:T(1,128)} %clips.7) | copy-start | bytes 772
  23.8 2.7 %collective-permute-start.2 = (bf16[2,16,112,128]{3,2,1,0:T(8,128)(2,1)S(1)}, bf16[2,16,112,128]{3,2,1,0:T(8,128)(2,1)S(1)}, u32[]{:S(2)}, u32[]{:S(2)}) collective-permute-start(bf16[2,16,112,128]{3,2,1,0:T(8,128)(2,1)S(1)} %get-tuple-element.67), channel_id=1, source_target_pairs={{0,1},{1,0},{2,3},{3,2},{4,5},{5,4},{6,7},{7,6},{8,9},{9,8},{10,11... | collective-permute-start | bytes 2752520 | tf_op jit(solution)/shard_map/ppermute | solution.py:428
  26.8 16.0 %collective-permute-start.3 = (bf16[2,4,112,128]{3,2,1,0:T(8,128)(2,1)S(1)}, bf16[2,4,112,128]{3,2,1,0:T(8,128)(2,1)S(1)}, u32[]{:S(2)}, u32[]{:S(2)}) collective-permute-start(bf16[2,4,112,128]{3,2,1,0:T(8,128)(2,1)S(1)} %get-tuple-element.73), channel_id=1, source_target_pairs={{0,2},{1,3},{2,4},{3,5},{4,6},{5,7},{6,0},{7,1},{8,10},{9,11},{10,... | collective-permute-start | bytes 688136 | tf_op jit(solution)/shard_map/ppermute | solution.py:428
  28.4 14.3 %collective-permute-start.4 = (bf16[2,4,112,128]{3,2,1,0:T(8,128)(2,1)S(1)}, bf16[2,4,112,128]{3,2,1,0:T(8,128)(2,1)S(1)}, u32[]{:S(2)}, u32[]{:S(2)}) collective-permute-start(bf16[2,4,112,128]{3,2,1,0:T(8,128)(2,1)S(1)} %get-tuple-element.74), channel_id=1, source_target_pairs={{0,4},{1,5},{2,6},{3,7},{4,0},{5,1},{6,2},{7,3},{8,12},{9,13},{10,... | collective-permute-start | bytes 688136 | tf_op jit(solution)/shard_map/ppermute | solution.py:428
  31.2 11.5 %collective-permute-start.5 = (bf16[2,4,112,128]{3,2,1,0:T(8,128)(2,1)S(1)}, bf16[2,4,112,128]{3,2,1,0:T(8,128)(2,1)S(1)}, u32[]{:S(2)}, u32[]{:S(2)}) collective-permute-start(bf16[2,4,112,128]{3,2,1,0:T(8,128)(2,1)S(1)} %get-tuple-element.75), channel_id=1, source_target_pairs={{0,6},{1,7},{2,0},{3,1},{4,2},{5,3},{6,4},{7,5},{8,14},{9,15},{10,... | collective-permute-start | bytes 688136 | tf_op jit(solution)/shard_map/ppermute | solution.py:428
  42.9 6.1 %collective-permute-start.6 = (bf16[2,112,128]{2,1,0:T(8,128)(2,1)S(1)}, bf16[2,112,128]{2,1,0:T(8,128)(2,1)S(1)}, u32[]{:S(2)}, u32[]{:S(2)}) collective-permute-start(bf16[2,112,128]{2,1,0:T(8,128)(2,1)S(1)} %get-tuple-element.87), channel_id=1, source_target_pairs={{0,8},{1,9},{2,10},{3,11},{4,12},{5,13},{6,14},{7,15},{8,16},{9,17... | collective-permute-start | bytes 172040 | tf_op jit(solution)/shard_map/ppermute | solution.py:428
  44.5 5.7 %collective-permute-start.7 = (bf16[2,112,128]{2,1,0:T(8,128)(2,1)S(1)}, bf16[2,112,128]{2,1,0:T(8,128)(2,1)S(1)}, u32[]{:S(2)}, u32[]{:S(2)}) collective-permute-start(bf16[2,112,128]{2,1,0:T(8,128)(2,1)S(1)} %get-tuple-element.88), channel_id=1, source_target_pairs={{0,16},{1,17},{2,18},{3,19},{4,20},{5,21},{6,22},{7,23},{8,24},{9,... | collective-permute-start | bytes 172040 | tf_op jit(solution)/shard_map/ppermute | solution.py:428
  47.4 4.2 %collective-permute-start.8 = (bf16[2,112,128]{2,1,0:T(8,128)(2,1)S(1)}, bf16[2,112,128]{2,1,0:T(8,128)(2,1)S(1)}, u32[]{:S(2)}, u32[]{:S(2)}) collective-permute-start(bf16[2,112,128]{2,1,0:T(8,128)(2,1)S(1)} %get-tuple-element.89), channel_id=1, source_target_pairs={{0,24},{1,25},{2,26},{3,27},{4,28},{5,29},{6,30},{7,31},{8,0},{9,1... | collective-permute-start | bytes 172040 | tf_op jit(solution)/shard_map/ppermute | solution.py:428
  51.6 4.3 %collective-permute-start.9 = (bf16[2,112,128]{2,1,0:T(8,128)(2,1)S(1)}, bf16[2,112,128]{2,1,0:T(8,128)(2,1)S(1)}, u32[]{:S(2)}, u32[]{:S(2)}) collective-permute-start(bf16[2,112,128]{2,1,0:T(8,128)(2,1)S(1)} %shard_map.91.keep_ref), channel_id=1, source_target_pairs={{0,32},{32,0},{64,96},{96,64},{128,160},{160,128},{192,224},{224,1... | collective-permute-start | bytes 172040 | tf_op jit(solution)/shard_map/ppermute | solution.py:432
  55.9 10.6 %collective-permute-start.12 = (bf16[2,112,128]{2,1,0:T(8,128)(2,1)S(1)}, bf16[2,112,128]{2,1,0:T(8,128)(2,1)S(1)}, u32[]{:S(2)}, u32[]{:S(2)}) collective-permute-start(bf16[2,112,128]{2,1,0:T(8,128)(2,1)S(1)} %shard_map.92.refs_0_), channel_id=1, source_target_pairs={{0,160},{32,128},{64,224},{96,192},{128,32},{160,0},{192,96},{224,... | collective-permute-start | bytes 172040 | tf_op jit(solution)/shard_map/ppermute | solution.py:432
  62.7 5.1 %collective-permute-start.11 = (bf16[2,112,128]{2,1,0:T(8,128)(2,1)S(1)}, bf16[2,112,128]{2,1,0:T(8,128)(2,1)S(1)}, u32[]{:S(2)}, u32[]{:S(2)}) collective-permute-start(bf16[2,112,128]{2,1,0:T(8,128)(2,1)S(1)} %shard_map.92.refs_0_), channel_id=1, source_target_pairs={{0,192},{32,96},{64,0},{96,160},{128,64},{160,224},{192,128},{224,... | collective-permute-start | bytes 172040 | tf_op jit(solution)/shard_map/ppermute | solution.py:432
  64.5 5.4 %collective-permute-start.10 = (bf16[2,112,128]{2,1,0:T(8,128)(2,1)S(1)}, bf16[2,112,128]{2,1,0:T(8,128)(2,1)S(1)}, u32[]{:S(2)}, u32[]{:S(2)}) collective-permute-start(bf16[2,112,128]{2,1,0:T(8,128)(2,1)S(1)} %shard_map.92.refs_0_), channel_id=1, source_target_pairs={{0,224},{32,64},{64,32},{96,128},{128,96},{160,192},{192,160},{224... | collective-permute-start | bytes 172040 | tf_op jit(solution)/shard_map/ppermute | solution.py:432

commit v3 on v2

--- a/solution.py
+++ b/solution.py
@@ -139,8 +139,9 @@
     return lax.axis_index("seq") * F
 
 
-def halo_kernel(frames, cot, tail, head, sems):
+def halo_kernel(clips, frames, cot, clips_copy, tail, head, sems):
     copies = [
+        pltpu.make_async_copy(clips, clips_copy, sems.at[3]),
         pltpu.make_async_copy(frames.at[F - 4 :], tail, sems.at[0]),
         pltpu.make_async_copy(frames.at[:2], head.at[:2], sems.at[1]),
         pltpu.make_async_copy(cot.at[:4], head.at[2:], sems.at[2]),
@@ -306,22 +307,8 @@
         out_ref[t] = (frames[t].astype(F32) + out).astype(BF16)
 
 
-def backward_kernel(
-    clips,
-    act_grad_in,
-    frames,
-    cot,
-    head,
-    conv_weight,
-    back_weight,
-    weight1,
-    out_ref,
-    window,
-    cot_window,
-    act,
-    back,
-    act_grad,
-    weight,
+def next_grad_kernel(
+    clips, frames, head, conv_weight, back_weight, out_ref, window, cot_window, act, back
 ):
     first = first_frame()
     zero = jnp.zeros((POS, C), BF16)
@@ -337,10 +324,16 @@
         back[t] = conv_frame(cot_window, next_slots(clips, first, F + t, -F, 4), back_weight)
     scale = normalize(act, 2)
     for t, rounded in enumerate(norm_adjoint(act, back, scale, 2)):
-        act_grad[F + t] = rounded
+        out_ref[t] = rounded
+
+
+def backward_kernel(clips, act_grad_in, next_in, cot, weight1, out_ref, act_grad, weight):
+    first = first_frame()
     for f in range(F):
         act_grad[f] = act_grad_in[f]
-    act_grad[F + 2] = zero
+    for f in range(2):
+        act_grad[F + f] = next_in[f]
+    act_grad[F + 2] = jnp.zeros((POS, C), BF16)
     adjoint_weight(weight1, weight)
     for t in range(F):
         out = conv_frame(act_grad, next_slots(clips, first, t, 0, F + 2), weight)
@@ -419,9 +412,7 @@
 
 
 def shifted(value, steps):
-    count = lax.axis_size("seq")
-    first, last = (max(0, -steps), min(count, count - steps))
-    return lax.ppermute(value, "seq", [(source, source + steps) for source in range(first, last)])
+    return seq_permute(value, lambda z: z + steps)
 
 
 def dp_permute(value, target):
@@ -435,16 +426,16 @@
 def per_device(frames, clip_ids, cotangent, conv1_weight, conv2_weight):
     own_frames = frames.reshape(F, POS, C)
     own_cot = cotangent.reshape(F, POS, C)
-    own_frames, own_cot, conv1_weight, conv2_weight = (
+    clip_ids, own_frames, own_cot, conv1_weight, conv2_weight = (
         pltpu.with_memory_space_constraint(value, pltpu.HBM)
-        for value in (own_frames, own_cot, conv1_weight, conv2_weight)
-    )
-    tail, head = call(
+        for value in (clip_ids, own_frames, own_cot, conv1_weight, conv2_weight)
+    )
+    clip_ids, tail, head = call(
         halo_kernel,
-        (own_frames, own_cot),
-        [HBM, HBM],
-        [frame_shape(4), frame_shape(6)],
-        [pltpu.SemaphoreType.DMA((3,))],
+        (clip_ids, own_frames, own_cot),
+        [HBM, HBM, HBM],
+        [(clip_ids.shape, jnp.int32), frame_shape(4), frame_shape(6)],
+        [pltpu.SemaphoreType.DMA((4,))],
     )
     head = shifted(head, -1)
     tail = shifted(tail, 1)
@@ -491,13 +482,24 @@
         limit=40,
     )
     recv = dp_permute(send, lambda d: d ^ 1)
+    head, keep = lax.optimization_barrier((head, keep))
+    (act_grad_next,) = call(
+        next_grad_kernel,
+        (clip_ids, frame_copy, head, conv_weight, back_weight),
+        [SMEM] + [VMEM] * 4,
+        [frame_shape(2)],
+        [frame_shape(5), frame_shape(5), frame_shape(2, F32), frame_shape(2, F32)],
+        flops=CONV_FLOPS // 2,
+        limit=8,
+    )
+    recv, act_grad_next = lax.optimization_barrier((recv, act_grad_next))
     keep, *sent = call(
         x_kernel,
         (keep.reshape(2, 4, 4, PADDED, C), recv.reshape(2, 4, 4, PADDED, C)),
         [VMEM] * 2,
         [((2, 4, PADDED, C), F32)] + [((2, 4, PADDED, C), BF16)] * 3,
     )
-    sent, hidden, act_grad = lax.optimization_barrier((sent, hidden, act_grad))
+    sent, hidden = lax.optimization_barrier((sent, hidden))
     recv = [
         dp_permute(part, lambda d, s=s: (d // 8) * 8 + (d % 8 + 2 * s) % 8)
         for s, part in zip((1, 2, 3), sent)
@@ -511,26 +513,21 @@
         flops=CONV_FLOPS * 5 // 4,
         limit=12,
     )
+    recv, block_out = lax.optimization_barrier((recv, block_out))
+    pair = (2, PADDED, C)
+    keep, *sent = call(y_kernel, (keep, *recv), [VMEM] * 4, [(pair, F32)] + [(pair, BF16)] * 3)
+    sent, act_grad = lax.optimization_barrier((sent, act_grad))
+    recv = [dp_permute(part, lambda d, s=s: (d + 8 * s) % 32) for s, part in zip((1, 2, 3), sent)]
     (input_grad,) = call(
         backward_kernel,
-        (clip_ids, act_grad, frame_copy, cot_copy, head, conv_weight, back_weight, weight1),
-        [SMEM] + [VMEM] * 7,
+        (clip_ids, act_grad, act_grad_next, cot_copy, weight1),
+        [SMEM] + [VMEM] * 4,
         [frame_shape(F)],
-        [
-            frame_shape(5),
-            frame_shape(5),
-            frame_shape(2, F32),
-            frame_shape(2, F32),
-            frame_shape(F + 3),
-            WIDE,
-        ],
-        flops=CONV_FLOPS * 3 // 2,
-        limit=12,
-    )
-    recv, block_out, input_grad = lax.optimization_barrier((recv, block_out, input_grad))
-    pair = (2, PADDED, C)
-    keep, *sent = call(y_kernel, (keep, *recv), [VMEM] * 4, [(pair, F32)] + [(pair, BF16)] * 3)
-    recv = [dp_permute(part, lambda d, s=s: (d + 8 * s) % 32) for s, part in zip((1, 2, 3), sent)]
+        [frame_shape(F + 3), WIDE],
+        flops=CONV_FLOPS,
+        limit=8,
+    )
+    recv, input_grad = lax.optimization_barrier((recv, input_grad))
     (total,) = call(sum_kernel, (keep, *recv), [VMEM] * 4, [(pair, BF16)])
     other = seq_permute(total, lambda z: z ^ 1)
     (total,) = call(sum_kernel, (total, other), [VMEM] * 2, [(pair, BF16)])

time: 71.2 us -> 69.4 us (0.975)
  starting transfers between devices: 29.6 us -> 23.6 us
  waiting for transfers between devices: 10.9 us -> 15.1 us
  Pallas kernels: 28.7 us -> 29.8 us
    ppermute x2 -> x0, starting transfers between devices: 5.85 us -> none  [shifted(): lax.ppermute(value, 'seq', [(source, source + steps) for source in range(...]
    ppermute x4 -> x6, waiting for transfers between devices: 5.57 us -> 10.3 us  [seq_permute(): lax.ppermute(value, 'seq', [(source, target(source) % 8) for source in ra...]
    pallas_call x10 -> x11, Pallas kernels: 28.7 us -> 29.8 us  [call(): pl.pallas_call(kernel, out_shape=[jax.ShapeDtypeStruct(shape, dtype) for...]
    ppermute x4 -> x6, starting transfers between devices: 12.7 us -> 12.6 us  [seq_permute(): lax.ppermute(value, 'seq', [(source, target(source) % 8) for source in ra...]
  transfers between devices with their start and end apart: 13 -> 13, of which waited for: 7 -> 7; matrix products, arithmetic and copies ran while one was open for 0% -> 0% of each run, Pallas kernels for 25% -> 27%
where the time goes in v3:
time: 69.4 us; the launch traced here: 69.3 us
  Pallas kernels  29.8 us (43%)
  starting transfers between devices  23.6 us (34%)
  waiting for transfers between devices  15.1 us (22%)
  between operations  0.71 us (1%)
    pallas_call x11, Pallas kernels, call(): pl.pallas_call(kernel, out_shape=[jax.ShapeDtypeStruct(shape, dtype) for...  29.8 us
    ppermute x6, starting transfers between devices, seq_permute(): lax.ppermute(value, 'seq', [(source, target(source) % 8) for source in ra...  12.6 us
    ppermute x7, starting transfers between devices, dp_permute(): lax.ppermute(value, 'dp', [(source, target(source)) for source in range(3...  11 us
    ppermute x6, waiting for transfers between devices, seq_permute(): lax.ppermute(value, 'seq', [(source, target(source) % 8) for source in ra...  10.3 us
    ppermute x7, waiting for transfers between devices, dp_permute(): lax.ppermute(value, 'dp', [(source, target(source)) for source in range(3...  4.8 us
  transfers between devices with their start and end apart: 13, of which 7 were waited for; matrix products, arithmetic and copies ran while one was open for 0% of the time, Pallas kernels for 27%

profile of v3, /device:TPU:2, one launch (start us, length us, event | category | flops | bytes accessed | tf_op | source)
XLA Modules:
  0.0 69.3 jit_solution(8637723954369382232)
XLA Ops:
  0.6 1.1 %shard_map.84 = (s32[1,64]{1,0:T(1,128)S(1)}, bf16[4,256,128]{2,1,0:T(8,128)(2,1)S(1)}, bf16[6,256,128]{2,1,0:T(8,128)(2,1)S(1)}) custom-call(s32[1,64]{1,0:T(1,128)} %clips.1, bf16[8,256,128]{2,1,0:T(8,128)(2,1)} %bitcast.8, bf16[8,256,128]{2,1,0:T(8,128)(2,1)} %bitcast.10), custom_call_target="tpu_custom_call" | custom-call | bytes 1048576 | tf_op jit(solution)/shard_map/pallas_call | solution.py:393
  1.8 5.9 %collective-permute-start.1 = (bf16[6,256,128]{2,1,0:T(8,128)(2,1)S(1)}, bf16[6,256,128]{2,1,0:T(8,128)(2,1)S(1)}, u32[]{:S(2)}, u32[]{:S(2)}) collective-permute-start(bf16[6,256,128]{2,1,0:T(8,128)(2,1)S(1)} %get-tuple-element.60), channel_id=1, source_target_pairs={{0,224},{32,0},{64,32},{96,64},{128,96},{160,128},{192,160},{224,1... | collective-permute-start | bytes 1179656 | tf_op jit(solution)/shard_map/ppermute | solution.py:423
  7.7 0.0 collective-permute-start
  7.7 6.4 %shard_map.85 = (bf16[9,256,128]{2,1,0:T(8,128)(2,1)S(1)}, bf16[9,256,128]{2,1,0:T(8,128)(2,1)S(1)}, bf16[3456,128]{1,0:T(8,128)(2,1)S(1)}, bf16[3456,128]{1,0:T...) custom-call(s32[1,64]{1,0:T(1,128)S(1)} %get-tuple-element.61.clips,, ...), custom_call_target="tpu_custom_call" | custom-call | flops 2717908992 | bytes 1048576 | tf_op jit(solution)/shard_map/pallas_call | solution.py:393
  14.2 2.5 %collective-permute-done.tail = bf16[4,256,128]{2,1,0:T(8,128)(2,1)S(1)} collective-permute-done((bf16[4,256,128]{2,1,0:T(8,128)(2,1)S(1)}, bf16[4,256,128]{2,1,0:T(8,128)(2,1)S(1)}, u32[]{:S(2)}, u32[]{:S(2)}) %collective-permute-start) | collective-permute-done | bytes 262176 | tf_op jit(solution)/shard_map/ppermute | solution.py:423
  16.7 0.0 collective-permute-done.1.head
  16.7 9.1 %shard_map.86 = (bf16[8,256,128]{2,1,0:T(8,128)(2,1)S(1)}, bf16[8,256,128]{2,1,0:T(8,128)(2,1)S(1)}, f32[2,16,112,128]{3,2,1,0:T(8,128)S(1)}, bf16[2,16,112,128]{3,2,1,0:T(8,128)(2,1)S(1)}) custom-call(s32[1,64]{1,0:T(1,128)S(1)} %get-tuple-element.61.clips, bf16[9,256,128]{2,1,0:T(8,128)(2,1)S(1)} %get-tuple-element.71.frames, ...), custom_call_target="tpu_custom_call" | custom-call | flops 4529848320 | bytes 1048576 | tf_op jit(solution)/shard_map/pallas_call | solution.py:393
  25.8 0.3 collective-permute-start.2
  26.1 2.4 %shard_map.87.next_in = bf16[2,256,128]{2,1,0:T(8,128)(2,1)S(1)} custom-call(s32[1,64]{1,0:T(1,128)S(1)} %get-tuple-element.61.clips, bf16[9,256,128]{2,1,0:T(8,128)(2,1)S(1)} %get-tuple-element.71.frames, bf16[6,256,128]{2,1,0:T(8,128)(2,1)S(1)} %collective-permute-done.1.head, bf16[1152,384]{1,0:T(8,128)(2,1)S(1)} %get-tuple-element.74.conv_weight, ...), custom_call_target="tpu_custom_call" | custom-call | flops 905969664 | bytes 1048576 | tf_op jit(solution)/shard_map/pallas_call | solution.py:393
  28.6 0.0 collective-permute-done.2
  28.6 0.2 shard_map.88
  28.8 1.6 %collective-permute-start.3 = (bf16[2,4,112,128]{3,2,1,0:T(8,128)(2,1)S(1)}, bf16[2,4,112,128]{3,2,1,0:T(8,128)(2,1)S(1)}, u32[]{:S(2)}, u32[]{:S(2)}) collective-permute-start(bf16[2,4,112,128]{3,2,1,0:T(8,128)(2,1)S(1)} %get-tuple-element.87), channel_id=1, source_target_pairs={{0,2},{1,3},{2,4},{3,5},{4,6},{5,7},{6,0},{7,1},{8,10},{9,11},{10,... | collective-permute-start | bytes 688136 | tf_op jit(solution)/shard_map/ppermute | solution.py:419
  30.3 1.1 %collective-permute-start.4 = (bf16[2,4,112,128]{3,2,1,0:T(8,128)(2,1)S(1)}, bf16[2,4,112,128]{3,2,1,0:T(8,128)(2,1)S(1)}, u32[]{:S(2)}, u32[]{:S(2)}) collective-permute-start(bf16[2,4,112,128]{3,2,1,0:T(8,128)(2,1)S(1)} %get-tuple-element.88), channel_id=1, source_target_pairs={{0,4},{1,5},{2,6},{3,7},{4,0},{5,1},{6,2},{7,3},{8,12},{9,13},{10,... | collective-permute-start | bytes 688136 | tf_op jit(solution)/shard_map/ppermute | solution.py:419
  31.5 2.2 %collective-permute-start.5 = (bf16[2,4,112,128]{3,2,1,0:T(8,128)(2,1)S(1)}, bf16[2,4,112,128]{3,2,1,0:T(8,128)(2,1)S(1)}, u32[]{:S(2)}, u32[]{:S(2)}) collective-permute-start(bf16[2,4,112,128]{3,2,1,0:T(8,128)(2,1)S(1)} %get-tuple-element.89), channel_id=1, source_target_pairs={{0,6},{1,7},{2,0},{3,1},{4,2},{5,3},{6,4},{7,5},{8,14},{9,15},{10,... | collective-permute-start | bytes 688136 | tf_op jit(solution)/shard_map/ppermute | solution.py:419
  33.6 5.4 %shard_map.89 = bf16[8,256,128]{2,1,0:T(8,128)(2,1)} custom-call(s32[1,64]{1,0:T(1,128)S(1)} %get-tuple-element.61.clips, bf16[8,256,128]{2,1,0:T(8,128)(2,1)S(1)} %get-tuple-element.90.hidden_in, bf16[9,256,128]{2,1,0:T(8,128)(2,1)S(1)} %get-tuple-element.71.frames, bf16[4,256,128]{2,1,0:T(8,128)(2,1)S(1)} %collective-permute-done.tail, ...), custom_call_target="tpu_custom_call" | custom-call | flops 2264924160 | bytes 1048576 | tf_op jit(solution)/shard_map/pallas_call | solution.py:393
  39.0 0.0 collective-permute-done.3.refs_0_
  39.0 1.3 %collective-permute-done.4.refs_1_ = bf16[2,4,112,128]{3,2,1,0:T(8,128)(2,1)S(1)} collective-permute-done((bf16[2,4,112,128]{3,2,1,0:T(8,128)(2,1)S(1)}, bf16[2,4,112,128]{3,2,1,0:T(8,128)(2,1)S(1)}, u32[]{:S(2)}, u32[]{:S(2)}) %collective-permute-start.4) | collective-permute-done | bytes 229408 | tf_op jit(solution)/shard_map/ppermute | solution.py:419
  40.3 3.5 %collective-permute-done.5.refs_2_ = bf16[2,4,112,128]{3,2,1,0:T(8,128)(2,1)S(1)} collective-permute-done((bf16[2,4,112,128]{3,2,1,0:T(8,128)(2,1)S(1)}, bf16[2,4,112,128]{3,2,1,0:T(8,128)(2,1)S(1)}, u32[]{:S(2)}, u32[]{:S(2)}) %collective-permute-start.5) | collective-permute-done | bytes 229408 | tf_op jit(solution)/shard_map/ppermute | solution.py:419
  43.8 0.1 shard_map.90
  43.9 1.6 %collective-permute-start.6 = (bf16[2,112,128]{2,1,0:T(8,128)(2,1)S(1)}, bf16[2,112,128]{2,1,0:T(8,128)(2,1)S(1)}, u32[]{:S(2)}, u32[]{:S(2)}) collective-permute-start(bf16[2,112,128]{2,1,0:T(8,128)(2,1)S(1)} %get-tuple-element.101), channel_id=1, source_target_pairs={{0,8},{1,9},{2,10},{3,11},{4,12},{5,13},{6,14},{7,15},{8,16},{9,17... | collective-permute-start | bytes 172040 | tf_op jit(solution)/shard_map/ppermute | solution.py:419
  45.6 2.9 %collective-permute-start.7 = (bf16[2,112,128]{2,1,0:T(8,128)(2,1)S(1)}, bf16[2,112,128]{2,1,0:T(8,128)(2,1)S(1)}, u32[]{:S(2)}, u32[]{:S(2)}) collective-permute-start(bf16[2,112,128]{2,1,0:T(8,128)(2,1)S(1)} %get-tuple-element.102), channel_id=1, source_target_pairs={{0,16},{1,17},{2,18},{3,19},{4,20},{5,21},{6,22},{7,23},{8,24},{9,... | collective-permute-start | bytes 172040 | tf_op jit(solution)/shard_map/ppermute | solution.py:419
  48.4 1.4 %collective-permute-start.8 = (bf16[2,112,128]{2,1,0:T(8,128)(2,1)S(1)}, bf16[2,112,128]{2,1,0:T(8,128)(2,1)S(1)}, u32[]{:S(2)}, u32[]{:S(2)}) collective-permute-start(bf16[2,112,128]{2,1,0:T(8,128)(2,1)S(1)} %get-tuple-element.103), channel_id=1, source_target_pairs={{0,24},{1,25},{2,26},{3,27},{4,28},{5,29},{6,30},{7,31},{8,0},{9,1... | collective-permute-start | bytes 172040 | tf_op jit(solution)/shard_map/ppermute | solution.py:419
  49.8 4.3 %shard_map.91 = bf16[8,256,128]{2,1,0:T(8,128)(2,1)} custom-call(s32[1,64]{1,0:T(1,128)S(1)} %get-tuple-element.61.clips, bf16[8,256,128]{2,1,0:T(8,128)(2,1)S(1)} %get-tuple-element.104.act_grad_in, bf16[2,256,128]{2,1,0:T(8,128)(2,1)S(1)} %shard_map.87.next_in, bf16[9,256,128]{2,1,0:T(8,128)(2,1)S(1)} %get-tuple-element.72.cot, ...), custom_call_target="tpu_custom_call" | custom-call | flops 1811939328 | bytes 1048576 | tf_op jit(solution)/shard_map/pallas_call | solution.py:393
  54.1 0.0 collective-permute-done.6.refs_0_
  54.1 0.0 collective-permute-done.7.refs_1_
  54.1 0.0 collective-permute-done.8.refs_2_
  54.1 0.1 collective-permute-start.9
  54.2 4.2 %collective-permute-done.9.refs_0_ = bf16[2,112,128]{2,1,0:T(8,128)(2,1)S(1)} collective-permute-done((bf16[2,112,128]{2,1,0:T(8,128)(2,1)S(1)}, bf16[2,112,128]{2,1,0:T(8,128)(2,1)S(1)}, u32[]{:S(2)}, u32[]{:S(2)}) %collective-permute-start.9) | collective-permute-done | bytes 57376 | tf_op jit(solution)/shard_map/ppermute | solution.py:423
  58.4 2.8 %collective-permute-start.12 = (bf16[2,112,128]{2,1,0:T(8,128)(2,1)S(1)}, bf16[2,112,128]{2,1,0:T(8,128)(2,1)S(1)}, u32[]{:S(2)}, u32[]{:S(2)}) collective-permute-start(bf16[2,112,128]{2,1,0:T(8,128)(2,1)S(1)} %shard_map.93.refs_0_), channel_id=1, source_target_pairs={{0,160},{32,128},{64,224},{96,192},{128,32},{160,0},{192,96},{224,... | collective-permute-start | bytes 172040 | tf_op jit(solution)/shard_map/ppermute | solution.py:423
  61.2 2.0 %collective-permute-start.11 = (bf16[2,112,128]{2,1,0:T(8,128)(2,1)S(1)}, bf16[2,112,128]{2,1,0:T(8,128)(2,1)S(1)}, u32[]{:S(2)}, u32[]{:S(2)}) collective-permute-start(bf16[2,112,128]{2,1,0:T(8,128)(2,1)S(1)} %shard_map.93.refs_0_), channel_id=1, source_target_pairs={{0,192},{32,96},{64,0},{96,160},{128,64},{160,224},{192,128},{224,... | collective-permute-start | bytes 172040 | tf_op jit(solution)/shard_map/ppermute | solution.py:423
  63.2 1.8 %collective-permute-start.10 = (bf16[2,112,128]{2,1,0:T(8,128)(2,1)S(1)}, bf16[2,112,128]{2,1,0:T(8,128)(2,1)S(1)}, u32[]{:S(2)}, u32[]{:S(2)}) collective-permute-start(bf16[2,112,128]{2,1,0:T(8,128)(2,1)S(1)} %shard_map.93.refs_0_), channel_id=1, source_target_pairs={{0,224},{32,64},{64,32},{96,128},{128,96},{160,192},{192,160},{224... | collective-permute-start | bytes 172040 | tf_op jit(solution)/shard_map/ppermute | solution.py:423
  65.0 0.7 %collective-permute-done.12.refs_3_ = bf16[2,112,128]{2,1,0:T(8,128)(2,1)S(1)} collective-permute-done((bf16[2,112,128]{2,1,0:T(8,128)(2,1)S(1)}, bf16[2,112,128]{2,1,0:T(8,128)(2,1)S(1)}, u32[]{:S(2)}, u32[]{:S(2)}) %collective-permute-start.12) | collective-permute-done | bytes 57376 | tf_op jit(solution)/shard_map/ppermute | solution.py:423
  65.7 1.0 %collective-permute-done.11.refs_2_ = bf16[2,112,128]{2,1,0:T(8,128)(2,1)S(1)} collective-permute-done((bf16[2,112,128]{2,1,0:T(8,128)(2,1)S(1)}, bf16[2,112,128]{2,1,0:T(8,128)(2,1)S(1)}, u32[]{:S(2)}, u32[]{:S(2)}) %collective-permute-start.11) | collective-permute-done | bytes 57376 | tf_op jit(solution)/shard_map/ppermute | solution.py:423
  66.7 1.9 %collective-permute-done.10.refs_1_ = bf16[2,112,128]{2,1,0:T(8,128)(2,1)S(1)} collective-permute-done((bf16[2,112,128]{2,1,0:T(8,128)(2,1)S(1)}, bf16[2,112,128]{2,1,0:T(8,128)(2,1)S(1)}, u32[]{:S(2)}, u32[]{:S(2)}) %collective-permute-start.10) | collective-permute-done | bytes 57376 | tf_op jit(solution)/shard_map/ppermute | solution.py:423
  68.6 0.7 shard_map.94
  (2 shorter events, 0.0 us)
Async XLA Ops:
  1.8 14.9 %collective-permute-start.1 = (bf16[6,256,128]{2,1,0:T(8,128)(2,1)S(1)}, bf16[6,256,128]{2,1,0:T(8,128)(2,1)S(1)}, u32[]{:S(2)}, u32[]{:S(2)}) collective-permute-start(bf16[6,256,128]{2,1,0:T(8,128)(2,1)S(1)} %get-tuple-element.60), channel_id=1, source_target_pairs={{0,224},{32,0},{64,32},{96,64},{128,96},{160,128},{192,160},{224,1... | collective-permute-start | bytes 1179656 | tf_op jit(solution)/shard_map/ppermute | solution.py:423
  7.7 9.0 %collective-permute-start = (bf16[4,256,128]{2,1,0:T(8,128)(2,1)S(1)}, bf16[4,256,128]{2,1,0:T(8,128)(2,1)S(1)}, u32[]{:S(2)}, u32[]{:S(2)}) collective-permute-start(bf16[4,256,128]{2,1,0:T(8,128)(2,1)S(1)} %get-tuple-element.59), channel_id=1, source_target_pairs={{0,32},{32,64},{64,96},{96,128},{128,160},{160,192},{192,224},{224... | collective-permute-start | bytes 786440 | tf_op jit(solution)/shard_map/ppermute | solution.py:423
  25.8 2.7 %collective-permute-start.2 = (bf16[2,16,112,128]{3,2,1,0:T(8,128)(2,1)S(1)}, bf16[2,16,112,128]{3,2,1,0:T(8,128)(2,1)S(1)}, u32[]{:S(2)}, u32[]{:S(2)}) collective-permute-start(bf16[2,16,112,128]{3,2,1,0:T(8,128)(2,1)S(1)} %get-tuple-element.80), channel_id=1, source_target_pairs={{0,1},{1,0},{2,3},{3,2},{4,5},{5,4},{6,7},{7,6},{8,9},{9,8},{10,11... | collective-permute-start | bytes 2752520 | tf_op jit(solution)/shard_map/ppermute | solution.py:419
  28.8 10.3 %collective-permute-start.3 = (bf16[2,4,112,128]{3,2,1,0:T(8,128)(2,1)S(1)}, bf16[2,4,112,128]{3,2,1,0:T(8,128)(2,1)S(1)}, u32[]{:S(2)}, u32[]{:S(2)}) collective-permute-start(bf16[2,4,112,128]{3,2,1,0:T(8,128)(2,1)S(1)} %get-tuple-element.87), channel_id=1, source_target_pairs={{0,2},{1,3},{2,4},{3,5},{4,6},{5,7},{6,0},{7,1},{8,10},{9,11},{10,... | collective-permute-start | bytes 688136 | tf_op jit(solution)/shard_map/ppermute | solution.py:419
  30.3 10.0 %collective-permute-start.4 = (bf16[2,4,112,128]{3,2,1,0:T(8,128)(2,1)S(1)}, bf16[2,4,112,128]{3,2,1,0:T(8,128)(2,1)S(1)}, u32[]{:S(2)}, u32[]{:S(2)}) collective-permute-start(bf16[2,4,112,128]{3,2,1,0:T(8,128)(2,1)S(1)} %get-tuple-element.88), channel_id=1, source_target_pairs={{0,4},{1,5},{2,6},{3,7},{4,0},{5,1},{6,2},{7,3},{8,12},{9,13},{10,... | collective-permute-start | bytes 688136 | tf_op jit(solution)/shard_map/ppermute | solution.py:419
  31.5 12.4 %collective-permute-start.5 = (bf16[2,4,112,128]{3,2,1,0:T(8,128)(2,1)S(1)}, bf16[2,4,112,128]{3,2,1,0:T(8,128)(2,1)S(1)}, u32[]{:S(2)}, u32[]{:S(2)}) collective-permute-start(bf16[2,4,112,128]{3,2,1,0:T(8,128)(2,1)S(1)} %get-tuple-element.89), channel_id=1, source_target_pairs={{0,6},{1,7},{2,0},{3,1},{4,2},{5,3},{6,4},{7,5},{8,14},{9,15},{10,... | collective-permute-start | bytes 688136 | tf_op jit(solution)/shard_map/ppermute | solution.py:419
  43.9 10.2 %collective-permute-start.6 = (bf16[2,112,128]{2,1,0:T(8,128)(2,1)S(1)}, bf16[2,112,128]{2,1,0:T(8,128)(2,1)S(1)}, u32[]{:S(2)}, u32[]{:S(2)}) collective-permute-start(bf16[2,112,128]{2,1,0:T(8,128)(2,1)S(1)} %get-tuple-element.101), channel_id=1, source_target_pairs={{0,8},{1,9},{2,10},{3,11},{4,12},{5,13},{6,14},{7,15},{8,16},{9,17... | collective-permute-start | bytes 172040 | tf_op jit(solution)/shard_map/ppermute | solution.py:419
  45.6 8.5 %collective-permute-start.7 = (bf16[2,112,128]{2,1,0:T(8,128)(2,1)S(1)}, bf16[2,112,128]{2,1,0:T(8,128)(2,1)S(1)}, u32[]{:S(2)}, u32[]{:S(2)}) collective-permute-start(bf16[2,112,128]{2,1,0:T(8,128)(2,1)S(1)} %get-tuple-element.102), channel_id=1, source_target_pairs={{0,16},{1,17},{2,18},{3,19},{4,20},{5,21},{6,22},{7,23},{8,24},{9,... | collective-permute-start | bytes 172040 | tf_op jit(solution)/shard_map/ppermute | solution.py:419
  48.4 5.7 %collective-permute-start.8 = (bf16[2,112,128]{2,1,0:T(8,128)(2,1)S(1)}, bf16[2,112,128]{2,1,0:T(8,128)(2,1)S(1)}, u32[]{:S(2)}, u32[]{:S(2)}) collective-permute-start(bf16[2,112,128]{2,1,0:T(8,128)(2,1)S(1)} %get-tuple-element.103), channel_id=1, source_target_pairs={{0,24},{1,25},{2,26},{3,27},{4,28},{5,29},{6,30},{7,31},{8,0},{9,1... | collective-permute-start | bytes 172040 | tf_op jit(solution)/shard_map/ppermute | solution.py:419
  54.1 4.3 %collective-permute-start.9 = (bf16[2,112,128]{2,1,0:T(8,128)(2,1)S(1)}, bf16[2,112,128]{2,1,0:T(8,128)(2,1)S(1)}, u32[]{:S(2)}, u32[]{:S(2)}) collective-permute-start(bf16[2,112,128]{2,1,0:T(8,128)(2,1)S(1)} %shard_map.92.keep_ref), channel_id=1, source_target_pairs={{0,32},{32,0},{64,96},{96,64},{128,160},{160,128},{192,224},{224,1... | collective-permute-start | bytes 172040 | tf_op jit(solution)/shard_map/ppermute | solution.py:423
  58.4 7.3 %collective-permute-start.12 = (bf16[2,112,128]{2,1,0:T(8,128)(2,1)S(1)}, bf16[2,112,128]{2,1,0:T(8,128)(2,1)S(1)}, u32[]{:S(2)}, u32[]{:S(2)}) collective-permute-start(bf16[2,112,128]{2,1,0:T(8,128)(2,1)S(1)} %shard_map.93.refs_0_), channel_id=1, source_target_pairs={{0,160},{32,128},{64,224},{96,192},{128,32},{160,0},{192,96},{224,... | collective-permute-start | bytes 172040 | tf_op jit(solution)/shard_map/ppermute | solution.py:423
  61.2 5.4 %collective-permute-start.11 = (bf16[2,112,128]{2,1,0:T(8,128)(2,1)S(1)}, bf16[2,112,128]{2,1,0:T(8,128)(2,1)S(1)}, u32[]{:S(2)}, u32[]{:S(2)}) collective-permute-start(bf16[2,112,128]{2,1,0:T(8,128)(2,1)S(1)} %shard_map.93.refs_0_), channel_id=1, source_target_pairs={{0,192},{32,96},{64,0},{96,160},{128,64},{160,224},{192,128},{224,... | collective-permute-start | bytes 172040 | tf_op jit(solution)/shard_map/ppermute | solution.py:423
  63.2 5.4 %collective-permute-start.10 = (bf16[2,112,128]{2,1,0:T(8,128)(2,1)S(1)}, bf16[2,112,128]{2,1,0:T(8,128)(2,1)S(1)}, u32[]{:S(2)}, u32[]{:S(2)}) collective-permute-start(bf16[2,112,128]{2,1,0:T(8,128)(2,1)S(1)} %shard_map.93.refs_0_), channel_id=1, source_target_pairs={{0,224},{32,64},{64,32},{96,128},{128,96},{160,192},{192,160},{224... | collective-permute-start | bytes 172040 | tf_op jit(solution)/shard_map/ppermute | solution.py:423

commit v4 on v3

--- a/solution.py
+++ b/solution.py
@@ -340,22 +340,30 @@
         out_ref[t] = (cot[t].astype(F32) + out).astype(BF16)
 
 
-def x_kernel(keep_ref, part, kept_ref, *sent_refs):
-    own = lax.rem(lax.div(lax.axis_index("dp"), 2), 4)
+def place():
+    index = lax.axis_index("dp")
+    return lax.div(index, 8), lax.rem(lax.div(index, 2), 4), lax.rem(index, 2) == 0
+
+
+def first_kernel(keep_ref, part, kept_ref, *sent_refs):
+    y, x, along_x = place()
     for g in range(2):
-        for y in range(4):
+        for other in range(4):
             for step in range(4):
-                block = lax.rem(own + step, 4)
-                total = keep_ref[g, y, block] + part[g, y, block].astype(F32)
+                block = jnp.where(
+                    along_x, 4 * other + lax.rem(x + step, 4), 4 * lax.rem(y + step, 4) + other
+                )
+                total = keep_ref[g, block] + part[g, block].astype(F32)
                 if step == 0:
-                    kept_ref[g, y] = total
+                    kept_ref[g, other] = total
                 else:
-                    sent_refs[step - 1][g, y] = total.astype(BF16)
-
-
-def y_kernel(keep_ref, *refs):
+                    sent_refs[step - 1][g, other] = total.astype(BF16)
+
+
+def second_kernel(keep_ref, *refs):
     received, (kept_ref, *sent_refs) = refs[:3], refs[3:]
-    own = lax.div(lax.axis_index("dp"), 8)
+    y, x, along_x = place()
+    own = jnp.where(along_x, y, x)
     for g in range(2):
         for step in range(4):
             block = lax.rem(own + step, 4)
@@ -417,6 +425,18 @@
 
 def dp_permute(value, target):
     return lax.ppermute(value, "dp", [(source, target(source)) for source in range(32)])
+
+
+def along_x(step):
+    return lambda d: (d // 8) * 8 + (d % 8 + 2 * step) % 8
+
+
+def along_y(step):
+    return lambda d: (d + 8 * step) % 32
+
+
+def crossed(first, second):
+    return lambda d: second(d) if d % 2 else first(d)
 
 
 def seq_permute(value, target):
@@ -494,15 +514,14 @@
     )
     recv, act_grad_next = lax.optimization_barrier((recv, act_grad_next))
     keep, *sent = call(
-        x_kernel,
-        (keep.reshape(2, 4, 4, PADDED, C), recv.reshape(2, 4, 4, PADDED, C)),
+        first_kernel,
+        (keep, recv),
         [VMEM] * 2,
         [((2, 4, PADDED, C), F32)] + [((2, 4, PADDED, C), BF16)] * 3,
     )
     sent, hidden = lax.optimization_barrier((sent, hidden))
     recv = [
-        dp_permute(part, lambda d, s=s: (d // 8) * 8 + (d % 8 + 2 * s) % 8)
-        for s, part in zip((1, 2, 3), sent)
+        dp_permute(part, crossed(along_x(s), along_y(s))) for s, part in zip((1, 2, 3), sent)
     ]
     (block_out,) = call(
         forward_kernel,
@@ -515,9 +534,19 @@
     )
     recv, block_out = lax.optimization_barrier((recv, block_out))
     pair = (2, PADDED, C)
-    keep, *sent = call(y_kernel, (keep, *recv), [VMEM] * 4, [(pair, F32)] + [(pair, BF16)] * 3)
-    sent, act_grad = lax.optimization_barrier((sent, act_grad))
-    recv = [dp_permute(part, lambda d, s=s: (d + 8 * s) % 32) for s, part in zip((1, 2, 3), sent)]
+    keep, *sent = call(
+        second_kernel, (keep, *recv), [VMEM] * 4, [(pair, F32)] + [(pair, BF16)] * 3
+    )
+    recv = [
+        dp_permute(part, crossed(along_y(s), along_x(s))) for s, part in zip((1, 2, 3), sent)
+    ]
+    (total,) = call(sum_kernel, (keep, *recv), [VMEM] * 4, [(pair, BF16)])
+    other = seq_permute(total, lambda z: z ^ 1)
+    (total,) = call(sum_kernel, (total, other), [VMEM] * 2, [(pair, BF16)])
+    total, act_grad = lax.optimization_barrier((total, act_grad))
+    others = [
+        seq_permute(total, lambda z, s=s: z + s if z % 2 else z - s) for s in (1, 2, 3)
+    ]
     (input_grad,) = call(
         backward_kernel,
         (clip_ids, act_grad, act_grad_next, cot_copy, weight1),
@@ -527,13 +556,7 @@
         flops=CONV_FLOPS,
         limit=8,
     )
-    recv, input_grad = lax.optimization_barrier((recv, input_grad))
-    (total,) = call(sum_kernel, (keep, *recv), [VMEM] * 4, [(pair, BF16)])
-    other = seq_permute(total, lambda z: z ^ 1)
-    (total,) = call(sum_kernel, (total, other), [VMEM] * 2, [(pair, BF16)])
-    others = [
-        seq_permute(total, lambda z, s=s: z + s if z % 2 else z - s) for s in (1, 2, 3)
-    ]
+    others, input_grad = lax.optimization_barrier((others, input_grad))
     rows = lax.axis_size("dp") * lax.axis_size("seq") * F * POS
     first_grad, second_grad = call(
         lambda *refs: last_kernel(rows**-0.5, *refs),

time: 69.4 us -> 65.5 us (0.944); the launches traced: 69.3 us -> 64.6 us
  waiting for transfers between devices: 15.1 us -> 10.3 us
    ppermute x6, waiting for transfers between devices: 10.3 us -> 6.7 us  [seq_permute(): lax.ppermute(value, 'seq', [(source, target(source) % 8) for source in ra...]
    ppermute x7, waiting for transfers between devices: 4.8 us -> 3.64 us  [dp_permute(): lax.ppermute(value, 'dp', [(source, target(source)) for source in range(3...]
  transfers between devices with their start and end apart: 13 -> 13, of which waited for: 7 -> 5; matrix products, arithmetic and copies ran while one was open for 0% -> 0% of each run, Pallas kernels for 27% -> 29%
where the time goes in v4:
time: 65.5 us; the launch traced here: 64.6 us
  Pallas kernels  29.9 us (46%)
  starting transfers between devices  23.7 us (36%)
  waiting for transfers between devices  10.3 us (16%)
  between operations  0.71 us (1%)
    pallas_call x11, Pallas kernels, call(): pl.pallas_call(kernel, out_shape=[jax.ShapeDtypeStruct(shape, dtype) for...  29.9 us
    ppermute x6, starting transfers between devices, seq_permute(): lax.ppermute(value, 'seq', [(source, target(source) % 8) for source in ra...  12.6 us
    ppermute x7, starting transfers between devices, dp_permute(): lax.ppermute(value, 'dp', [(source, target(source)) for source in range(3...  11.1 us
    ppermute x6, waiting for transfers between devices, seq_permute(): lax.ppermute(value, 'seq', [(source, target(source) % 8) for source in ra...  6.7 us
    ppermute x7, waiting for transfers between devices, dp_permute(): lax.ppermute(value, 'dp', [(source, target(source)) for source in range(3...  3.64 us
  transfers between devices with their start and end apart: 13, of which 5 were waited for; matrix products, arithmetic and copies ran while one was open for 0% of the time, Pallas kernels for 29%

profile of v4, /device:TPU:2, one launch (start us, length us, event | category | flops | bytes accessed | tf_op | source)
XLA Modules:
  0.0 64.6 jit_solution(16557104649687082350)
XLA Ops:
  0.6 1.1 %shard_map.84 = (s32[1,64]{1,0:T(1,128)S(1)}, bf16[4,256,128]{2,1,0:T(8,128)(2,1)S(1)}, bf16[6,256,128]{2,1,0:T(8,128)(2,1)S(1)}) custom-call(s32[1,64]{1,0:T(1,128)} %clips.1, bf16[8,256,128]{2,1,0:T(8,128)(2,1)} %bitcast.4, bf16[8,256,128]{2,1,0:T(8,128)(2,1)} %bitcast.6), custom_call_target="tpu_custom_call" | custom-call | bytes 1048576 | tf_op jit(solution)/shard_map/pallas_call | solution.py:401
  1.8 5.9 %collective-permute-start.1 = (bf16[6,256,128]{2,1,0:T(8,128)(2,1)S(1)}, bf16[6,256,128]{2,1,0:T(8,128)(2,1)S(1)}, u32[]{:S(2)}, u32[]{:S(2)}) collective-permute-start(bf16[6,256,128]{2,1,0:T(8,128)(2,1)S(1)} %get-tuple-element.58), channel_id=1, source_target_pairs={{0,224},{32,0},{64,32},{96,64},{128,96},{160,128},{192,160},{224,1... | collective-permute-start | bytes 1179656 | tf_op jit(solution)/shard_map/ppermute | solution.py:443
  7.7 0.0 collective-permute-start
  7.7 6.4 %shard_map.85 = (bf16[9,256,128]{2,1,0:T(8,128)(2,1)S(1)}, bf16[9,256,128]{2,1,0:T(8,128)(2,1)S(1)}, bf16[3456,128]{1,0:T(8,128)(2,1)S(1)}, bf16[3456,128]{1,0:T...) custom-call(s32[1,64]{1,0:T(1,128)S(1)} %get-tuple-element.59.clips,, ...), custom_call_target="tpu_custom_call" | custom-call | flops 2717908992 | bytes 1048576 | tf_op jit(solution)/shard_map/pallas_call | solution.py:401
  14.2 2.5 %collective-permute-done.tail = bf16[4,256,128]{2,1,0:T(8,128)(2,1)S(1)} collective-permute-done((bf16[4,256,128]{2,1,0:T(8,128)(2,1)S(1)}, bf16[4,256,128]{2,1,0:T(8,128)(2,1)S(1)}, u32[]{:S(2)}, u32[]{:S(2)}) %collective-permute-start) | collective-permute-done | bytes 262176 | tf_op jit(solution)/shard_map/ppermute | solution.py:443
  16.7 0.0 collective-permute-done.1.head
  16.7 9.1 %shard_map.86 = (bf16[8,256,128]{2,1,0:T(8,128)(2,1)S(1)}, bf16[8,256,128]{2,1,0:T(8,128)(2,1)S(1)}, f32[2,16,112,128]{3,2,1,0:T(8,128)S(1)}, bf16[2,16,112,128]{3,2,1,0:T(8,128)(2,1)S(1)}) custom-call(s32[1,64]{1,0:T(1,128)S(1)} %get-tuple-element.59.clips, bf16[9,256,128]{2,1,0:T(8,128)(2,1)S(1)} %get-tuple-element.69.frames, ...), custom_call_target="tpu_custom_call" | custom-call | flops 4529848320 | bytes 1048576 | tf_op jit(solution)/shard_map/pallas_call | solution.py:401
  25.8 0.3 collective-permute-start.2
  26.1 2.4 %shard_map.87.next_in = bf16[2,256,128]{2,1,0:T(8,128)(2,1)S(1)} custom-call(s32[1,64]{1,0:T(1,128)S(1)} %get-tuple-element.59.clips, bf16[9,256,128]{2,1,0:T(8,128)(2,1)S(1)} %get-tuple-element.69.frames, bf16[6,256,128]{2,1,0:T(8,128)(2,1)S(1)} %collective-permute-done.1.head, bf16[1152,384]{1,0:T(8,128)(2,1)S(1)} %get-tuple-element.72.conv_weight, ...), custom_call_target="tpu_custom_call" | custom-call | flops 905969664 | bytes 1048576 | tf_op jit(solution)/shard_map/pallas_call | solution.py:401
  28.6 0.0 collective-permute-done.2.part
  28.6 0.2 shard_map.88
  28.8 1.5 %collective-permute-start.3 = (bf16[2,4,112,128]{3,2,1,0:T(8,128)(2,1)S(1)}, bf16[2,4,112,128]{3,2,1,0:T(8,128)(2,1)S(1)}, u32[]{:S(2)}, u32[]{:S(2)}) collective-permute-start(bf16[2,4,112,128]{3,2,1,0:T(8,128)(2,1)S(1)} %get-tuple-element.85), channel_id=1, source_target_pairs={{0,2},{1,9},{2,4},{3,11},{4,6},{5,13},{6,0},{7,15},{8,10},{9,17},{... | collective-permute-start | bytes 688136 | tf_op jit(solution)/shard_map/ppermute | solution.py:427
  30.3 1.1 %collective-permute-start.4 = (bf16[2,4,112,128]{3,2,1,0:T(8,128)(2,1)S(1)}, bf16[2,4,112,128]{3,2,1,0:T(8,128)(2,1)S(1)}, u32[]{:S(2)}, u32[]{:S(2)}) collective-permute-start(bf16[2,4,112,128]{3,2,1,0:T(8,128)(2,1)S(1)} %get-tuple-element.86), channel_id=1, source_target_pairs={{0,4},{1,17},{2,6},{3,19},{4,0},{5,21},{6,2},{7,23},{8,12},{9,25},... | collective-permute-start | bytes 688136 | tf_op jit(solution)/shard_map/ppermute | solution.py:427
  31.4 2.2 %collective-permute-start.5 = (bf16[2,4,112,128]{3,2,1,0:T(8,128)(2,1)S(1)}, bf16[2,4,112,128]{3,2,1,0:T(8,128)(2,1)S(1)}, u32[]{:S(2)}, u32[]{:S(2)}) collective-permute-start(bf16[2,4,112,128]{3,2,1,0:T(8,128)(2,1)S(1)} %get-tuple-element.87), channel_id=1, source_target_pairs={{0,6},{1,25},{2,0},{3,27},{4,2},{5,29},{6,4},{7,31},{8,14},{9,1},{... | collective-permute-start | bytes 688136 | tf_op jit(solution)/shard_map/ppermute | solution.py:427
  33.6 5.4 %shard_map.89 = bf16[8,256,128]{2,1,0:T(8,128)(2,1)} custom-call(s32[1,64]{1,0:T(1,128)S(1)} %get-tuple-element.59.clips, bf16[8,256,128]{2,1,0:T(8,128)(2,1)S(1)} %get-tuple-element.88.hidden_in, bf16[9,256,128]{2,1,0:T(8,128)(2,1)S(1)} %get-tuple-element.69.frames, bf16[4,256,128]{2,1,0:T(8,128)(2,1)S(1)} %collective-permute-done.tail, ...), custom_call_target="tpu_custom_call" | custom-call | flops 2264924160 | bytes 1048576 | tf_op jit(solution)/shard_map/pallas_call | solution.py:401
  39.0 0.0 collective-permute-done.3.refs_0_
  39.0 0.0 collective-permute-done.4.refs_1_
  39.0 0.8 %collective-permute-done.5.refs_2_ = bf16[2,4,112,128]{3,2,1,0:T(8,128)(2,1)S(1)} collective-permute-done((bf16[2,4,112,128]{3,2,1,0:T(8,128)(2,1)S(1)}, bf16[2,4,112,128]{3,2,1,0:T(8,128)(2,1)S(1)}, u32[]{:S(2)}, u32[]{:S(2)}) %collective-permute-start.5) | collective-permute-done | bytes 229408 | tf_op jit(solution)/shard_map/ppermute | solution.py:427
  39.9 0.1 shard_map.90
  40.0 1.7 %collective-permute-start.6 = (bf16[2,112,128]{2,1,0:T(8,128)(2,1)S(1)}, bf16[2,112,128]{2,1,0:T(8,128)(2,1)S(1)}, u32[]{:S(2)}, u32[]{:S(2)}) collective-permute-start(bf16[2,112,128]{2,1,0:T(8,128)(2,1)S(1)} %get-tuple-element.96), channel_id=1, source_target_pairs={{0,8},{1,3},{2,10},{3,5},{4,12},{5,7},{6,14},{7,1},{8,16},{9,11},{... | collective-permute-start | bytes 172040 | tf_op jit(solution)/shard_map/ppermute | solution.py:427
  41.7 2.8 %collective-permute-start.7 = (bf16[2,112,128]{2,1,0:T(8,128)(2,1)S(1)}, bf16[2,112,128]{2,1,0:T(8,128)(2,1)S(1)}, u32[]{:S(2)}, u32[]{:S(2)}) collective-permute-start(bf16[2,112,128]{2,1,0:T(8,128)(2,1)S(1)} %get-tuple-element.97), channel_id=1, source_target_pairs={{0,16},{1,5},{2,18},{3,7},{4,20},{5,1},{6,22},{7,3},{8,24},{9,13},... | collective-permute-start | bytes 172040 | tf_op jit(solution)/shard_map/ppermute | solution.py:427
  44.5 1.4 %collective-permute-start.8 = (bf16[2,112,128]{2,1,0:T(8,128)(2,1)S(1)}, bf16[2,112,128]{2,1,0:T(8,128)(2,1)S(1)}, u32[]{:S(2)}, u32[]{:S(2)}) collective-permute-start(bf16[2,112,128]{2,1,0:T(8,128)(2,1)S(1)} %get-tuple-element.98), channel_id=1, source_target_pairs={{0,24},{1,7},{2,26},{3,1},{4,28},{5,3},{6,30},{7,5},{8,0},{9,15},{... | collective-permute-start | bytes 172040 | tf_op jit(solution)/shard_map/ppermute | solution.py:427
  45.9 0.0 collective-permute-done.6.refs_0_
  45.9 1.4 %collective-permute-done.7.refs_1_ = bf16[2,112,128]{2,1,0:T(8,128)(2,1)S(1)} collective-permute-done((bf16[2,112,128]{2,1,0:T(8,128)(2,1)S(1)}, bf16[2,112,128]{2,1,0:T(8,128)(2,1)S(1)}, u32[]{:S(2)}, u32[]{:S(2)}) %collective-permute-start.7) | collective-permute-done | bytes 57376 | tf_op jit(solution)/shard_map/ppermute | solution.py:427
  47.4 1.3 %collective-permute-done.8.refs_2_ = bf16[2,112,128]{2,1,0:T(8,128)(2,1)S(1)} collective-permute-done((bf16[2,112,128]{2,1,0:T(8,128)(2,1)S(1)}, bf16[2,112,128]{2,1,0:T(8,128)(2,1)S(1)}, u32[]{:S(2)}, u32[]{:S(2)}) %collective-permute-start.8) | collective-permute-done | bytes 57376 | tf_op jit(solution)/shard_map/ppermute | solution.py:427
  48.7 0.1 collective-permute-start.9
  48.8 4.2 %collective-permute-done.9.refs_0_ = bf16[2,112,128]{2,1,0:T(8,128)(2,1)S(1)} collective-permute-done((bf16[2,112,128]{2,1,0:T(8,128)(2,1)S(1)}, bf16[2,112,128]{2,1,0:T(8,128)(2,1)S(1)}, u32[]{:S(2)}, u32[]{:S(2)}) %collective-permute-start.9) | collective-permute-done | bytes 57376 | tf_op jit(solution)/shard_map/ppermute | solution.py:443
  53.0 2.9 %collective-permute-start.12 = (bf16[2,112,128]{2,1,0:T(8,128)(2,1)S(1)}, bf16[2,112,128]{2,1,0:T(8,128)(2,1)S(1)}, u32[]{:S(2)}, u32[]{:S(2)}) collective-permute-start(bf16[2,112,128]{2,1,0:T(8,128)(2,1)S(1)} %shard_map.92.refs_0_), channel_id=1, source_target_pairs={{0,160},{32,128},{64,224},{96,192},{128,32},{160,0},{192,96},{224,... | collective-permute-start | bytes 172040 | tf_op jit(solution)/shard_map/ppermute | solution.py:443
  55.9 1.9 %collective-permute-start.11 = (bf16[2,112,128]{2,1,0:T(8,128)(2,1)S(1)}, bf16[2,112,128]{2,1,0:T(8,128)(2,1)S(1)}, u32[]{:S(2)}, u32[]{:S(2)}) collective-permute-start(bf16[2,112,128]{2,1,0:T(8,128)(2,1)S(1)} %shard_map.92.refs_0_), channel_id=1, source_target_pairs={{0,192},{32,96},{64,0},{96,160},{128,64},{160,224},{192,128},{224,... | collective-permute-start | bytes 172040 | tf_op jit(solution)/shard_map/ppermute | solution.py:443
  57.9 1.8 %collective-permute-start.10 = (bf16[2,112,128]{2,1,0:T(8,128)(2,1)S(1)}, bf16[2,112,128]{2,1,0:T(8,128)(2,1)S(1)}, u32[]{:S(2)}, u32[]{:S(2)}) collective-permute-start(bf16[2,112,128]{2,1,0:T(8,128)(2,1)S(1)} %shard_map.92.refs_0_), channel_id=1, source_target_pairs={{0,224},{32,64},{64,32},{96,128},{128,96},{160,192},{192,160},{224... | collective-permute-start | bytes 172040 | tf_op jit(solution)/shard_map/ppermute | solution.py:443
  59.6 4.3 %shard_map.93 = bf16[8,256,128]{2,1,0:T(8,128)(2,1)} custom-call(s32[1,64]{1,0:T(1,128)S(1)} %get-tuple-element.59.clips, bf16[8,256,128]{2,1,0:T(8,128)(2,1)S(1)} %get-tuple-element.101.act_grad_in, bf16[2,256,128]{2,1,0:T(8,128)(2,1)S(1)} %shard_map.87.next_in, bf16[9,256,128]{2,1,0:T(8,128)(2,1)S(1)} %get-tuple-element.70.cot, ...), custom_call_target="tpu_custom_call" | custom-call | flops 1811939328 | bytes 1048576 | tf_op jit(solution)/shard_map/pallas_call | solution.py:401
  63.9 0.0 collective-permute-done.12.refs_3_
  63.9 0.0 collective-permute-done.11.refs_2_
  63.9 0.0 collective-permute-done.10.refs_1_
  63.9 0.7 %shard_map.94 = (f32[108,128]{1,0:T(8,128)}, f32[108,128]{1,0:T(8,128)}) custom-call(bf16[2,112,128]{2,1,0:T(8,128)(2,1)S(1)} %shard_map.92.refs_0_, bf16[2,112,128]{2,1,0:T(8,128)(2,1)S(1)} %collective-permute-done.10.refs_1_, bf16[2,112,128]{2,1,0:T(8,128)(2,1)S(1)} %collective-permute-done.11.refs_2_, bf16[2,112,128]{2,1,0:T(8,128)(2,1)S(1)} %collective-permute-done.12.refs_3_), custom_call_target="tpu_custom_call" | custom-call | bytes 1048576 | tf_op jit(solution)/shard_map/pallas_call | solution.py:401
  (2 shorter events, 0.0 us)
Async XLA Ops:
  1.8 14.9 %collective-permute-start.1 = (bf16[6,256,128]{2,1,0:T(8,128)(2,1)S(1)}, bf16[6,256,128]{2,1,0:T(8,128)(2,1)S(1)}, u32[]{:S(2)}, u32[]{:S(2)}) collective-permute-start(bf16[6,256,128]{2,1,0:T(8,128)(2,1)S(1)} %get-tuple-element.58), channel_id=1, source_target_pairs={{0,224},{32,0},{64,32},{96,64},{128,96},{160,128},{192,160},{224,1... | collective-permute-start | bytes 1179656 | tf_op jit(solution)/shard_map/ppermute | solution.py:443
  7.7 9.0 %collective-permute-start = (bf16[4,256,128]{2,1,0:T(8,128)(2,1)S(1)}, bf16[4,256,128]{2,1,0:T(8,128)(2,1)S(1)}, u32[]{:S(2)}, u32[]{:S(2)}) collective-permute-start(bf16[4,256,128]{2,1,0:T(8,128)(2,1)S(1)} %get-tuple-element.57), channel_id=1, source_target_pairs={{0,32},{32,64},{64,96},{96,128},{128,160},{160,192},{192,224},{224... | collective-permute-start | bytes 786440 | tf_op jit(solution)/shard_map/ppermute | solution.py:443
  25.8 2.7 %collective-permute-start.2 = (bf16[2,16,112,128]{3,2,1,0:T(8,128)(2,1)S(1)}, bf16[2,16,112,128]{3,2,1,0:T(8,128)(2,1)S(1)}, u32[]{:S(2)}, u32[]{:S(2)}) collective-permute-start(bf16[2,16,112,128]{3,2,1,0:T(8,128)(2,1)S(1)} %get-tuple-element.78), channel_id=1, source_target_pairs={{0,1},{1,0},{2,3},{3,2},{4,5},{5,4},{6,7},{7,6},{8,9},{9,8},{10,11... | collective-permute-start | bytes 2752520 | tf_op jit(solution)/shard_map/ppermute | solution.py:427
  28.8 10.2 %collective-permute-start.3 = (bf16[2,4,112,128]{3,2,1,0:T(8,128)(2,1)S(1)}, bf16[2,4,112,128]{3,2,1,0:T(8,128)(2,1)S(1)}, u32[]{:S(2)}, u32[]{:S(2)}) collective-permute-start(bf16[2,4,112,128]{3,2,1,0:T(8,128)(2,1)S(1)} %get-tuple-element.85), channel_id=1, source_target_pairs={{0,2},{1,9},{2,4},{3,11},{4,6},{5,13},{6,0},{7,15},{8,10},{9,17},{... | collective-permute-start | bytes 688136 | tf_op jit(solution)/shard_map/ppermute | solution.py:427
  30.3 8.7 %collective-permute-start.4 = (bf16[2,4,112,128]{3,2,1,0:T(8,128)(2,1)S(1)}, bf16[2,4,112,128]{3,2,1,0:T(8,128)(2,1)S(1)}, u32[]{:S(2)}, u32[]{:S(2)}) collective-permute-start(bf16[2,4,112,128]{3,2,1,0:T(8,128)(2,1)S(1)} %get-tuple-element.86), channel_id=1, source_target_pairs={{0,4},{1,17},{2,6},{3,19},{4,0},{5,21},{6,2},{7,23},{8,12},{9,25},... | collective-permute-start | bytes 688136 | tf_op jit(solution)/shard_map/ppermute | solution.py:427
  31.4 8.5 %collective-permute-start.5 = (bf16[2,4,112,128]{3,2,1,0:T(8,128)(2,1)S(1)}, bf16[2,4,112,128]{3,2,1,0:T(8,128)(2,1)S(1)}, u32[]{:S(2)}, u32[]{:S(2)}) collective-permute-start(bf16[2,4,112,128]{3,2,1,0:T(8,128)(2,1)S(1)} %get-tuple-element.87), channel_id=1, source_target_pairs={{0,6},{1,25},{2,0},{3,27},{4,2},{5,29},{6,4},{7,31},{8,14},{9,1},{... | collective-permute-start | bytes 688136 | tf_op jit(solution)/shard_map/ppermute | solution.py:427
  40.0 5.9 %collective-permute-start.6 = (bf16[2,112,128]{2,1,0:T(8,128)(2,1)S(1)}, bf16[2,112,128]{2,1,0:T(8,128)(2,1)S(1)}, u32[]{:S(2)}, u32[]{:S(2)}) collective-permute-start(bf16[2,112,128]{2,1,0:T(8,128)(2,1)S(1)} %get-tuple-element.96), channel_id=1, source_target_pairs={{0,8},{1,3},{2,10},{3,5},{4,12},{5,7},{6,14},{7,1},{8,16},{9,11},{... | collective-permute-start | bytes 172040 | tf_op jit(solution)/shard_map/ppermute | solution.py:427
  41.7 5.7 %collective-permute-start.7 = (bf16[2,112,128]{2,1,0:T(8,128)(2,1)S(1)}, bf16[2,112,128]{2,1,0:T(8,128)(2,1)S(1)}, u32[]{:S(2)}, u32[]{:S(2)}) collective-permute-start(bf16[2,112,128]{2,1,0:T(8,128)(2,1)S(1)} %get-tuple-element.97), channel_id=1, source_target_pairs={{0,16},{1,5},{2,18},{3,7},{4,20},{5,1},{6,22},{7,3},{8,24},{9,13},... | collective-permute-start | bytes 172040 | tf_op jit(solution)/shard_map/ppermute | solution.py:427
  44.5 4.2 %collective-permute-start.8 = (bf16[2,112,128]{2,1,0:T(8,128)(2,1)S(1)}, bf16[2,112,128]{2,1,0:T(8,128)(2,1)S(1)}, u32[]{:S(2)}, u32[]{:S(2)}) collective-permute-start(bf16[2,112,128]{2,1,0:T(8,128)(2,1)S(1)} %get-tuple-element.98), channel_id=1, source_target_pairs={{0,24},{1,7},{2,26},{3,1},{4,28},{5,3},{6,30},{7,5},{8,0},{9,15},{... | collective-permute-start | bytes 172040 | tf_op jit(solution)/shard_map/ppermute | solution.py:427
  48.7 4.3 %collective-permute-start.9 = (bf16[2,112,128]{2,1,0:T(8,128)(2,1)S(1)}, bf16[2,112,128]{2,1,0:T(8,128)(2,1)S(1)}, u32[]{:S(2)}, u32[]{:S(2)}) collective-permute-start(bf16[2,112,128]{2,1,0:T(8,128)(2,1)S(1)} %shard_map.91.keep_ref), channel_id=1, source_target_pairs={{0,32},{32,0},{64,96},{96,64},{128,160},{160,128},{192,224},{224,1... | collective-permute-start | bytes 172040 | tf_op jit(solution)/shard_map/ppermute | solution.py:443
  53.0 10.9 %collective-permute-start.12 = (bf16[2,112,128]{2,1,0:T(8,128)(2,1)S(1)}, bf16[2,112,128]{2,1,0:T(8,128)(2,1)S(1)}, u32[]{:S(2)}, u32[]{:S(2)}) collective-permute-start(bf16[2,112,128]{2,1,0:T(8,128)(2,1)S(1)} %shard_map.92.refs_0_), channel_id=1, source_target_pairs={{0,160},{32,128},{64,224},{96,192},{128,32},{160,0},{192,96},{224,... | collective-permute-start | bytes 172040 | tf_op jit(solution)/shard_map/ppermute | solution.py:443
  55.9 8.0 %collective-permute-start.11 = (bf16[2,112,128]{2,1,0:T(8,128)(2,1)S(1)}, bf16[2,112,128]{2,1,0:T(8,128)(2,1)S(1)}, u32[]{:S(2)}, u32[]{:S(2)}) collective-permute-start(bf16[2,112,128]{2,1,0:T(8,128)(2,1)S(1)} %shard_map.92.refs_0_), channel_id=1, source_target_pairs={{0,192},{32,96},{64,0},{96,160},{128,64},{160,224},{192,128},{224,... | collective-permute-start | bytes 172040 | tf_op jit(solution)/shard_map/ppermute | solution.py:443
  57.9 6.0 %collective-permute-start.10 = (bf16[2,112,128]{2,1,0:T(8,128)(2,1)S(1)}, bf16[2,112,128]{2,1,0:T(8,128)(2,1)S(1)}, u32[]{:S(2)}, u32[]{:S(2)}) collective-permute-start(bf16[2,112,128]{2,1,0:T(8,128)(2,1)S(1)} %shard_map.92.refs_0_), channel_id=1, source_target_pairs={{0,224},{32,64},{64,32},{96,128},{128,96},{160,192},{192,160},{224... | collective-permute-start | bytes 172040 | tf_op jit(solution)/shard_map/ppermute | solution.py:443

commit v5 on v4

--- a/solution.py
+++ b/solution.py
@@ -121,18 +121,22 @@
     return 1.0 / (1.0 + jnp.exp(-normed))
 
 
-def norm_adjoint(act, back, scale, count):
+def hidden_of(normed):
+    return (normed * gate_of(normed)).astype(BF16)
+
+
+def norm_adjoint(act, back, scale, work):
+    count = len(scale)
     first, second = [], []
     for t in range(count):
-        gate = gate_of(act[t])
-        grad = back[t] * (gate * (1.0 + act[t] * (1.0 - gate)))
-        back[t] = grad
+        normed = act(t)
+        gate = gate_of(normed)
+        grad = back(t) * (gate * (1.0 + normed * (1.0 - gate)))
+        work[t] = grad
         first.append(tile_sum(grad))
-        second.append(tile_sum(grad * act[t]))
+        second.append(tile_sum(grad * normed))
     first, second = group_mean(first), group_mean(second)
-    return [
-        (scale[t] * (back[t] - first[t] - act[t] * second[t])).astype(BF16) for t in range(count)
-    ]
+    return [(scale[t] * (work[t] - first[t] - act(t) * second[t])).astype(BF16) for t in range(count)]
 
 
 def first_frame():
@@ -150,6 +154,9 @@
         copy.start()
     for copy in copies:
         copy.wait()
+
+
+EDGE = F - 2
 
 
 def local_kernel(
@@ -166,6 +173,13 @@
     back_weight,
     act,
     back,
+    scales,
+    hidden,
+    frame_t,
+    cot_shifted,
+    second_part,
+    hidden_t,
+    cot_taps,
     sems,
 ):
     copies = [
@@ -178,17 +192,46 @@
         copy.start()
     window[F] = jnp.zeros((POS, C), BF16)
     cot_window[F] = jnp.zeros((POS, C), BF16)
+    frame_t[F] = jnp.zeros((3 * C, POS), BF16)
+    cot_shifted[F] = jnp.zeros((POS, 3 * C), BF16)
     first = first_frame()
     copies[0].wait()
     forward_weight(weight1_copy, conv_weight)
-    copies[1].wait()
+    for copy in copies[1:]:
+        copy.wait()
     for t in range(2, F):
         act[t] = conv_frame(window, past_slots(clips, first, t, 0, F), conv_weight)
-    copies[2].wait()
     adjoint_weight(weight2_copy, back_weight)
-    copies[3].wait()
-    for t in range(F - 2):
+    for f in range(F):
+        cot_shifted[f] = column_pieces(cot_window[f])
+        for a, piece in enumerate(row_pieces(window[f])):
+            frame_t[f, a * C : (a + 1) * C, :] = piece.T
+    for t in range(EDGE):
         back[t] = conv_frame(cot_window, next_slots(clips, first, t, 0, F), back_weight)
+    for t, scale in enumerate(normalize(act.at[2:F], F - 2)):
+        scales[2 + t : 3 + t] = scale
+    for t in range(2, F):
+        value = hidden_of(act[t])
+        hidden[t] = value
+        if t < EDGE:
+            place = slice((t - 2) * POS, (t - 1) * POS)
+            for a, piece in enumerate(row_pieces(value)):
+                hidden_t[a * C : (a + 1) * C, place] = piece.T
+            slots = next_slots(clips, first, t, 0, F)
+            for k in range(3):
+                cot_taps[place, 3 * C * k : 3 * C * (k + 1)] = cot_shifted[slots[2 - k]]
+    second_part[...] = jnp.dot(hidden_t[...], cot_taps[...], preferred_element_type=F32)
+
+
+def split_rows(grads, g, keep_ref, send_ref):
+    own = lax.rem(lax.axis_index("dp"), 2) == 0
+    for m in range(16):
+        low = grads[g, 2 * BLOCK * m : 2 * BLOCK * m + BLOCK]
+        high = grads[g, 2 * BLOCK * m + BLOCK : 2 * BLOCK * (m + 1)]
+        keep_ref[g, m, :BLOCK] = jnp.where(own, low, high)
+        keep_ref[g, m, BLOCK:] = jnp.zeros((PADDED - BLOCK, C), F32)
+        send_ref[g, m, :BLOCK] = jnp.where(own, high, low).astype(BF16)
+        send_ref[g, m, BLOCK:] = jnp.zeros((PADDED - BLOCK, C), BF16)
 
 
 def main_kernel(
@@ -201,6 +244,11 @@
     back_weight,
     act_in,
     back_in,
+    scales,
+    hidden_in,
+    frame_t_in,
+    cot_shifted_in,
+    second_part,
     hidden_ref,
     act_grad_ref,
     keep_ref,
@@ -209,6 +257,7 @@
     cot_window,
     act,
     back,
+    work,
     cot_shifted,
     cot_taps,
     frame_t,
@@ -217,41 +266,44 @@
     grad_shifted,
     grads,
 ):
-    none = F + 2
     first = first_frame()
-    past = [past_slots(clips, first, t, 2, none) for t in range(F)]
-    following = [next_slots(clips, first, t, 0, none) for t in range(F)]
+    zero = jnp.zeros((POS, C), BF16)
     for f in range(2):
         window[f] = tail[2 + f]
-        cot_window[F + f] = head[2 + f]
-    for f in range(F):
         window[2 + f] = frames[f]
-        cot_window[f] = cot[f]
-    window[none] = jnp.zeros((POS, C), BF16)
-    cot_window[none] = jnp.zeros((POS, C), BF16)
-
+        cot_window[f] = cot[EDGE + f]
+        cot_window[2 + f] = head[2 + f]
+    window[4] = zero
+    cot_window[4] = zero
+
+    for t in range(2):
+        act[t] = conv_frame(window, past_slots(clips, first, t, 2, 4), conv_weight)
+        back[t] = conv_frame(
+            cot_window, next_slots(clips, first, EDGE + t, -EDGE, 4), back_weight
+        )
+    for f in range(2):
+        cot_shifted[f] = column_pieces(cot_window[2 + f])
+        for a, piece in enumerate(row_pieces(window[f])):
+            frame_t[f, a * C : (a + 1) * C, :] = piece.T
+    cot_shifted[2] = jnp.zeros((POS, 3 * C), BF16)
+    frame_t[2] = jnp.zeros((3 * C, POS), BF16)
+    scale = normalize(act, 2) + [scales[t : t + 1] for t in range(2, F)]
     for t in range(F):
-        act[t] = conv_frame(window, past[t], conv_weight) if t < 2 else act_in[t]
-        back[t] = back_in[t] if t < F - 2 else conv_frame(cot_window, following[t], back_weight)
-    scale = normalize(act, F)
-    for t in range(F):
-        hidden = (act[t] * gate_of(act[t])).astype(BF16)
-        hidden_ref[t] = hidden
-        for a, piece in enumerate(row_pieces(hidden)):
-            hidden_t[a * C : (a + 1) * C, t * POS : (t + 1) * POS] = piece.T
-    for t, rounded in enumerate(norm_adjoint(act, back, scale, F)):
-        act_grad_ref[t] = rounded
-        grad_shifted[t * POS : (t + 1) * POS] = column_pieces(rounded)
-
-    for f in range(F + 2):
-        cot_shifted[f] = column_pieces(cot_window[f])
-    cot_shifted[none] = jnp.zeros((POS, 3 * C), BF16)
-    for s in range(F):
+        hidden_ref[t] = hidden_of(act[t]) if t < 2 else hidden_in[t]
+
+    for n, s in enumerate((0, 1, EDGE, EDGE + 1)):
+        place = slice(n * POS, (n + 1) * POS)
+        for a, piece in enumerate(row_pieces(hidden_ref[s])):
+            hidden_t[a * C : (a + 1) * C, place] = piece.T
+        near = next_slots(clips, first, s, 0, F)
+        far = next_slots(clips, first, s, -F, 2)
         for k in range(3):
-            cot_taps[s * POS : (s + 1) * POS, 3 * C * k : 3 * C * (k + 1)] = cot_shifted[
-                following[s][2 - k]
-            ]
-    second_grad = jnp.dot(hidden_t[...], cot_taps[...], preferred_element_type=F32)
+            cot_taps[place, 3 * C * k : 3 * C * (k + 1)] = (
+                cot_shifted_in[near[2 - k]] if s + 2 - k < F else cot_shifted[far[2 - k]]
+            )
+    second_grad = second_part[...] + jnp.dot(
+        hidden_t[...], cot_taps[...], preferred_element_type=F32
+    )
     for k in range(3):
         for a in range(3):
             for b in range(3):
@@ -260,13 +312,22 @@
                     a * C : (a + 1) * C, (k * 3 + b) * C : (k * 3 + b + 1) * C
                 ]
 
-    for f in range(F + 2):
-        for a, piece in enumerate(row_pieces(window[f])):
-            frame_t[f, a * C : (a + 1) * C, :] = piece.T
-    frame_t[none] = jnp.zeros((3 * C, POS), BF16)
+    rounded = norm_adjoint(
+        lambda t: act[t] if t < 2 else act_in[t],
+        lambda t: back_in[t] if t < EDGE else back[t - EDGE],
+        scale,
+        work,
+    )
     for t in range(F):
+        act_grad_ref[t] = rounded[t]
+        grad_shifted[t * POS : (t + 1) * POS] = column_pieces(rounded[t])
+        near = past_slots(clips, first, t, 0, F)
+        far = past_slots(clips, first, t, 2, 2)
         for k in range(3):
-            frame_taps[3 * C * k : 3 * C * (k + 1), t * POS : (t + 1) * POS] = frame_t[past[t][k]]
+            frame_taps[3 * C * k : 3 * C * (k + 1), t * POS : (t + 1) * POS] = (
+                frame_t_in[near[k]] if t + k - 2 >= 0 else frame_t[far[k]]
+            )
+    split_rows(grads, 1, keep_ref, send_ref)
     first_grad = jnp.dot(frame_taps[...], grad_shifted[...], preferred_element_type=F32)
     for outer in range(9):
         for b in range(3):
@@ -274,16 +335,7 @@
             grads[0, tap * C : (tap + 1) * C] = first_grad[
                 outer * C : (outer + 1) * C, b * C : (b + 1) * C
             ]
-
-    own = lax.rem(lax.axis_index("dp"), 2) == 0
-    for g in range(2):
-        for m in range(16):
-            low = grads[g, 2 * BLOCK * m : 2 * BLOCK * m + BLOCK]
-            high = grads[g, 2 * BLOCK * m + BLOCK : 2 * BLOCK * (m + 1)]
-            keep_ref[g, m, :BLOCK] = jnp.where(own, low, high)
-            keep_ref[g, m, BLOCK:] = jnp.zeros((PADDED - BLOCK, C), F32)
-            send_ref[g, m, :BLOCK] = jnp.where(own, high, low).astype(BF16)
-            send_ref[g, m, BLOCK:] = jnp.zeros((PADDED - BLOCK, C), BF16)
+    split_rows(grads, 0, keep_ref, send_ref)
 
 
 def forward_kernel(
@@ -297,7 +349,7 @@
         act[t] = conv_frame(window, past_slots(clips, first, t - 2, 4, 4), conv_weight)
     normalize(act, 2)
     for t in range(2):
-        hidden[t] = (act[t] * gate_of(act[t])).astype(BF16)
+        hidden[t] = hidden_of(act[t])
     for f in range(F):
         hidden[2 + f] = hidden_in[f]
     hidden[F + 2] = jnp.zeros((POS, C), BF16)
@@ -323,7 +375,9 @@
         act[t] = conv_frame(window, past_slots(clips, first, F + t, 2 - F, 4), conv_weight)
         back[t] = conv_frame(cot_window, next_slots(clips, first, F + t, -F, 4), back_weight)
     scale = normalize(act, 2)
-    for t, rounded in enumerate(norm_adjoint(act, back, scale, 2)):
+    for t, rounded in enumerate(
+        norm_adjoint(lambda t: act[t], lambda t: back[t], scale, back)
+    ):
         out_ref[t] = rounded
 
 
@@ -472,34 +526,44 @@
             WIDE,
             frame_shape(F, F32),
             frame_shape(F, F32),
+            ((F, C), F32),
+            frame_shape(F),
+            ((F + 1, 3 * C, POS), BF16),
+            ((F + 1, POS, 3 * C), BF16),
+            ((3 * C, 9 * C), F32),
         ],
-        [pltpu.SemaphoreType.DMA((4,))],
-        flops=CONV_FLOPS * 3 // 2,
+        [
+            ((3 * C, 4 * POS), BF16),
+            ((4 * POS, 9 * C), BF16),
+            pltpu.SemaphoreType.DMA((4,)),
+        ],
+        flops=CONV_FLOPS * 2,
         limit=16,
     )
     tail, head, local = lax.optimization_barrier((tail, head, local))
-    frame_copy, cot_copy, weight1, weight2, conv_weight, back_weight, act, back = local
+    frame_copy, cot_copy, weight1, weight2, conv_weight, back_weight, *partial = local
     block = ((2, 16, PADDED, C), F32)
     hidden, act_grad, keep, send = call(
         main_kernel,
-        (clip_ids, frame_copy, cot_copy, tail, head, conv_weight, back_weight, act, back),
-        [SMEM] + [VMEM] * 8,
+        (clip_ids, frame_copy, cot_copy, tail, head, conv_weight, back_weight, *partial),
+        [SMEM] + [VMEM] * 13,
         [frame_shape(F), frame_shape(F), block, (block[0], BF16)],
         [
-            frame_shape(F + 3),
-            frame_shape(F + 3),
+            frame_shape(5),
+            frame_shape(5),
+            frame_shape(2, F32),
+            frame_shape(2, F32),
             frame_shape(F, F32),
-            frame_shape(F, F32),
-            ((F + 3, POS, 3 * C), BF16),
-            ((F * POS, 9 * C), BF16),
-            ((F + 3, 3 * C, POS), BF16),
+            ((3, POS, 3 * C), BF16),
+            ((4 * POS, 9 * C), BF16),
+            ((3, 3 * C, POS), BF16),
             ((9 * C, F * POS), BF16),
-            ((3 * C, F * POS), BF16),
+            ((3 * C, 4 * POS), BF16),
             ((F * POS, 3 * C), BF16),
             ((2, 27 * C, C), F32),
         ],
-        flops=CONV_FLOPS * 5 // 2,
-        limit=40,
+        flops=CONV_FLOPS * 2,
+        limit=32,
     )
     recv = dp_permute(send, lambda d: d ^ 1)
     head, keep = lax.optimization_barrier((head, keep))

time: 65.5 us -> 63.6 us (0.971)
  waiting for transfers between devices: 10.3 us -> 8.58 us
    ppermute x6, waiting for transfers between devices: 6.7 us -> 4.86 us  [seq_permute(): lax.ppermute(value, 'seq', [(source, target(source) % 8) for source in ra...]
  transfers between devices with their start and end apart: 13 -> 13, of which waited for: 5 -> 5; matrix products, arithmetic and copies ran while one was open for 0% -> 0% of each run, Pallas kernels for 29% -> 33%
where the time goes in v5:
time: 63.6 us; the launch traced here: 62.7 us
  Pallas kernels  29.8 us (47%)
  starting transfers between devices  23.6 us (37%)
  waiting for transfers between devices  8.58 us (13%)
  between operations  0.71 us (1%)
    pallas_call x11, Pallas kernels, call(): pl.pallas_call(kernel, out_shape=[jax.ShapeDtypeStruct(shape, dtype) for...  29.8 us
    ppermute x6, starting transfers between devices, seq_permute(): lax.ppermute(value, 'seq', [(source, target(source) % 8) for source in ra...  12.6 us
    ppermute x7, starting transfers between devices, dp_permute(): lax.ppermute(value, 'dp', [(source, target(source)) for source in range(3...  11 us
    ppermute x6, waiting for transfers between devices, seq_permute(): lax.ppermute(value, 'seq', [(source, target(source) % 8) for source in ra...  4.86 us
    ppermute x7, waiting for transfers between devices, dp_permute(): lax.ppermute(value, 'dp', [(source, target(source)) for source in range(3...  3.72 us
  transfers between devices with their start and end apart: 13, of which 5 were waited for; matrix products, arithmetic and copies ran while one was open for 0% of the time, Pallas kernels for 33%

profile of v5, /device:TPU:2, one launch (start us, length us, event | category | flops | bytes accessed | tf_op | source)
XLA Modules:
  0.0 62.7 jit_solution(813220893609169668)
XLA Ops:
  0.6 1.1 %shard_map.84 = (s32[1,64]{1,0:T(1,128)S(1)}, bf16[4,256,128]{2,1,0:T(8,128)(2,1)S(1)}, bf16[6,256,128]{2,1,0:T(8,128)(2,1)S(1)}) custom-call(s32[1,64]{1,0:T(1,128)} %clips.1, bf16[8,256,128]{2,1,0:T(8,128)(2,1)} %bitcast.4, bf16[8,256,128]{2,1,0:T(8,128)(2,1)} %bitcast.6), custom_call_target="tpu_custom_call" | custom-call | bytes 1048576 | tf_op jit(solution)/shard_map/pallas_call | solution.py:455
  1.8 5.9 %collective-permute-start.1 = (bf16[6,256,128]{2,1,0:T(8,128)(2,1)S(1)}, bf16[6,256,128]{2,1,0:T(8,128)(2,1)S(1)}, u32[]{:S(2)}, u32[]{:S(2)}) collective-permute-start(bf16[6,256,128]{2,1,0:T(8,128)(2,1)S(1)} %get-tuple-element.68), channel_id=1, source_target_pairs={{0,224},{32,0},{64,32},{96,64},{128,96},{160,128},{192,160},{224,1... | collective-permute-start | bytes 1179656 | tf_op jit(solution)/shard_map/ppermute | solution.py:497
  7.7 0.0 collective-permute-start
  7.7 8.3 %shard_map.85 = (bf16[9,256,128]{2,1,0:T(8,128)(2,1)S(1)}, bf16[9,256,128]{2,1,0:T(8,128)(2,1)S(1)}, bf16[3456,128]{1,0:T(8,128)(2,1)S(1)}, bf16[3456,128]{1,0:T...) custom-call(s32[1,64]{1,0:T(1,128)S(1)} %get-tuple-element.69.clips,, ...), custom_call_target="tpu_custom_call" | custom-call | flops 3623878656 | bytes 1048576 | tf_op jit(solution)/shard_map/pallas_call | solution.py:455
  16.0 0.7 %collective-permute-done.tail = bf16[4,256,128]{2,1,0:T(8,128)(2,1)S(1)} collective-permute-done((bf16[4,256,128]{2,1,0:T(8,128)(2,1)S(1)}, bf16[4,256,128]{2,1,0:T(8,128)(2,1)S(1)}, u32[]{:S(2)}, u32[]{:S(2)}) %collective-permute-start) | collective-permute-done | bytes 262176 | tf_op jit(solution)/shard_map/ppermute | solution.py:497
  16.7 0.0 collective-permute-done.1.head
  16.7 7.2 %shard_map.86 = (bf16[8,256,128]{2,1,0:T(8,128)(2,1)S(1)}, bf16[8,256,128]{2,1,0:T(8,128)(2,1)S(1)}, f32[2,16,112,128]{3,2,1,0:T(8,128)S(1)}, bf16[2,16,112,128]{3,2,1,0:T(8,128)(2,1)S(1)}) custom-call(s32[1,64]{1,0:T(1,128)S(1)} %get-tuple-element.69.clips, bf16[9,256,128]{2,1,0:T(8,128)(2,1)S(1)} %get-tuple-element.84.frames, ...), custom_call_target="tpu_custom_call" | custom-call | flops 3623878656 | bytes 1048576 | tf_op jit(solution)/shard_map/pallas_call | solution.py:455
  23.9 0.3 collective-permute-start.2
  24.2 2.4 %shard_map.87.next_in = bf16[2,256,128]{2,1,0:T(8,128)(2,1)S(1)} custom-call(s32[1,64]{1,0:T(1,128)S(1)} %get-tuple-element.69.clips, bf16[9,256,128]{2,1,0:T(8,128)(2,1)S(1)} %get-tuple-element.84.frames, bf16[6,256,128]{2,1,0:T(8,128)(2,1)S(1)} %collective-permute-done.1.head, bf16[1152,384]{1,0:T(8,128)(2,1)S(1)} %get-tuple-element.87.conv_weight, ...), custom_call_target="tpu_custom_call" | custom-call | flops 905969664 | bytes 1048576 | tf_op jit(solution)/shard_map/pallas_call | solution.py:455
  26.7 0.0 collective-permute-done.2.part
  26.7 0.2 shard_map.88
  26.9 1.6 %collective-permute-start.3 = (bf16[2,4,112,128]{3,2,1,0:T(8,128)(2,1)S(1)}, bf16[2,4,112,128]{3,2,1,0:T(8,128)(2,1)S(1)}, u32[]{:S(2)}, u32[]{:S(2)}) collective-permute-start(bf16[2,4,112,128]{3,2,1,0:T(8,128)(2,1)S(1)} %get-tuple-element.105), channel_id=1, source_target_pairs={{0,2},{1,9},{2,4},{3,11},{4,6},{5,13},{6,0},{7,15},{8,10},{9,17},{... | collective-permute-start | bytes 688136 | tf_op jit(solution)/shard_map/ppermute | solution.py:481
  28.4 1.1 %collective-permute-start.4 = (bf16[2,4,112,128]{3,2,1,0:T(8,128)(2,1)S(1)}, bf16[2,4,112,128]{3,2,1,0:T(8,128)(2,1)S(1)}, u32[]{:S(2)}, u32[]{:S(2)}) collective-permute-start(bf16[2,4,112,128]{3,2,1,0:T(8,128)(2,1)S(1)} %get-tuple-element.106), channel_id=1, source_target_pairs={{0,4},{1,17},{2,6},{3,19},{4,0},{5,21},{6,2},{7,23},{8,12},{9,25},... | collective-permute-start | bytes 688136 | tf_op jit(solution)/shard_map/ppermute | solution.py:481
  29.5 2.2 %collective-permute-start.5 = (bf16[2,4,112,128]{3,2,1,0:T(8,128)(2,1)S(1)}, bf16[2,4,112,128]{3,2,1,0:T(8,128)(2,1)S(1)}, u32[]{:S(2)}, u32[]{:S(2)}) collective-permute-start(bf16[2,4,112,128]{3,2,1,0:T(8,128)(2,1)S(1)} %get-tuple-element.107), channel_id=1, source_target_pairs={{0,6},{1,25},{2,0},{3,27},{4,2},{5,29},{6,4},{7,31},{8,14},{9,1},{... | collective-permute-start | bytes 688136 | tf_op jit(solution)/shard_map/ppermute | solution.py:481
  31.7 5.4 %shard_map.89 = bf16[8,256,128]{2,1,0:T(8,128)(2,1)} custom-call(s32[1,64]{1,0:T(1,128)S(1)} %get-tuple-element.69.clips, bf16[8,256,128]{2,1,0:T(8,128)(2,1)S(1)} %get-tuple-element.108.hidden_in, bf16[9,256,128]{2,1,0:T(8,128)(2,1)S(1)} %get-tuple-element.84.frames, bf16[4,256,128]{2,1,0:T(8,128)(2,1)S(1)} %collective-permute-done.tail, ...), custom_call_target="tpu_custom_call" | custom-call | flops 2264924160 | bytes 1048576 | tf_op jit(solution)/shard_map/pallas_call | solution.py:455
  37.1 0.0 collective-permute-done.3.refs_0_
  37.1 0.0 collective-permute-done.4.refs_1_
  37.1 0.9 %collective-permute-done.5.refs_2_ = bf16[2,4,112,128]{3,2,1,0:T(8,128)(2,1)S(1)} collective-permute-done((bf16[2,4,112,128]{3,2,1,0:T(8,128)(2,1)S(1)}, bf16[2,4,112,128]{3,2,1,0:T(8,128)(2,1)S(1)}, u32[]{:S(2)}, u32[]{:S(2)}) %collective-permute-start.5) | collective-permute-done | bytes 229408 | tf_op jit(solution)/shard_map/ppermute | solution.py:481
  38.0 0.1 shard_map.90
  38.1 1.7 %collective-permute-start.6 = (bf16[2,112,128]{2,1,0:T(8,128)(2,1)S(1)}, bf16[2,112,128]{2,1,0:T(8,128)(2,1)S(1)}, u32[]{:S(2)}, u32[]{:S(2)}) collective-permute-start(bf16[2,112,128]{2,1,0:T(8,128)(2,1)S(1)} %get-tuple-element.116), channel_id=1, source_target_pairs={{0,8},{1,3},{2,10},{3,5},{4,12},{5,7},{6,14},{7,1},{8,16},{9,11},{... | collective-permute-start | bytes 172040 | tf_op jit(solution)/shard_map/ppermute | solution.py:481
  39.8 2.9 %collective-permute-start.7 = (bf16[2,112,128]{2,1,0:T(8,128)(2,1)S(1)}, bf16[2,112,128]{2,1,0:T(8,128)(2,1)S(1)}, u32[]{:S(2)}, u32[]{:S(2)}) collective-permute-start(bf16[2,112,128]{2,1,0:T(8,128)(2,1)S(1)} %get-tuple-element.117), channel_id=1, source_target_pairs={{0,16},{1,5},{2,18},{3,7},{4,20},{5,1},{6,22},{7,3},{8,24},{9,13},... | collective-permute-start | bytes 172040 | tf_op jit(solution)/shard_map/ppermute | solution.py:481
  42.7 1.4 %collective-permute-start.8 = (bf16[2,112,128]{2,1,0:T(8,128)(2,1)S(1)}, bf16[2,112,128]{2,1,0:T(8,128)(2,1)S(1)}, u32[]{:S(2)}, u32[]{:S(2)}) collective-permute-start(bf16[2,112,128]{2,1,0:T(8,128)(2,1)S(1)} %get-tuple-element.118), channel_id=1, source_target_pairs={{0,24},{1,7},{2,26},{3,1},{4,28},{5,3},{6,30},{7,5},{8,0},{9,15},{... | collective-permute-start | bytes 172040 | tf_op jit(solution)/shard_map/ppermute | solution.py:481
  44.1 0.0 collective-permute-done.6.refs_0_
  44.1 1.4 %collective-permute-done.7.refs_1_ = bf16[2,112,128]{2,1,0:T(8,128)(2,1)S(1)} collective-permute-done((bf16[2,112,128]{2,1,0:T(8,128)(2,1)S(1)}, bf16[2,112,128]{2,1,0:T(8,128)(2,1)S(1)}, u32[]{:S(2)}, u32[]{:S(2)}) %collective-permute-start.7) | collective-permute-done | bytes 57376 | tf_op jit(solution)/shard_map/ppermute | solution.py:481
  45.5 1.4 %collective-permute-done.8.refs_2_ = bf16[2,112,128]{2,1,0:T(8,128)(2,1)S(1)} collective-permute-done((bf16[2,112,128]{2,1,0:T(8,128)(2,1)S(1)}, bf16[2,112,128]{2,1,0:T(8,128)(2,1)S(1)}, u32[]{:S(2)}, u32[]{:S(2)}) %collective-permute-start.8) | collective-permute-done | bytes 57376 | tf_op jit(solution)/shard_map/ppermute | solution.py:481
  46.9 0.1 collective-permute-start.9
  47.0 4.2 %collective-permute-done.9.refs_0_ = bf16[2,112,128]{2,1,0:T(8,128)(2,1)S(1)} collective-permute-done((bf16[2,112,128]{2,1,0:T(8,128)(2,1)S(1)}, bf16[2,112,128]{2,1,0:T(8,128)(2,1)S(1)}, u32[]{:S(2)}, u32[]{:S(2)}) %collective-permute-start.9) | collective-permute-done | bytes 57376 | tf_op jit(solution)/shard_map/ppermute | solution.py:497
  51.2 2.9 %collective-permute-start.12 = (bf16[2,112,128]{2,1,0:T(8,128)(2,1)S(1)}, bf16[2,112,128]{2,1,0:T(8,128)(2,1)S(1)}, u32[]{:S(2)}, u32[]{:S(2)}) collective-permute-start(bf16[2,112,128]{2,1,0:T(8,128)(2,1)S(1)} %shard_map.92.refs_0_), channel_id=1, source_target_pairs={{0,160},{32,128},{64,224},{96,192},{128,32},{160,0},{192,96},{224,... | collective-permute-start | bytes 172040 | tf_op jit(solution)/shard_map/ppermute | solution.py:497
  54.1 1.9 %collective-permute-start.11 = (bf16[2,112,128]{2,1,0:T(8,128)(2,1)S(1)}, bf16[2,112,128]{2,1,0:T(8,128)(2,1)S(1)}, u32[]{:S(2)}, u32[]{:S(2)}) collective-permute-start(bf16[2,112,128]{2,1,0:T(8,128)(2,1)S(1)} %shard_map.92.refs_0_), channel_id=1, source_target_pairs={{0,192},{32,96},{64,0},{96,160},{128,64},{160,224},{192,128},{224,... | collective-permute-start | bytes 172040 | tf_op jit(solution)/shard_map/ppermute | solution.py:497
  56.0 1.7 %collective-permute-start.10 = (bf16[2,112,128]{2,1,0:T(8,128)(2,1)S(1)}, bf16[2,112,128]{2,1,0:T(8,128)(2,1)S(1)}, u32[]{:S(2)}, u32[]{:S(2)}) collective-permute-start(bf16[2,112,128]{2,1,0:T(8,128)(2,1)S(1)} %shard_map.92.refs_0_), channel_id=1, source_target_pairs={{0,224},{32,64},{64,32},{96,128},{128,96},{160,192},{192,160},{224... | collective-permute-start | bytes 172040 | tf_op jit(solution)/shard_map/ppermute | solution.py:497
  57.7 4.3 %shard_map.93 = bf16[8,256,128]{2,1,0:T(8,128)(2,1)} custom-call(s32[1,64]{1,0:T(1,128)S(1)} %get-tuple-element.69.clips, bf16[8,256,128]{2,1,0:T(8,128)(2,1)S(1)} %get-tuple-element.121.act_grad_in, bf16[2,256,128]{2,1,0:T(8,128)(2,1)S(1)} %shard_map.87.next_in, bf16[9,256,128]{2,1,0:T(8,128)(2,1)S(1)} %get-tuple-element.85.cot, ...), custom_call_target="tpu_custom_call" | custom-call | flops 1811939328 | bytes 1048576 | tf_op jit(solution)/shard_map/pallas_call | solution.py:455
  62.0 0.0 collective-permute-done.12.refs_3_
  62.0 0.0 collective-permute-done.11.refs_2_
  62.0 0.0 collective-permute-done.10.refs_1_
  62.0 0.7 %shard_map.94 = (f32[108,128]{1,0:T(8,128)}, f32[108,128]{1,0:T(8,128)}) custom-call(bf16[2,112,128]{2,1,0:T(8,128)(2,1)S(1)} %shard_map.92.refs_0_, bf16[2,112,128]{2,1,0:T(8,128)(2,1)S(1)} %collective-permute-done.10.refs_1_, bf16[2,112,128]{2,1,0:T(8,128)(2,1)S(1)} %collective-permute-done.11.refs_2_, bf16[2,112,128]{2,1,0:T(8,128)(2,1)S(1)} %collective-permute-done.12.refs_3_), custom_call_target="tpu_custom_call" | custom-call | bytes 1048576 | tf_op jit(solution)/shard_map/pallas_call | solution.py:455
  (2 shorter events, 0.0 us)
Async XLA Ops:
  1.8 14.9 %collective-permute-start.1 = (bf16[6,256,128]{2,1,0:T(8,128)(2,1)S(1)}, bf16[6,256,128]{2,1,0:T(8,128)(2,1)S(1)}, u32[]{:S(2)}, u32[]{:S(2)}) collective-permute-start(bf16[6,256,128]{2,1,0:T(8,128)(2,1)S(1)} %get-tuple-element.68), channel_id=1, source_target_pairs={{0,224},{32,0},{64,32},{96,64},{128,96},{160,128},{192,160},{224,1... | collective-permute-start | bytes 1179656 | tf_op jit(solution)/shard_map/ppermute | solution.py:497
  7.7 9.0 %collective-permute-start = (bf16[4,256,128]{2,1,0:T(8,128)(2,1)S(1)}, bf16[4,256,128]{2,1,0:T(8,128)(2,1)S(1)}, u32[]{:S(2)}, u32[]{:S(2)}) collective-permute-start(bf16[4,256,128]{2,1,0:T(8,128)(2,1)S(1)} %get-tuple-element.67), channel_id=1, source_target_pairs={{0,32},{32,64},{64,96},{96,128},{128,160},{160,192},{192,224},{224... | collective-permute-start | bytes 786440 | tf_op jit(solution)/shard_map/ppermute | solution.py:497
  23.9 2.7 %collective-permute-start.2 = (bf16[2,16,112,128]{3,2,1,0:T(8,128)(2,1)S(1)}, bf16[2,16,112,128]{3,2,1,0:T(8,128)(2,1)S(1)}, u32[]{:S(2)}, u32[]{:S(2)}) collective-permute-start(bf16[2,16,112,128]{3,2,1,0:T(8,128)(2,1)S(1)} %get-tuple-element.98), channel_id=1, source_target_pairs={{0,1},{1,0},{2,3},{3,2},{4,5},{5,4},{6,7},{7,6},{8,9},{9,8},{10,11... | collective-permute-start | bytes 2752520 | tf_op jit(solution)/shard_map/ppermute | solution.py:481
  26.9 10.3 %collective-permute-start.3 = (bf16[2,4,112,128]{3,2,1,0:T(8,128)(2,1)S(1)}, bf16[2,4,112,128]{3,2,1,0:T(8,128)(2,1)S(1)}, u32[]{:S(2)}, u32[]{:S(2)}) collective-permute-start(bf16[2,4,112,128]{3,2,1,0:T(8,128)(2,1)S(1)} %get-tuple-element.105), channel_id=1, source_target_pairs={{0,2},{1,9},{2,4},{3,11},{4,6},{5,13},{6,0},{7,15},{8,10},{9,17},{... | collective-permute-start | bytes 688136 | tf_op jit(solution)/shard_map/ppermute | solution.py:481
  28.4 8.7 %collective-permute-start.4 = (bf16[2,4,112,128]{3,2,1,0:T(8,128)(2,1)S(1)}, bf16[2,4,112,128]{3,2,1,0:T(8,128)(2,1)S(1)}, u32[]{:S(2)}, u32[]{:S(2)}) collective-permute-start(bf16[2,4,112,128]{3,2,1,0:T(8,128)(2,1)S(1)} %get-tuple-element.106), channel_id=1, source_target_pairs={{0,4},{1,17},{2,6},{3,19},{4,0},{5,21},{6,2},{7,23},{8,12},{9,25},... | collective-permute-start | bytes 688136 | tf_op jit(solution)/shard_map/ppermute | solution.py:481
  29.5 8.5 %collective-permute-start.5 = (bf16[2,4,112,128]{3,2,1,0:T(8,128)(2,1)S(1)}, bf16[2,4,112,128]{3,2,1,0:T(8,128)(2,1)S(1)}, u32[]{:S(2)}, u32[]{:S(2)}) collective-permute-start(bf16[2,4,112,128]{3,2,1,0:T(8,128)(2,1)S(1)} %get-tuple-element.107), channel_id=1, source_target_pairs={{0,6},{1,25},{2,0},{3,27},{4,2},{5,29},{6,4},{7,31},{8,14},{9,1},{... | collective-permute-start | bytes 688136 | tf_op jit(solution)/shard_map/ppermute | solution.py:481
  38.1 5.9 %collective-permute-start.6 = (bf16[2,112,128]{2,1,0:T(8,128)(2,1)S(1)}, bf16[2,112,128]{2,1,0:T(8,128)(2,1)S(1)}, u32[]{:S(2)}, u32[]{:S(2)}) collective-permute-start(bf16[2,112,128]{2,1,0:T(8,128)(2,1)S(1)} %get-tuple-element.116), channel_id=1, source_target_pairs={{0,8},{1,3},{2,10},{3,5},{4,12},{5,7},{6,14},{7,1},{8,16},{9,11},{... | collective-permute-start | bytes 172040 | tf_op jit(solution)/shard_map/ppermute | solution.py:481
  39.8 5.7 %collective-permute-start.7 = (bf16[2,112,128]{2,1,0:T(8,128)(2,1)S(1)}, bf16[2,112,128]{2,1,0:T(8,128)(2,1)S(1)}, u32[]{:S(2)}, u32[]{:S(2)}) collective-permute-start(bf16[2,112,128]{2,1,0:T(8,128)(2,1)S(1)} %get-tuple-element.117), channel_id=1, source_target_pairs={{0,16},{1,5},{2,18},{3,7},{4,20},{5,1},{6,22},{7,3},{8,24},{9,13},... | collective-permute-start | bytes 172040 | tf_op jit(solution)/shard_map/ppermute | solution.py:481
  42.7 4.2 %collective-permute-start.8 = (bf16[2,112,128]{2,1,0:T(8,128)(2,1)S(1)}, bf16[2,112,128]{2,1,0:T(8,128)(2,1)S(1)}, u32[]{:S(2)}, u32[]{:S(2)}) collective-permute-start(bf16[2,112,128]{2,1,0:T(8,128)(2,1)S(1)} %get-tuple-element.118), channel_id=1, source_target_pairs={{0,24},{1,7},{2,26},{3,1},{4,28},{5,3},{6,30},{7,5},{8,0},{9,15},{... | collective-permute-start | bytes 172040 | tf_op jit(solution)/shard_map/ppermute | solution.py:481
  46.9 4.3 %collective-permute-start.9 = (bf16[2,112,128]{2,1,0:T(8,128)(2,1)S(1)}, bf16[2,112,128]{2,1,0:T(8,128)(2,1)S(1)}, u32[]{:S(2)}, u32[]{:S(2)}) collective-permute-start(bf16[2,112,128]{2,1,0:T(8,128)(2,1)S(1)} %shard_map.91.keep_ref), channel_id=1, source_target_pairs={{0,32},{32,0},{64,96},{96,64},{128,160},{160,128},{192,224},{224,1... | collective-permute-start | bytes 172040 | tf_op jit(solution)/shard_map/ppermute | solution.py:497
  51.2 10.8 %collective-permute-start.12 = (bf16[2,112,128]{2,1,0:T(8,128)(2,1)S(1)}, bf16[2,112,128]{2,1,0:T(8,128)(2,1)S(1)}, u32[]{:S(2)}, u32[]{:S(2)}) collective-permute-start(bf16[2,112,128]{2,1,0:T(8,128)(2,1)S(1)} %shard_map.92.refs_0_), channel_id=1, source_target_pairs={{0,160},{32,128},{64,224},{96,192},{128,32},{160,0},{192,96},{224,... | collective-permute-start | bytes 172040 | tf_op jit(solution)/shard_map/ppermute | solution.py:497
  54.1 7.9 %collective-permute-start.11 = (bf16[2,112,128]{2,1,0:T(8,128)(2,1)S(1)}, bf16[2,112,128]{2,1,0:T(8,128)(2,1)S(1)}, u32[]{:S(2)}, u32[]{:S(2)}) collective-permute-start(bf16[2,112,128]{2,1,0:T(8,128)(2,1)S(1)} %shard_map.92.refs_0_), channel_id=1, source_target_pairs={{0,192},{32,96},{64,0},{96,160},{128,64},{160,224},{192,128},{224,... | collective-permute-start | bytes 172040 | tf_op jit(solution)/shard_map/ppermute | solution.py:497
  56.0 6.0 %collective-permute-start.10 = (bf16[2,112,128]{2,1,0:T(8,128)(2,1)S(1)}, bf16[2,112,128]{2,1,0:T(8,128)(2,1)S(1)}, u32[]{:S(2)}, u32[]{:S(2)}) collective-permute-start(bf16[2,112,128]{2,1,0:T(8,128)(2,1)S(1)} %shard_map.92.refs_0_), channel_id=1, source_target_pairs={{0,224},{32,64},{64,32},{96,128},{128,96},{160,192},{192,160},{224... | collective-permute-start | bytes 172040 | tf_op jit(solution)/shard_map/ppermute | solution.py:497

commit v6 on v5

--- a/solution.py
+++ b/solution.py
@@ -143,8 +143,9 @@
     return lax.axis_index("seq") * F
 
 
-def halo_kernel(clips, frames, cot, clips_copy, tail, head, sems):
+def halo_kernel(clips, frames, cot, weight1, clips_copy, tail, head, weight1_copy, sems):
     copies = [
+        pltpu.make_async_copy(weight1, weight1_copy, sems.at[4]),
         pltpu.make_async_copy(clips, clips_copy, sems.at[3]),
         pltpu.make_async_copy(frames.at[F - 4 :], tail, sems.at[0]),
         pltpu.make_async_copy(frames.at[:2], head.at[:2], sems.at[1]),
@@ -167,7 +168,6 @@
     weight2,
     window,
     cot_window,
-    weight1_copy,
     weight2_copy,
     conv_weight,
     back_weight,
@@ -183,10 +183,9 @@
     sems,
 ):
     copies = [
-        pltpu.make_async_copy(weight1, weight1_copy, sems.at[0]),
-        pltpu.make_async_copy(frames, window.at[:F], sems.at[1]),
-        pltpu.make_async_copy(weight2, weight2_copy, sems.at[2]),
-        pltpu.make_async_copy(cot, cot_window.at[:F], sems.at[3]),
+        pltpu.make_async_copy(frames, window.at[:F], sems.at[0]),
+        pltpu.make_async_copy(weight2, weight2_copy, sems.at[1]),
+        pltpu.make_async_copy(cot, cot_window.at[:F], sems.at[2]),
     ]
     for copy in copies:
         copy.start()
@@ -195,9 +194,8 @@
     frame_t[F] = jnp.zeros((3 * C, POS), BF16)
     cot_shifted[F] = jnp.zeros((POS, 3 * C), BF16)
     first = first_frame()
-    copies[0].wait()
-    forward_weight(weight1_copy, conv_weight)
-    for copy in copies[1:]:
+    forward_weight(weight1, conv_weight)
+    for copy in copies:
         copy.wait()
     for t in range(2, F):
         act[t] = conv_frame(window, past_slots(clips, first, t, 0, F), conv_weight)
@@ -338,25 +336,46 @@
     split_rows(grads, 0, keep_ref, send_ref)
 
 
+HALF = F // 2
+
+
+def residual_frames(clips, frames, hidden, weight, out_ref, start):
+    first = first_frame()
+    for t in range(HALF):
+        slots = past_slots(clips, first, start + t, 2 - start, HALF + 2)
+        out = conv_frame(hidden, slots, weight)
+        out_ref[start + t] = (frames[start + t].astype(F32) + out).astype(BF16)
+
+
+def fill(window, parts):
+    count = 0
+    for part in parts:
+        for f in range(part.shape[0]):
+            window[count] = part[f]
+            count += 1
+    window[count] = jnp.zeros((POS, C), BF16)
+
+
 def forward_kernel(
-    clips, hidden_in, frames, tail, conv_weight, weight2, out_ref, window, act, hidden, weight
+    clips, hidden_in, frames, tail, conv_weight, weight2, out_ref, weight, window, act, hidden
 ):
     first = first_frame()
-    for f in range(4):
-        window[f] = tail[f]
-    window[4] = jnp.zeros((POS, C), BF16)
+    fill(window, [tail])
     for t in range(2):
         act[t] = conv_frame(window, past_slots(clips, first, t - 2, 4, 4), conv_weight)
     normalize(act, 2)
     for t in range(2):
         hidden[t] = hidden_of(act[t])
-    for f in range(F):
-        hidden[2 + f] = hidden_in[f]
-    hidden[F + 2] = jnp.zeros((POS, C), BF16)
+    fill(hidden.at[2:], [hidden_in.at[:HALF]])
     forward_weight(weight2, weight)
-    for t in range(F):
-        out = conv_frame(hidden, past_slots(clips, first, t, 2, F + 2), weight)
-        out_ref[t] = (frames[t].astype(F32) + out).astype(BF16)
+    residual_frames(clips, frames, hidden, weight, out_ref, 0)
+
+
+def rest_kernel(clips, hidden_in, frames, weight, half, out_ref, hidden):
+    fill(hidden, [hidden_in.at[HALF - 2 :]])
+    for t in range(HALF):
+        out_ref[t] = half[t]
+    residual_frames(clips, frames, hidden, weight, out_ref, HALF)
 
 
 def next_grad_kernel(
@@ -394,6 +413,9 @@
         out_ref[t] = (cot[t].astype(F32) + out).astype(BF16)
 
 
+STEPS = (2, 1, 3)
+
+
 def place():
     index = lax.axis_index("dp")
     return lax.div(index, 8), lax.rem(lax.div(index, 2), 4), lax.rem(index, 2) == 0
@@ -403,7 +425,7 @@
     y, x, along_x = place()
     for g in range(2):
         for other in range(4):
-            for step in range(4):
+            for n, step in enumerate((0, *STEPS)):
                 block = jnp.where(
                     along_x, 4 * other + lax.rem(x + step, 4), 4 * lax.rem(y + step, 4) + other
                 )
@@ -411,7 +433,7 @@
                 if step == 0:
                     kept_ref[g, other] = total
                 else:
-                    sent_refs[step - 1][g, other] = total.astype(BF16)
+                    sent_refs[n - 1][g, other] = total.astype(BF16)
 
 
 def second_kernel(keep_ref, *refs):
@@ -419,7 +441,7 @@
     y, x, along_x = place()
     own = jnp.where(along_x, y, x)
     for g in range(2):
-        for step in range(4):
+        for n, step in enumerate((0, *STEPS)):
             block = lax.rem(own + step, 4)
             total = keep_ref[g, block]
             for part in received:
@@ -427,7 +449,7 @@
             if step == 0:
                 kept_ref[g] = total
             else:
-                sent_refs[step - 1][g] = total.astype(BF16)
+                sent_refs[n - 1][g] = total.astype(BF16)
 
 
 def sum_kernel(keep_ref, *refs):
@@ -504,23 +526,22 @@
         pltpu.with_memory_space_constraint(value, pltpu.HBM)
         for value in (clip_ids, own_frames, own_cot, conv1_weight, conv2_weight)
     )
-    clip_ids, tail, head = call(
+    clip_ids, tail, head, weight1 = call(
         halo_kernel,
-        (clip_ids, own_frames, own_cot),
-        [HBM, HBM, HBM],
-        [(clip_ids.shape, jnp.int32), frame_shape(4), frame_shape(6)],
-        [pltpu.SemaphoreType.DMA((4,))],
+        (clip_ids, own_frames, own_cot, conv1_weight),
+        [HBM] * 4,
+        [(clip_ids.shape, jnp.int32), frame_shape(4), frame_shape(6), ((27 * C, C), BF16)],
+        [pltpu.SemaphoreType.DMA((5,))],
     )
     head = shifted(head, -1)
     tail = shifted(tail, 1)
     local = call(
         local_kernel,
-        (clip_ids, own_frames, own_cot, conv1_weight, conv2_weight),
-        [SMEM, HBM, HBM, HBM, HBM],
+        (clip_ids, own_frames, own_cot, weight1, conv2_weight),
+        [SMEM, HBM, HBM, VMEM, HBM],
         [
             frame_shape(F + 1),
             frame_shape(F + 1),
-            ((27 * C, C), BF16),
             ((27 * C, C), BF16),
             WIDE,
             WIDE,
@@ -535,13 +556,13 @@
         [
             ((3 * C, 4 * POS), BF16),
             ((4 * POS, 9 * C), BF16),
-            pltpu.SemaphoreType.DMA((4,)),
+            pltpu.SemaphoreType.DMA((3,)),
         ],
         flops=CONV_FLOPS * 2,
         limit=16,
     )
     tail, head, local = lax.optimization_barrier((tail, head, local))
-    frame_copy, cot_copy, weight1, weight2, conv_weight, back_weight, *partial = local
+    frame_copy, cot_copy, weight2, conv_weight, back_weight, *partial = local
     block = ((2, 16, PADDED, C), F32)
     hidden, act_grad, keep, send = call(
         main_kernel,
@@ -585,25 +606,36 @@
     )
     sent, hidden = lax.optimization_barrier((sent, hidden))
     recv = [
-        dp_permute(part, crossed(along_x(s), along_y(s))) for s, part in zip((1, 2, 3), sent)
+        dp_permute(part, crossed(along_x(s), along_y(s))) for s, part in zip(STEPS, sent)
     ]
-    (block_out,) = call(
+    half_out, wide_weight = call(
         forward_kernel,
         (clip_ids, hidden, frame_copy, tail, conv_weight, weight2),
         [SMEM] + [VMEM] * 5,
-        [frame_shape(F)],
-        [frame_shape(5), frame_shape(2, F32), frame_shape(F + 3), WIDE],
-        flops=CONV_FLOPS * 5 // 4,
+        [frame_shape(HALF), WIDE],
+        [frame_shape(5), frame_shape(2, F32), frame_shape(HALF + 3)],
+        flops=CONV_FLOPS * 3 // 4,
         limit=12,
     )
-    recv, block_out = lax.optimization_barrier((recv, block_out))
+    recv, half_out = lax.optimization_barrier((recv, half_out))
     pair = (2, PADDED, C)
     keep, *sent = call(
         second_kernel, (keep, *recv), [VMEM] * 4, [(pair, F32)] + [(pair, BF16)] * 3
     )
+    sent, half_out = lax.optimization_barrier((sent, half_out))
     recv = [
-        dp_permute(part, crossed(along_y(s), along_x(s))) for s, part in zip((1, 2, 3), sent)
+        dp_permute(part, crossed(along_y(s), along_x(s))) for s, part in zip(STEPS, sent)
     ]
+    (block_out,) = call(
+        rest_kernel,
+        (clip_ids, hidden, frame_copy, wide_weight, half_out),
+        [SMEM] + [VMEM] * 4,
+        [frame_shape(F)],
+        [frame_shape(HALF + 3)],
+        flops=CONV_FLOPS // 2,
+        limit=8,
+    )
+    recv, block_out = lax.optimization_barrier((recv, block_out))
     (total,) = call(sum_kernel, (keep, *recv), [VMEM] * 4, [(pair, BF16)])
     other = seq_permute(total, lambda z: z ^ 1)
     (total,) = call(sum_kernel, (total, other), [VMEM] * 2, [(pair, BF16)])

time: 63.6 us -> 63.3 us (level)
  waiting for transfers between devices: 8.58 us -> 7.77 us
  Pallas kernels: 29.8 us -> 30.5 us
    ppermute x7, waiting for transfers between devices: 3.72 us -> 2.61 us  [dp_permute(): lax.ppermute(value, 'dp', [(source, target(source)) for source in range(3...]
    pallas_call x11 -> x12, Pallas kernels: 29.8 us -> 30.5 us  [call(): pl.pallas_call(kernel, out_shape=[jax.ShapeDtypeStruct(shape, dtype) for...]
  transfers between devices with their start and end apart: 13 -> 13, of which waited for: 5 -> 4; matrix products, arithmetic and copies ran while one was open for 0% -> 0% of each run, Pallas kernels for 33% -> 33%
where the time goes in v6:
time: 63.3 us; the launch traced here: 62.5 us
  Pallas kernels  30.5 us (48%)
  starting transfers between devices  23.6 us (37%)
  waiting for transfers between devices  7.77 us (12%)
  between operations  0.72 us (1%)
    pallas_call x12, Pallas kernels, call(): pl.pallas_call(kernel, out_shape=[jax.ShapeDtypeStruct(shape, dtype) for...  30.5 us
    ppermute x6, starting transfers between devices, seq_permute(): lax.ppermute(value, 'seq', [(source, target(source) % 8) for source in ra...  12.6 us
    ppermute x7, starting transfers between devices, dp_permute(): lax.ppermute(value, 'dp', [(source, target(source)) for source in range(3...  11 us
    ppermute x6, waiting for transfers between devices, seq_permute(): lax.ppermute(value, 'seq', [(source, target(source) % 8) for source in ra...  5.15 us
    ppermute x7, waiting for transfers between devices, dp_permute(): lax.ppermute(value, 'dp', [(source, target(source)) for source in range(3...  2.61 us
  transfers between devices with their start and end apart: 13, of which 4 were waited for; matrix products, arithmetic and copies ran while one was open for 0% of the time, Pallas kernels for 33%

profile of v6, /device:TPU:2, one launch (start us, length us, event | category | flops | bytes accessed | tf_op | source)
XLA Modules:
  0.0 62.5 jit_solution(81902551764720731)
XLA Ops:
  0.6 1.4 %shard_map.84 = (s32[1,64]{1,0:T(1,128)S(1)}, bf16[4,256,128]{2,1,0:T(8,128)(2,1)S(1)}, bf16[6,256,128]{2,1,0:T(8,128)(2,1)S(1)}, bf16[3456,128]{1,0:T(8,128)(2,1)S(1)}) custom-call(s32[1,64]{1,0:T(1,128)} %clips.1, bf16[8,256,128]{2,1,0:T(8,128)(2,1)} %bitcast.4, bf16[8,256,128]{2,1,0:T(8,128)(2,1)} %bitcast.6, bf16[3456,128]{1,0:T(8,128)(2,1)} %weight1.1), custom_call_target="tpu_custom_call" | custom-call | bytes 1048576 | tf_op jit(solution)/shard_map/pallas_call | solution.py:477
  2.0 5.9 %collective-permute-start.1 = (bf16[6,256,128]{2,1,0:T(8,128)(2,1)S(1)}, bf16[6,256,128]{2,1,0:T(8,128)(2,1)S(1)}, u32[]{:S(2)}, u32[]{:S(2)}) collective-permute-start(bf16[6,256,128]{2,1,0:T(8,128)(2,1)S(1)} %get-tuple-element.77), channel_id=1, source_target_pairs={{0,224},{32,0},{64,32},{96,64},{128,96},{160,128},{192,160},{224,1... | collective-permute-start | bytes 1179656 | tf_op jit(solution)/shard_map/ppermute | solution.py:519
  8.0 0.0 collective-permute-start
  8.0 8.0 %shard_map.85 = (bf16[9,256,128]{2,1,0:T(8,128)(2,1)S(1)}, bf16[9,256,128]{2,1,0:T(8,128)(2,1)S(1)}, bf16[3456,128]{1,0:T(8,128)(2,1)S(1)}, bf16[1152,384]{1,0:T...) custom-call(s32[1,64]{1,0:T(1,128)S(1)} %get-tuple-element.78.clips,, ...), custom_call_target="tpu_custom_call" | custom-call | flops 3623878656 | bytes 1048576 | tf_op jit(solution)/shard_map/pallas_call | solution.py:477
  16.0 1.0 %collective-permute-done.tail = bf16[4,256,128]{2,1,0:T(8,128)(2,1)S(1)} collective-permute-done((bf16[4,256,128]{2,1,0:T(8,128)(2,1)S(1)}, bf16[4,256,128]{2,1,0:T(8,128)(2,1)S(1)}, u32[]{:S(2)}, u32[]{:S(2)}) %collective-permute-start) | collective-permute-done | bytes 262176 | tf_op jit(solution)/shard_map/ppermute | solution.py:519
  16.9 0.0 collective-permute-done.1.head
  16.9 7.2 %shard_map.86 = (bf16[8,256,128]{2,1,0:T(8,128)(2,1)S(1)}, bf16[8,256,128]{2,1,0:T(8,128)(2,1)S(1)}, f32[2,16,112,128]{3,2,1,0:T(8,128)S(1)}, bf16[2,16,112,128]{3,2,1,0:T(8,128)(2,1)S(1)}) custom-call(s32[1,64]{1,0:T(1,128)S(1)} %get-tuple-element.78.clips, bf16[9,256,128]{2,1,0:T(8,128)(2,1)S(1)} %get-tuple-element.93.frames, ...), custom_call_target="tpu_custom_call" | custom-call | flops 3623878656 | bytes 1048576 | tf_op jit(solution)/shard_map/pallas_call | solution.py:477
  24.2 0.3 collective-permute-start.2
  24.4 2.4 %shard_map.87.next_in = bf16[2,256,128]{2,1,0:T(8,128)(2,1)S(1)} custom-call(s32[1,64]{1,0:T(1,128)S(1)} %get-tuple-element.78.clips, bf16[9,256,128]{2,1,0:T(8,128)(2,1)S(1)} %get-tuple-element.93.frames, bf16[6,256,128]{2,1,0:T(8,128)(2,1)S(1)} %collective-permute-done.1.head, bf16[1152,384]{1,0:T(8,128)(2,1)S(1)} %get-tuple-element.96.conv_weight, ...), custom_call_target="tpu_custom_call" | custom-call | flops 905969664 | bytes 1048576 | tf_op jit(solution)/shard_map/pallas_call | solution.py:477
  26.9 0.0 collective-permute-done.2.part
  26.9 0.2 shard_map.88
  27.1 2.2 %collective-permute-start.3 = (bf16[2,4,112,128]{3,2,1,0:T(8,128)(2,1)S(1)}, bf16[2,4,112,128]{3,2,1,0:T(8,128)(2,1)S(1)}, u32[]{:S(2)}, u32[]{:S(2)}) collective-permute-start(bf16[2,4,112,128]{3,2,1,0:T(8,128)(2,1)S(1)} %get-tuple-element.115), channel_id=1, source_target_pairs={{0,4},{1,17},{2,6},{3,19},{4,0},{5,21},{6,2},{7,23},{8,12},{9,25},... | collective-permute-start | bytes 688136 | tf_op jit(solution)/shard_map/ppermute | solution.py:503
  29.3 0.0 collective-permute-start.4
  29.3 2.0 %collective-permute-start.5 = (bf16[2,4,112,128]{3,2,1,0:T(8,128)(2,1)S(1)}, bf16[2,4,112,128]{3,2,1,0:T(8,128)(2,1)S(1)}, u32[]{:S(2)}, u32[]{:S(2)}) collective-permute-start(bf16[2,4,112,128]{3,2,1,0:T(8,128)(2,1)S(1)} %get-tuple-element.117), channel_id=1, source_target_pairs={{0,6},{1,25},{2,0},{3,27},{4,2},{5,29},{6,4},{7,31},{8,14},{9,1},{... | collective-permute-start | bytes 688136 | tf_op jit(solution)/shard_map/ppermute | solution.py:503
  31.3 3.3 %shard_map.89 = (bf16[4,256,128]{2,1,0:T(8,128)(2,1)S(1)}, bf16[1152,384]{1,0:T(8,128)(2,1)S(1)}) custom-call(s32[1,64]{1,0:T(1,128)S(1)} %get-tuple-element.78.clips, bf16[8,256,128]{2,1,0:T(8,128)(2,1)S(1)} %get-tuple-element.118.hidden_in, bf16[9,256,128]{2,1,0:T(8,128)(2,1)S(1)} %get-tuple-element.93.frames, ...), custom_call_target="tpu_custom_call" | custom-call | flops 1358954496 | bytes 1048576 | tf_op jit(solution)/shard_map/pallas_call | solution.py:477
  34.7 0.2 collective-permute-done.3.refs_0_
  34.8 2.4 %collective-permute-done.4.refs_1_ = bf16[2,4,112,128]{3,2,1,0:T(8,128)(2,1)S(1)} collective-permute-done((bf16[2,4,112,128]{3,2,1,0:T(8,128)(2,1)S(1)}, bf16[2,4,112,128]{3,2,1,0:T(8,128)(2,1)S(1)}, u32[]{:S(2)}, u32[]{:S(2)}) %collective-permute-start.4) | collective-permute-done | bytes 229408 | tf_op jit(solution)/shard_map/ppermute | solution.py:503
  37.3 0.0 collective-permute-done.5.refs_2_
  37.3 0.1 shard_map.90
  37.4 3.3 %collective-permute-start.6 = (bf16[2,112,128]{2,1,0:T(8,128)(2,1)S(1)}, bf16[2,112,128]{2,1,0:T(8,128)(2,1)S(1)}, u32[]{:S(2)}, u32[]{:S(2)}) collective-permute-start(bf16[2,112,128]{2,1,0:T(8,128)(2,1)S(1)} %get-tuple-element.128), channel_id=1, source_target_pairs={{0,16},{1,5},{2,18},{3,7},{4,20},{5,1},{6,22},{7,3},{8,24},{9,13},... | collective-permute-start | bytes 172040 | tf_op jit(solution)/shard_map/ppermute | solution.py:503
  40.7 0.7 %collective-permute-start.7 = (bf16[2,112,128]{2,1,0:T(8,128)(2,1)S(1)}, bf16[2,112,128]{2,1,0:T(8,128)(2,1)S(1)}, u32[]{:S(2)}, u32[]{:S(2)}) collective-permute-start(bf16[2,112,128]{2,1,0:T(8,128)(2,1)S(1)} %get-tuple-element.129), channel_id=1, source_target_pairs={{0,8},{1,3},{2,10},{3,5},{4,12},{5,7},{6,14},{7,1},{8,16},{9,11},{... | collective-permute-start | bytes 172040 | tf_op jit(solution)/shard_map/ppermute | solution.py:503
  41.3 2.6 %collective-permute-start.8 = (bf16[2,112,128]{2,1,0:T(8,128)(2,1)S(1)}, bf16[2,112,128]{2,1,0:T(8,128)(2,1)S(1)}, u32[]{:S(2)}, u32[]{:S(2)}) collective-permute-start(bf16[2,112,128]{2,1,0:T(8,128)(2,1)S(1)} %get-tuple-element.130), channel_id=1, source_target_pairs={{0,24},{1,7},{2,26},{3,1},{4,28},{5,3},{6,30},{7,5},{8,0},{9,15},{... | collective-permute-start | bytes 172040 | tf_op jit(solution)/shard_map/ppermute | solution.py:503
  43.9 2.8 %shard_map.91 = bf16[8,256,128]{2,1,0:T(8,128)(2,1)} custom-call(s32[1,64]{1,0:T(1,128)S(1)} %get-tuple-element.78.clips, bf16[8,256,128]{2,1,0:T(8,128)(2,1)S(1)} %get-tuple-element.118.hidden_in, bf16[9,256,128]{2,1,0:T(8,128)(2,1)S(1)} %get-tuple-element.93.frames, bf16[1152,384]{1,0:T(8,128)(2,1)S(1)} %get-tuple-element.131.weight, ...), custom_call_target="tpu_custom_call" | custom-call | flops 905969664 | bytes 1048576 | tf_op jit(solution)/shard_map/pallas_call | solution.py:477
  46.7 0.0 collective-permute-done.6.refs_0_
  46.7 0.0 collective-permute-done.7.refs_1_
  46.7 0.0 collective-permute-done.8.refs_2_
  46.8 0.1 collective-permute-start.9
  46.9 4.2 %collective-permute-done.9.refs_0_ = bf16[2,112,128]{2,1,0:T(8,128)(2,1)S(1)} collective-permute-done((bf16[2,112,128]{2,1,0:T(8,128)(2,1)S(1)}, bf16[2,112,128]{2,1,0:T(8,128)(2,1)S(1)}, u32[]{:S(2)}, u32[]{:S(2)}) %collective-permute-start.9) | collective-permute-done | bytes 57376 | tf_op jit(solution)/shard_map/ppermute | solution.py:519
  51.1 2.8 %collective-permute-start.12 = (bf16[2,112,128]{2,1,0:T(8,128)(2,1)S(1)}, bf16[2,112,128]{2,1,0:T(8,128)(2,1)S(1)}, u32[]{:S(2)}, u32[]{:S(2)}) collective-permute-start(bf16[2,112,128]{2,1,0:T(8,128)(2,1)S(1)} %shard_map.93.refs_0_), channel_id=1, source_target_pairs={{0,160},{32,128},{64,224},{96,192},{128,32},{160,0},{192,96},{224,... | collective-permute-start | bytes 172040 | tf_op jit(solution)/shard_map/ppermute | solution.py:519
  53.9 1.9 %collective-permute-start.11 = (bf16[2,112,128]{2,1,0:T(8,128)(2,1)S(1)}, bf16[2,112,128]{2,1,0:T(8,128)(2,1)S(1)}, u32[]{:S(2)}, u32[]{:S(2)}) collective-permute-start(bf16[2,112,128]{2,1,0:T(8,128)(2,1)S(1)} %shard_map.93.refs_0_), channel_id=1, source_target_pairs={{0,192},{32,96},{64,0},{96,160},{128,64},{160,224},{192,128},{224,... | collective-permute-start | bytes 172040 | tf_op jit(solution)/shard_map/ppermute | solution.py:519
  55.9 1.7 %collective-permute-start.10 = (bf16[2,112,128]{2,1,0:T(8,128)(2,1)S(1)}, bf16[2,112,128]{2,1,0:T(8,128)(2,1)S(1)}, u32[]{:S(2)}, u32[]{:S(2)}) collective-permute-start(bf16[2,112,128]{2,1,0:T(8,128)(2,1)S(1)} %shard_map.93.refs_0_), channel_id=1, source_target_pairs={{0,224},{32,64},{64,32},{96,128},{128,96},{160,192},{192,160},{224... | collective-permute-start | bytes 172040 | tf_op jit(solution)/shard_map/ppermute | solution.py:519
  57.6 4.3 %shard_map.94 = bf16[8,256,128]{2,1,0:T(8,128)(2,1)} custom-call(s32[1,64]{1,0:T(1,128)S(1)} %get-tuple-element.78.clips, bf16[8,256,128]{2,1,0:T(8,128)(2,1)S(1)} %get-tuple-element.140.act_grad_in, bf16[2,256,128]{2,1,0:T(8,128)(2,1)S(1)} %shard_map.87.next_in, bf16[9,256,128]{2,1,0:T(8,128)(2,1)S(1)} %get-tuple-element.94.cot, ...), custom_call_target="tpu_custom_call" | custom-call | flops 1811939328 | bytes 1048576 | tf_op jit(solution)/shard_map/pallas_call | solution.py:477
  61.9 0.0 collective-permute-done.12.refs_3_
  61.9 0.0 collective-permute-done.11.refs_2_
  61.9 0.0 collective-permute-done.10.refs_1_
  61.9 0.7 %shard_map.95 = (f32[108,128]{1,0:T(8,128)}, f32[108,128]{1,0:T(8,128)}) custom-call(bf16[2,112,128]{2,1,0:T(8,128)(2,1)S(1)} %shard_map.93.refs_0_, bf16[2,112,128]{2,1,0:T(8,128)(2,1)S(1)} %collective-permute-done.10.refs_1_, bf16[2,112,128]{2,1,0:T(8,128)(2,1)S(1)} %collective-permute-done.11.refs_2_, bf16[2,112,128]{2,1,0:T(8,128)(2,1)S(1)} %collective-permute-done.12.refs_3_), custom_call_target="tpu_custom_call" | custom-call | bytes 1048576 | tf_op jit(solution)/shard_map/pallas_call | solution.py:477
  (2 shorter events, 0.0 us)
Async XLA Ops:
  2.0 14.9 %collective-permute-start.1 = (bf16[6,256,128]{2,1,0:T(8,128)(2,1)S(1)}, bf16[6,256,128]{2,1,0:T(8,128)(2,1)S(1)}, u32[]{:S(2)}, u32[]{:S(2)}) collective-permute-start(bf16[6,256,128]{2,1,0:T(8,128)(2,1)S(1)} %get-tuple-element.77), channel_id=1, source_target_pairs={{0,224},{32,0},{64,32},{96,64},{128,96},{160,128},{192,160},{224,1... | collective-permute-start | bytes 1179656 | tf_op jit(solution)/shard_map/ppermute | solution.py:519
  8.0 9.0 %collective-permute-start = (bf16[4,256,128]{2,1,0:T(8,128)(2,1)S(1)}, bf16[4,256,128]{2,1,0:T(8,128)(2,1)S(1)}, u32[]{:S(2)}, u32[]{:S(2)}) collective-permute-start(bf16[4,256,128]{2,1,0:T(8,128)(2,1)S(1)} %get-tuple-element.76), channel_id=1, source_target_pairs={{0,32},{32,64},{64,96},{96,128},{128,160},{160,192},{192,224},{224... | collective-permute-start | bytes 786440 | tf_op jit(solution)/shard_map/ppermute | solution.py:519
  24.2 2.7 %collective-permute-start.2 = (bf16[2,16,112,128]{3,2,1,0:T(8,128)(2,1)S(1)}, bf16[2,16,112,128]{3,2,1,0:T(8,128)(2,1)S(1)}, u32[]{:S(2)}, u32[]{:S(2)}) collective-permute-start(bf16[2,16,112,128]{3,2,1,0:T(8,128)(2,1)S(1)} %get-tuple-element.107), channel_id=1, source_target_pairs={{0,1},{1,0},{2,3},{3,2},{4,5},{5,4},{6,7},{7,6},{8,9},{9,8},{10,11... | collective-permute-start | bytes 2752520 | tf_op jit(solution)/shard_map/ppermute | solution.py:503
  27.1 7.7 %collective-permute-start.3 = (bf16[2,4,112,128]{3,2,1,0:T(8,128)(2,1)S(1)}, bf16[2,4,112,128]{3,2,1,0:T(8,128)(2,1)S(1)}, u32[]{:S(2)}, u32[]{:S(2)}) collective-permute-start(bf16[2,4,112,128]{3,2,1,0:T(8,128)(2,1)S(1)} %get-tuple-element.115), channel_id=1, source_target_pairs={{0,4},{1,17},{2,6},{3,19},{4,0},{5,21},{6,2},{7,23},{8,12},{9,25},... | collective-permute-start | bytes 688136 | tf_op jit(solution)/shard_map/ppermute | solution.py:503
  29.3 7.9 %collective-permute-start.4 = (bf16[2,4,112,128]{3,2,1,0:T(8,128)(2,1)S(1)}, bf16[2,4,112,128]{3,2,1,0:T(8,128)(2,1)S(1)}, u32[]{:S(2)}, u32[]{:S(2)}) collective-permute-start(bf16[2,4,112,128]{3,2,1,0:T(8,128)(2,1)S(1)} %get-tuple-element.116), channel_id=1, source_target_pairs={{0,2},{1,9},{2,4},{3,11},{4,6},{5,13},{6,0},{7,15},{8,10},{9,17},{... | collective-permute-start | bytes 688136 | tf_op jit(solution)/shard_map/ppermute | solution.py:503
  29.3 7.9 %collective-permute-start.5 = (bf16[2,4,112,128]{3,2,1,0:T(8,128)(2,1)S(1)}, bf16[2,4,112,128]{3,2,1,0:T(8,128)(2,1)S(1)}, u32[]{:S(2)}, u32[]{:S(2)}) collective-permute-start(bf16[2,4,112,128]{3,2,1,0:T(8,128)(2,1)S(1)} %get-tuple-element.117), channel_id=1, source_target_pairs={{0,6},{1,25},{2,0},{3,27},{4,2},{5,29},{6,4},{7,31},{8,14},{9,1},{... | collective-permute-start | bytes 688136 | tf_op jit(solution)/shard_map/ppermute | solution.py:503
  37.4 9.4 %collective-permute-start.6 = (bf16[2,112,128]{2,1,0:T(8,128)(2,1)S(1)}, bf16[2,112,128]{2,1,0:T(8,128)(2,1)S(1)}, u32[]{:S(2)}, u32[]{:S(2)}) collective-permute-start(bf16[2,112,128]{2,1,0:T(8,128)(2,1)S(1)} %get-tuple-element.128), channel_id=1, source_target_pairs={{0,16},{1,5},{2,18},{3,7},{4,20},{5,1},{6,22},{7,3},{8,24},{9,13},... | collective-permute-start | bytes 172040 | tf_op jit(solution)/shard_map/ppermute | solution.py:503
  40.7 6.1 %collective-permute-start.7 = (bf16[2,112,128]{2,1,0:T(8,128)(2,1)S(1)}, bf16[2,112,128]{2,1,0:T(8,128)(2,1)S(1)}, u32[]{:S(2)}, u32[]{:S(2)}) collective-permute-start(bf16[2,112,128]{2,1,0:T(8,128)(2,1)S(1)} %get-tuple-element.129), channel_id=1, source_target_pairs={{0,8},{1,3},{2,10},{3,5},{4,12},{5,7},{6,14},{7,1},{8,16},{9,11},{... | collective-permute-start | bytes 172040 | tf_op jit(solution)/shard_map/ppermute | solution.py:503
  41.3 5.4 %collective-permute-start.8 = (bf16[2,112,128]{2,1,0:T(8,128)(2,1)S(1)}, bf16[2,112,128]{2,1,0:T(8,128)(2,1)S(1)}, u32[]{:S(2)}, u32[]{:S(2)}) collective-permute-start(bf16[2,112,128]{2,1,0:T(8,128)(2,1)S(1)} %get-tuple-element.130), channel_id=1, source_target_pairs={{0,24},{1,7},{2,26},{3,1},{4,28},{5,3},{6,30},{7,5},{8,0},{9,15},{... | collective-permute-start | bytes 172040 | tf_op jit(solution)/shard_map/ppermute | solution.py:503
  46.8 4.3 %collective-permute-start.9 = (bf16[2,112,128]{2,1,0:T(8,128)(2,1)S(1)}, bf16[2,112,128]{2,1,0:T(8,128)(2,1)S(1)}, u32[]{:S(2)}, u32[]{:S(2)}) collective-permute-start(bf16[2,112,128]{2,1,0:T(8,128)(2,1)S(1)} %shard_map.92.keep_ref), channel_id=1, source_target_pairs={{0,32},{32,0},{64,96},{96,64},{128,160},{160,128},{192,224},{224,1... | collective-permute-start | bytes 172040 | tf_op jit(solution)/shard_map/ppermute | solution.py:519
  51.1 10.8 %collective-permute-start.12 = (bf16[2,112,128]{2,1,0:T(8,128)(2,1)S(1)}, bf16[2,112,128]{2,1,0:T(8,128)(2,1)S(1)}, u32[]{:S(2)}, u32[]{:S(2)}) collective-permute-start(bf16[2,112,128]{2,1,0:T(8,128)(2,1)S(1)} %shard_map.93.refs_0_), channel_id=1, source_target_pairs={{0,160},{32,128},{64,224},{96,192},{128,32},{160,0},{192,96},{224,... | collective-permute-start | bytes 172040 | tf_op jit(solution)/shard_map/ppermute | solution.py:519
  53.9 8.0 %collective-permute-start.11 = (bf16[2,112,128]{2,1,0:T(8,128)(2,1)S(1)}, bf16[2,112,128]{2,1,0:T(8,128)(2,1)S(1)}, u32[]{:S(2)}, u32[]{:S(2)}) collective-permute-start(bf16[2,112,128]{2,1,0:T(8,128)(2,1)S(1)} %shard_map.93.refs_0_), channel_id=1, source_target_pairs={{0,192},{32,96},{64,0},{96,160},{128,64},{160,224},{192,128},{224,... | collective-permute-start | bytes 172040 | tf_op jit(solution)/shard_map/ppermute | solution.py:519
  55.9 6.0 %collective-permute-start.10 = (bf16[2,112,128]{2,1,0:T(8,128)(2,1)S(1)}, bf16[2,112,128]{2,1,0:T(8,128)(2,1)S(1)}, u32[]{:S(2)}, u32[]{:S(2)}) collective-permute-start(bf16[2,112,128]{2,1,0:T(8,128)(2,1)S(1)} %shard_map.93.refs_0_), channel_id=1, source_target_pairs={{0,224},{32,64},{64,32},{96,128},{128,96},{160,192},{192,160},{224... | collective-permute-start | bytes 172040 | tf_op jit(solution)/shard_map/ppermute | solution.py:519

commit v7 on v6

--- a/solution.py
+++ b/solution.py
@@ -143,9 +143,12 @@
     return lax.axis_index("seq") * F
 
 
-def halo_kernel(clips, frames, cot, weight1, clips_copy, tail, head, weight1_copy, sems):
+def halo_kernel(
+    clips, frames, cot, weight1, clips_copy, tail, head, weight1_copy, window, sems
+):
     copies = [
         pltpu.make_async_copy(weight1, weight1_copy, sems.at[4]),
+        pltpu.make_async_copy(frames, window.at[:F], sems.at[5]),
         pltpu.make_async_copy(clips, clips_copy, sems.at[3]),
         pltpu.make_async_copy(frames.at[F - 4 :], tail, sems.at[0]),
         pltpu.make_async_copy(frames.at[:2], head.at[:2], sems.at[1]),
@@ -153,20 +156,21 @@
     ]
     for copy in copies:
         copy.start()
+    window[F] = jnp.zeros((POS, C), BF16)
     for copy in copies:
         copy.wait()
 
 
+SIDES = (0, 1, F - 2, F - 1)
 EDGE = F - 2
 
 
 def local_kernel(
     clips,
-    frames,
+    window,
     cot,
     weight1,
     weight2,
-    window,
     cot_window,
     weight2_copy,
     conv_weight,
@@ -178,26 +182,30 @@
     frame_t,
     cot_shifted,
     second_part,
+    act_grad,
+    first_part,
     hidden_t,
     cot_taps,
+    frame_taps,
+    grad_shifted,
+    work,
     sems,
 ):
     copies = [
-        pltpu.make_async_copy(frames, window.at[:F], sems.at[0]),
-        pltpu.make_async_copy(weight2, weight2_copy, sems.at[1]),
-        pltpu.make_async_copy(cot, cot_window.at[:F], sems.at[2]),
+        pltpu.make_async_copy(weight2, weight2_copy, sems.at[0]),
+        pltpu.make_async_copy(cot, cot_window.at[:F], sems.at[1]),
     ]
     for copy in copies:
         copy.start()
-    window[F] = jnp.zeros((POS, C), BF16)
     cot_window[F] = jnp.zeros((POS, C), BF16)
     frame_t[F] = jnp.zeros((3 * C, POS), BF16)
     cot_shifted[F] = jnp.zeros((POS, 3 * C), BF16)
     first = first_frame()
     forward_weight(weight1, conv_weight)
-    for copy in copies:
-        copy.wait()
     for t in range(2, F):
+        if t == 4:
+            for copy in copies:
+                copy.wait()
         act[t] = conv_frame(window, past_slots(clips, first, t, 0, F), conv_weight)
     adjoint_weight(weight2_copy, back_weight)
     for f in range(F):
@@ -206,8 +214,9 @@
             frame_t[f, a * C : (a + 1) * C, :] = piece.T
     for t in range(EDGE):
         back[t] = conv_frame(cot_window, next_slots(clips, first, t, 0, F), back_weight)
-    for t, scale in enumerate(normalize(act.at[2:F], F - 2)):
-        scales[2 + t : 3 + t] = scale
+    scale = normalize(act.at[2:F], F - 2)
+    for t in range(2, F):
+        scales[t : t + 1] = scale[t - 2]
     for t in range(2, F):
         value = hidden_of(act[t])
         hidden[t] = value
@@ -219,6 +228,15 @@
             for k in range(3):
                 cot_taps[place, 3 * C * k : 3 * C * (k + 1)] = cot_shifted[slots[2 - k]]
     second_part[...] = jnp.dot(hidden_t[...], cot_taps[...], preferred_element_type=F32)
+    rounded = norm_adjoint(lambda n: act[2 + n], lambda n: back[2 + n], scale[: EDGE - 2], work)
+    for n, value in enumerate(rounded):
+        act_grad[2 + n] = value
+        place = slice(n * POS, (n + 1) * POS)
+        grad_shifted[place] = column_pieces(value)
+        slots = past_slots(clips, first, 2 + n, 0, F)
+        for k in range(3):
+            frame_taps[3 * C * k : 3 * C * (k + 1), place] = frame_t[slots[k]]
+    first_part[...] = jnp.dot(frame_taps[...], grad_shifted[...], preferred_element_type=F32)
 
 
 def split_rows(grads, g, keep_ref, send_ref):
@@ -247,6 +265,8 @@
     frame_t_in,
     cot_shifted_in,
     second_part,
+    act_grad_in,
+    first_part,
     hidden_ref,
     act_grad_ref,
     keep_ref,
@@ -285,11 +305,11 @@
             frame_t[f, a * C : (a + 1) * C, :] = piece.T
     cot_shifted[2] = jnp.zeros((POS, 3 * C), BF16)
     frame_t[2] = jnp.zeros((3 * C, POS), BF16)
-    scale = normalize(act, 2) + [scales[t : t + 1] for t in range(2, F)]
+    scale = normalize(act, 2) + [scales[t : t + 1] for t in SIDES[2:]]
     for t in range(F):
         hidden_ref[t] = hidden_of(act[t]) if t < 2 else hidden_in[t]
 
-    for n, s in enumerate((0, 1, EDGE, EDGE + 1)):
+    for n, s in enumerate(SIDES):
         place = slice(n * POS, (n + 1) * POS)
         for a, piece in enumerate(row_pieces(hidden_ref[s])):
             hidden_t[a * C : (a + 1) * C, place] = piece.T
@@ -311,22 +331,27 @@
                 ]
 
     rounded = norm_adjoint(
-        lambda t: act[t] if t < 2 else act_in[t],
-        lambda t: back_in[t] if t < EDGE else back[t - EDGE],
+        lambda n: act[n] if n < 2 else act_in[SIDES[n]],
+        lambda n: back_in[n] if n < 2 else back[n - 2],
         scale,
         work,
     )
-    for t in range(F):
-        act_grad_ref[t] = rounded[t]
-        grad_shifted[t * POS : (t + 1) * POS] = column_pieces(rounded[t])
+    for t in range(2, EDGE):
+        act_grad_ref[t] = act_grad_in[t]
+    for n, t in enumerate(SIDES):
+        act_grad_ref[t] = rounded[n]
+        place = slice(n * POS, (n + 1) * POS)
+        grad_shifted[place] = column_pieces(rounded[n])
         near = past_slots(clips, first, t, 0, F)
         far = past_slots(clips, first, t, 2, 2)
         for k in range(3):
-            frame_taps[3 * C * k : 3 * C * (k + 1), t * POS : (t + 1) * POS] = (
+            frame_taps[3 * C * k : 3 * C * (k + 1), place] = (
                 frame_t_in[near[k]] if t + k - 2 >= 0 else frame_t[far[k]]
             )
     split_rows(grads, 1, keep_ref, send_ref)
-    first_grad = jnp.dot(frame_taps[...], grad_shifted[...], preferred_element_type=F32)
+    first_grad = first_part[...] + jnp.dot(
+        frame_taps[...], grad_shifted[...], preferred_element_type=F32
+    )
     for outer in range(9):
         for b in range(3):
             tap = outer * 3 + b
@@ -526,21 +551,26 @@
         pltpu.with_memory_space_constraint(value, pltpu.HBM)
         for value in (clip_ids, own_frames, own_cot, conv1_weight, conv2_weight)
     )
-    clip_ids, tail, head, weight1 = call(
+    clip_ids, tail, head, weight1, frame_copy = call(
         halo_kernel,
         (clip_ids, own_frames, own_cot, conv1_weight),
         [HBM] * 4,
-        [(clip_ids.shape, jnp.int32), frame_shape(4), frame_shape(6), ((27 * C, C), BF16)],
-        [pltpu.SemaphoreType.DMA((5,))],
+        [
+            (clip_ids.shape, jnp.int32),
+            frame_shape(4),
+            frame_shape(6),
+            ((27 * C, C), BF16),
+            frame_shape(F + 1),
+        ],
+        [pltpu.SemaphoreType.DMA((6,))],
     )
     head = shifted(head, -1)
     tail = shifted(tail, 1)
     local = call(
         local_kernel,
-        (clip_ids, own_frames, own_cot, weight1, conv2_weight),
-        [SMEM, HBM, HBM, VMEM, HBM],
+        (clip_ids, frame_copy, own_cot, weight1, conv2_weight),
+        [SMEM, VMEM, HBM, VMEM, HBM],
         [
-            frame_shape(F + 1),
             frame_shape(F + 1),
             ((27 * C, C), BF16),
             WIDE,
@@ -552,52 +582,46 @@
             ((F + 1, 3 * C, POS), BF16),
             ((F + 1, POS, 3 * C), BF16),
             ((3 * C, 9 * C), F32),
+            frame_shape(F),
+            ((9 * C, 3 * C), F32),
         ],
         [
             ((3 * C, 4 * POS), BF16),
             ((4 * POS, 9 * C), BF16),
-            pltpu.SemaphoreType.DMA((3,)),
+            ((9 * C, 4 * POS), BF16),
+            ((4 * POS, 3 * C), BF16),
+            frame_shape(4, F32),
+            pltpu.SemaphoreType.DMA((2,)),
         ],
-        flops=CONV_FLOPS * 2,
-        limit=16,
+        flops=CONV_FLOPS * 5 // 2,
+        limit=24,
     )
     tail, head, local = lax.optimization_barrier((tail, head, local))
-    frame_copy, cot_copy, weight2, conv_weight, back_weight, *partial = local
+    cot_copy, weight2, conv_weight, back_weight, *partial = local
     block = ((2, 16, PADDED, C), F32)
     hidden, act_grad, keep, send = call(
         main_kernel,
         (clip_ids, frame_copy, cot_copy, tail, head, conv_weight, back_weight, *partial),
-        [SMEM] + [VMEM] * 13,
+        [SMEM] + [VMEM] * 15,
         [frame_shape(F), frame_shape(F), block, (block[0], BF16)],
         [
             frame_shape(5),
             frame_shape(5),
             frame_shape(2, F32),
             frame_shape(2, F32),
-            frame_shape(F, F32),
+            frame_shape(4, F32),
             ((3, POS, 3 * C), BF16),
             ((4 * POS, 9 * C), BF16),
             ((3, 3 * C, POS), BF16),
-            ((9 * C, F * POS), BF16),
+            ((9 * C, 4 * POS), BF16),
             ((3 * C, 4 * POS), BF16),
-            ((F * POS, 3 * C), BF16),
+            ((4 * POS, 3 * C), BF16),
             ((2, 27 * C, C), F32),
         ],
-        flops=CONV_FLOPS * 2,
-        limit=32,
+        flops=CONV_FLOPS * 3 // 2,
+        limit=28,
     )
     recv = dp_permute(send, lambda d: d ^ 1)
-    head, keep = lax.optimization_barrier((head, keep))
-    (act_grad_next,) = call(
-        next_grad_kernel,
-        (clip_ids, frame_copy, head, conv_weight, back_weight),
-        [SMEM] + [VMEM] * 4,
-        [frame_shape(2)],
-        [frame_shape(5), frame_shape(5), frame_shape(2, F32), frame_shape(2, F32)],
-        flops=CONV_FLOPS // 2,
-        limit=8,
-    )
-    recv, act_grad_next = lax.optimization_barrier((recv, act_grad_next))
     keep, *sent = call(
         first_kernel,
         (keep, recv),
@@ -637,7 +661,18 @@
     )
     recv, block_out = lax.optimization_barrier((recv, block_out))
     (total,) = call(sum_kernel, (keep, *recv), [VMEM] * 4, [(pair, BF16)])
+    head, total = lax.optimization_barrier((head, total))
     other = seq_permute(total, lambda z: z ^ 1)
+    (act_grad_next,) = call(
+        next_grad_kernel,
+        (clip_ids, frame_copy, head, conv_weight, back_weight),
+        [SMEM] + [VMEM] * 4,
+        [frame_shape(2)],
+        [frame_shape(5), frame_shape(5), frame_shape(2, F32), frame_shape(2, F32)],
+        flops=CONV_FLOPS // 2,
+        limit=8,
+    )
+    other, act_grad_next = lax.optimization_barrier((other, act_grad_next))
     (total,) = call(sum_kernel, (total, other), [VMEM] * 2, [(pair, BF16)])
     total, act_grad = lax.optimization_barrier((total, act_grad))
     others = [

time: 63.3 us -> 65 us (1.027)
  starting transfers between devices: 23.6 us -> 25.1 us
    ppermute x7, waiting for transfers between devices: 2.61 us -> 5.05 us  [dp_permute(): lax.ppermute(value, 'dp', [(source, target(source)) for source in range(3...]
    ppermute x6, waiting for transfers between devices: 5.15 us -> 2.84 us  [seq_permute(): lax.ppermute(value, 'seq', [(source, target(source) % 8) for source in ra...]
    ppermute x6, starting transfers between devices: 12.6 us -> 14.1 us  [seq_permute(): lax.ppermute(value, 'seq', [(source, target(source) % 8) for source in ra...]
  transfers between devices with their start and end apart: 13 -> 13, of which waited for: 4 -> 5; matrix products, arithmetic and copies ran while one was open for 0% -> 0% of each run, Pallas kernels for 33% -> 34%
where the time goes in v7:
time: 65 us; the launch traced here: 64.1 us
  Pallas kernels  30.3 us (47%)
  starting transfers between devices  25.1 us (39%)
  waiting for transfers between devices  7.9 us (12%)
  between operations  0.73 us (1%)
    pallas_call x12, Pallas kernels, call(): pl.pallas_call(kernel, out_shape=[jax.ShapeDtypeStruct(shape, dtype) for...  30.3 us
    ppermute x6, starting transfers between devices, seq_permute(): lax.ppermute(value, 'seq', [(source, target(source) % 8) for source in ra...  14.1 us
    ppermute x7, starting transfers between devices, dp_permute(): lax.ppermute(value, 'dp', [(source, target(source)) for source in range(3...  11 us
    ppermute x7, waiting for transfers between devices, dp_permute(): lax.ppermute(value, 'dp', [(source, target(source)) for source in range(3...  5.05 us
    ppermute x6, waiting for transfers between devices, seq_permute(): lax.ppermute(value, 'seq', [(source, target(source) % 8) for source in ra...  2.84 us
  transfers between devices with their start and end apart: 13, of which 5 were waited for; matrix products, arithmetic and copies ran while one was open for 0% of the time, Pallas kernels for 34%

profile of v7, /device:TPU:2, one launch (start us, length us, event | category | flops | bytes accessed | tf_op | source)
XLA Modules:
  0.0 64.1 jit_solution(9625772582230509745)
XLA Ops:
  0.6 1.6 %shard_map.84 = (s32[1,64]{1,0:T(1,128)S(1)}, bf16[4,256,128]{2,1,0:T(8,128)(2,1)S(1)}, bf16[6,256,128]{2,1,0:T(8,128)(2,1)S(1)}, bf16[3456,128]{1,0:T(8,128)(2,1)S(1)}, bf16[9,256,128]{2,1,0:T(8,128)(2,1)S(1)}) custom-call(s32[1,64]{1,0:T(1,128)} %clips.1, bf16[8,256,128]{2,1,0:T(8,128)(2,1)} %bitcast.4, bf16[8,256,128]{2,1,0:T(8,128)(2,1)} %bitcast.5, ...), custom_call_target="tpu_custom_call" | custom-call | bytes 1048576 | tf_op jit(solution)/shard_map/pallas_call | solution.py:502
  2.2 2.0 %collective-permute-start = (bf16[4,256,128]{2,1,0:T(8,128)(2,1)S(1)}, bf16[4,256,128]{2,1,0:T(8,128)(2,1)S(1)}, u32[]{:S(2)}, u32[]{:S(2)}) collective-permute-start(bf16[4,256,128]{2,1,0:T(8,128)(2,1)S(1)} %get-tuple-element.81), channel_id=1, source_target_pairs={{0,32},{32,64},{64,96},{96,128},{128,160},{160,192},{192,224},{224... | collective-permute-start | bytes 786440 | tf_op jit(solution)/shard_map/ppermute | solution.py:544
  4.2 4.0 %collective-permute-start.1 = (bf16[6,256,128]{2,1,0:T(8,128)(2,1)S(1)}, bf16[6,256,128]{2,1,0:T(8,128)(2,1)S(1)}, u32[]{:S(2)}, u32[]{:S(2)}) collective-permute-start(bf16[6,256,128]{2,1,0:T(8,128)(2,1)S(1)} %get-tuple-element.82), channel_id=1, source_target_pairs={{0,224},{32,0},{64,32},{96,64},{128,96},{160,128},{192,160},{224,1... | collective-permute-start | bytes 1179656 | tf_op jit(solution)/shard_map/ppermute | solution.py:544
  8.2 9.2 %shard_map.85 = (bf16[9,256,128]{2,1,0:T(8,128)(2,1)S(1)}, bf16[3456,128]{1,0:T(8,128)(2,1)S(1)}, bf16[1152,384]{1,0:T(8,128)(2,1)S(1)}, bf16[1152,384]{1,0:T(8,...) custom-call(s32[1,64]{1,0:T(1,128)S(1)} %get-tuple-element.79.clips,, ...), custom_call_target="tpu_custom_call" | custom-call | flops 4529848320 | bytes 1048576 | tf_op jit(solution)/shard_map/pallas_call | solution.py:502
  17.4 0.0 collective-permute-done.tail
  17.4 0.0 collective-permute-done.1.head
  17.5 5.7 %shard_map.86 = (bf16[8,256,128]{2,1,0:T(8,128)(2,1)S(1)}, bf16[8,256,128]{2,1,0:T(8,128)(2,1)S(1)}, f32[2,16,112,128]{3,2,1,0:T(8,128)S(1)}, bf16[2,16,112,128]{3,2,1,0:T(8,128)(2,1)S(1)}) custom-call(s32[1,64]{1,0:T(1,128)S(1)} %get-tuple-element.79.clips, bf16[9,256,128]{2,1,0:T(8,128)(2,1)S(1)} %get-tuple-element.80.window.frames, ...), custom_call_target="tpu_custom_call" | custom-call | flops 2717908992 | bytes 1048576 | tf_op jit(solution)/shard_map/pallas_call | solution.py:502
  23.2 0.3 collective-permute-start.2
  23.5 2.5 %collective-permute-done.2.part = bf16[2,16,112,128]{3,2,1,0:T(8,128)(2,1)S(1)} collective-permute-done((bf16[2,16,112,128]{3,2,1,0:T(8,128)(2,1)S(1)}, bf16[2,16,112,128]{3,2,1,0:T(8,128)(2,1)S(1)}, u32[]{:S(2)}, u32[]{:S(2)}) %collective-permute-start.2) | collective-permute-done | bytes 917536 | tf_op jit(solution)/shard_map/ppermute | solution.py:528
  25.9 0.2 shard_map.87
  26.1 2.2 %collective-permute-start.3 = (bf16[2,4,112,128]{3,2,1,0:T(8,128)(2,1)S(1)}, bf16[2,4,112,128]{3,2,1,0:T(8,128)(2,1)S(1)}, u32[]{:S(2)}, u32[]{:S(2)}) collective-permute-start(bf16[2,4,112,128]{3,2,1,0:T(8,128)(2,1)S(1)} %get-tuple-element.118), channel_id=1, source_target_pairs={{0,4},{1,17},{2,6},{3,19},{4,0},{5,21},{6,2},{7,23},{8,12},{9,25},... | collective-permute-start | bytes 688136 | tf_op jit(solution)/shard_map/ppermute | solution.py:528
  28.3 0.0 collective-permute-start.4
  28.3 2.0 %collective-permute-start.5 = (bf16[2,4,112,128]{3,2,1,0:T(8,128)(2,1)S(1)}, bf16[2,4,112,128]{3,2,1,0:T(8,128)(2,1)S(1)}, u32[]{:S(2)}, u32[]{:S(2)}) collective-permute-start(bf16[2,4,112,128]{3,2,1,0:T(8,128)(2,1)S(1)} %get-tuple-element.120), channel_id=1, source_target_pairs={{0,6},{1,25},{2,0},{3,27},{4,2},{5,29},{6,4},{7,31},{8,14},{9,1},{... | collective-permute-start | bytes 688136 | tf_op jit(solution)/shard_map/ppermute | solution.py:528
  30.3 3.3 %shard_map.88 = (bf16[4,256,128]{2,1,0:T(8,128)(2,1)S(1)}, bf16[1152,384]{1,0:T(8,128)(2,1)S(1)}) custom-call(s32[1,64]{1,0:T(1,128)S(1)} %get-tuple-element.79.clips, bf16[8,256,128]{2,1,0:T(8,128)(2,1)S(1)} %get-tuple-element.121.hidden_in, bf16[9,256,128]{2,1,0:T(8,128)(2,1)S(1)} %get-tuple-element.80.window.frames, ...), custom_call_target="tpu_custom_call" | custom-call | flops 1358954496 | bytes 1048576 | tf_op jit(solution)/shard_map/pallas_call | solution.py:502
  33.7 0.2 collective-permute-done.3.refs_0_
  33.8 2.4 %collective-permute-done.4.refs_1_ = bf16[2,4,112,128]{3,2,1,0:T(8,128)(2,1)S(1)} collective-permute-done((bf16[2,4,112,128]{3,2,1,0:T(8,128)(2,1)S(1)}, bf16[2,4,112,128]{3,2,1,0:T(8,128)(2,1)S(1)}, u32[]{:S(2)}, u32[]{:S(2)}) %collective-permute-start.4) | collective-permute-done | bytes 229408 | tf_op jit(solution)/shard_map/ppermute | solution.py:528
  36.2 0.0 collective-permute-done.5.refs_2_
  36.2 0.1 shard_map.89
  36.4 3.3 %collective-permute-start.6 = (bf16[2,112,128]{2,1,0:T(8,128)(2,1)S(1)}, bf16[2,112,128]{2,1,0:T(8,128)(2,1)S(1)}, u32[]{:S(2)}, u32[]{:S(2)}) collective-permute-start(bf16[2,112,128]{2,1,0:T(8,128)(2,1)S(1)} %get-tuple-element.131), channel_id=1, source_target_pairs={{0,16},{1,5},{2,18},{3,7},{4,20},{5,1},{6,22},{7,3},{8,24},{9,13},... | collective-permute-start | bytes 172040 | tf_op jit(solution)/shard_map/ppermute | solution.py:528
  39.7 0.7 %collective-permute-start.7 = (bf16[2,112,128]{2,1,0:T(8,128)(2,1)S(1)}, bf16[2,112,128]{2,1,0:T(8,128)(2,1)S(1)}, u32[]{:S(2)}, u32[]{:S(2)}) collective-permute-start(bf16[2,112,128]{2,1,0:T(8,128)(2,1)S(1)} %get-tuple-element.132), channel_id=1, source_target_pairs={{0,8},{1,3},{2,10},{3,5},{4,12},{5,7},{6,14},{7,1},{8,16},{9,11},{... | collective-permute-start | bytes 172040 | tf_op jit(solution)/shard_map/ppermute | solution.py:528
  40.4 2.5 %collective-permute-start.8 = (bf16[2,112,128]{2,1,0:T(8,128)(2,1)S(1)}, bf16[2,112,128]{2,1,0:T(8,128)(2,1)S(1)}, u32[]{:S(2)}, u32[]{:S(2)}) collective-permute-start(bf16[2,112,128]{2,1,0:T(8,128)(2,1)S(1)} %get-tuple-element.133), channel_id=1, source_target_pairs={{0,24},{1,7},{2,26},{3,1},{4,28},{5,3},{6,30},{7,5},{8,0},{9,15},{... | collective-permute-start | bytes 172040 | tf_op jit(solution)/shard_map/ppermute | solution.py:528
  42.9 2.8 %shard_map.90 = bf16[8,256,128]{2,1,0:T(8,128)(2,1)} custom-call(s32[1,64]{1,0:T(1,128)S(1)} %get-tuple-element.79.clips, bf16[8,256,128]{2,1,0:T(8,128)(2,1)S(1)} %get-tuple-element.121.hidden_in, bf16[9,256,128]{2,1,0:T(8,128)(2,1)S(1)} %get-tuple-element.80.window.frames, bf16[1152,384]{1,0:T(8,128)(2,1)S(1)} %get-tuple-element.134.weight, ...), custom_call_target="tpu_custom_call" | custom-call | flops 905969664 | bytes 1048576 | tf_op jit(solution)/shard_map/pallas_call | solution.py:502
  45.7 0.0 collective-permute-done.6.refs_0_
  45.7 0.0 collective-permute-done.7.refs_1_
  45.7 0.0 collective-permute-done.8.refs_2_
  45.8 0.1 collective-permute-start.9
  45.9 2.4 %shard_map.92.next_in = bf16[2,256,128]{2,1,0:T(8,128)(2,1)S(1)} custom-call(s32[1,64]{1,0:T(1,128)S(1)} %get-tuple-element.79.clips, bf16[9,256,128]{2,1,0:T(8,128)(2,1)S(1)} %get-tuple-element.80.window.frames, bf16[6,256,128]{2,1,0:T(8,128)(2,1)S(1)} %collective-permute-done.1.head, bf16[1152,384]{1,0:T(8,128)(2,1)S(1)} %get-tuple-element.100.conv_weight, ...), custom_call_target="tpu_custom_call" | custom-call | flops 905969664 | bytes 1048576 | tf_op jit(solution)/shard_map/pallas_call | solution.py:502
  48.3 1.7 %collective-permute-done.9.refs_0_ = bf16[2,112,128]{2,1,0:T(8,128)(2,1)S(1)} collective-permute-done((bf16[2,112,128]{2,1,0:T(8,128)(2,1)S(1)}, bf16[2,112,128]{2,1,0:T(8,128)(2,1)S(1)}, u32[]{:S(2)}, u32[]{:S(2)}) %collective-permute-start.9) | collective-permute-done | bytes 57376 | tf_op jit(solution)/shard_map/ppermute | solution.py:544
  50.1 3.4 %collective-permute-start.12 = (bf16[2,112,128]{2,1,0:T(8,128)(2,1)S(1)}, bf16[2,112,128]{2,1,0:T(8,128)(2,1)S(1)}, u32[]{:S(2)}, u32[]{:S(2)}) collective-permute-start(bf16[2,112,128]{2,1,0:T(8,128)(2,1)S(1)} %shard_map.93.refs_0_), channel_id=1, source_target_pairs={{0,160},{32,128},{64,224},{96,192},{128,32},{160,0},{192,96},{224,... | collective-permute-start | bytes 172040 | tf_op jit(solution)/shard_map/ppermute | solution.py:544
  53.5 4.5 %collective-permute-start.11 = (bf16[2,112,128]{2,1,0:T(8,128)(2,1)S(1)}, bf16[2,112,128]{2,1,0:T(8,128)(2,1)S(1)}, u32[]{:S(2)}, u32[]{:S(2)}) collective-permute-start(bf16[2,112,128]{2,1,0:T(8,128)(2,1)S(1)} %shard_map.93.refs_0_), channel_id=1, source_target_pairs={{0,192},{32,96},{64,0},{96,160},{128,64},{160,224},{192,128},{224,... | collective-permute-start | bytes 172040 | tf_op jit(solution)/shard_map/ppermute | solution.py:544
  58.0 0.0 collective-permute-start.10
  58.0 4.3 %shard_map.94 = bf16[8,256,128]{2,1,0:T(8,128)(2,1)} custom-call(s32[1,64]{1,0:T(1,128)S(1)} %get-tuple-element.79.clips, bf16[8,256,128]{2,1,0:T(8,128)(2,1)S(1)} %get-tuple-element.146.act_grad_in, bf16[2,256,128]{2,1,0:T(8,128)(2,1)S(1)} %shard_map.92.next_in, bf16[9,256,128]{2,1,0:T(8,128)(2,1)S(1)} %get-tuple-element.97.cot, ...), custom_call_target="tpu_custom_call" | custom-call | flops 1811939328 | bytes 1048576 | tf_op jit(solution)/shard_map/pallas_call | solution.py:502
  62.3 0.0 collective-permute-done.12.refs_3_
  62.3 0.0 collective-permute-done.11.refs_2_
  62.3 1.1 %collective-permute-done.10.refs_1_ = bf16[2,112,128]{2,1,0:T(8,128)(2,1)S(1)} collective-permute-done((bf16[2,112,128]{2,1,0:T(8,128)(2,1)S(1)}, bf16[2,112,128]{2,1,0:T(8,128)(2,1)S(1)}, u32[]{:S(2)}, u32[]{:S(2)}) %collective-permute-start.10) | collective-permute-done | bytes 57376 | tf_op jit(solution)/shard_map/ppermute | solution.py:544
  63.4 0.7 %shard_map.95 = (f32[108,128]{1,0:T(8,128)}, f32[108,128]{1,0:T(8,128)}) custom-call(bf16[2,112,128]{2,1,0:T(8,128)(2,1)S(1)} %shard_map.93.refs_0_, bf16[2,112,128]{2,1,0:T(8,128)(2,1)S(1)} %collective-permute-done.10.refs_1_, bf16[2,112,128]{2,1,0:T(8,128)(2,1)S(1)} %collective-permute-done.11.refs_2_, bf16[2,112,128]{2,1,0:T(8,128)(2,1)S(1)} %collective-permute-done.12.refs_3_), custom_call_target="tpu_custom_call" | custom-call | bytes 1048576 | tf_op jit(solution)/shard_map/pallas_call | solution.py:502
  (2 shorter events, 0.0 us)
Async XLA Ops:
  2.2 15.2 %collective-permute-start = (bf16[4,256,128]{2,1,0:T(8,128)(2,1)S(1)}, bf16[4,256,128]{2,1,0:T(8,128)(2,1)S(1)}, u32[]{:S(2)}, u32[]{:S(2)}) collective-permute-start(bf16[4,256,128]{2,1,0:T(8,128)(2,1)S(1)} %get-tuple-element.81), channel_id=1, source_target_pairs={{0,32},{32,64},{64,96},{96,128},{128,160},{160,192},{192,224},{224... | collective-permute-start | bytes 786440 | tf_op jit(solution)/shard_map/ppermute | solution.py:544
  4.2 13.3 %collective-permute-start.1 = (bf16[6,256,128]{2,1,0:T(8,128)(2,1)S(1)}, bf16[6,256,128]{2,1,0:T(8,128)(2,1)S(1)}, u32[]{:S(2)}, u32[]{:S(2)}) collective-permute-start(bf16[6,256,128]{2,1,0:T(8,128)(2,1)S(1)} %get-tuple-element.82), channel_id=1, source_target_pairs={{0,224},{32,0},{64,32},{96,64},{128,96},{160,128},{192,160},{224,1... | collective-permute-start | bytes 1179656 | tf_op jit(solution)/shard_map/ppermute | solution.py:544
  23.2 2.7 %collective-permute-start.2 = (bf16[2,16,112,128]{3,2,1,0:T(8,128)(2,1)S(1)}, bf16[2,16,112,128]{3,2,1,0:T(8,128)(2,1)S(1)}, u32[]{:S(2)}, u32[]{:S(2)}) collective-permute-start(bf16[2,16,112,128]{3,2,1,0:T(8,128)(2,1)S(1)} %get-tuple-element.112), channel_id=1, source_target_pairs={{0,1},{1,0},{2,3},{3,2},{4,5},{5,4},{6,7},{7,6},{8,9},{9,8},{10,11... | collective-permute-start | bytes 2752520 | tf_op jit(solution)/shard_map/ppermute | solution.py:528
  26.1 7.7 %collective-permute-start.3 = (bf16[2,4,112,128]{3,2,1,0:T(8,128)(2,1)S(1)}, bf16[2,4,112,128]{3,2,1,0:T(8,128)(2,1)S(1)}, u32[]{:S(2)}, u32[]{:S(2)}) collective-permute-start(bf16[2,4,112,128]{3,2,1,0:T(8,128)(2,1)S(1)} %get-tuple-element.118), channel_id=1, source_target_pairs={{0,4},{1,17},{2,6},{3,19},{4,0},{5,21},{6,2},{7,23},{8,12},{9,25},... | collective-permute-start | bytes 688136 | tf_op jit(solution)/shard_map/ppermute | solution.py:528
  28.3 7.9 %collective-permute-start.4 = (bf16[2,4,112,128]{3,2,1,0:T(8,128)(2,1)S(1)}, bf16[2,4,112,128]{3,2,1,0:T(8,128)(2,1)S(1)}, u32[]{:S(2)}, u32[]{:S(2)}) collective-permute-start(bf16[2,4,112,128]{3,2,1,0:T(8,128)(2,1)S(1)} %get-tuple-element.119), channel_id=1, source_target_pairs={{0,2},{1,9},{2,4},{3,11},{4,6},{5,13},{6,0},{7,15},{8,10},{9,17},{... | collective-permute-start | bytes 688136 | tf_op jit(solution)/shard_map/ppermute | solution.py:528
  28.3 7.9 %collective-permute-start.5 = (bf16[2,4,112,128]{3,2,1,0:T(8,128)(2,1)S(1)}, bf16[2,4,112,128]{3,2,1,0:T(8,128)(2,1)S(1)}, u32[]{:S(2)}, u32[]{:S(2)}) collective-permute-start(bf16[2,4,112,128]{3,2,1,0:T(8,128)(2,1)S(1)} %get-tuple-element.120), channel_id=1, source_target_pairs={{0,6},{1,25},{2,0},{3,27},{4,2},{5,29},{6,4},{7,31},{8,14},{9,1},{... | collective-permute-start | bytes 688136 | tf_op jit(solution)/shard_map/ppermute | solution.py:528
  36.4 9.4 %collective-permute-start.6 = (bf16[2,112,128]{2,1,0:T(8,128)(2,1)S(1)}, bf16[2,112,128]{2,1,0:T(8,128)(2,1)S(1)}, u32[]{:S(2)}, u32[]{:S(2)}) collective-permute-start(bf16[2,112,128]{2,1,0:T(8,128)(2,1)S(1)} %get-tuple-element.131), channel_id=1, source_target_pairs={{0,16},{1,5},{2,18},{3,7},{4,20},{5,1},{6,22},{7,3},{8,24},{9,13},... | collective-permute-start | bytes 172040 | tf_op jit(solution)/shard_map/ppermute | solution.py:528
  39.7 6.1 %collective-permute-start.7 = (bf16[2,112,128]{2,1,0:T(8,128)(2,1)S(1)}, bf16[2,112,128]{2,1,0:T(8,128)(2,1)S(1)}, u32[]{:S(2)}, u32[]{:S(2)}) collective-permute-start(bf16[2,112,128]{2,1,0:T(8,128)(2,1)S(1)} %get-tuple-element.132), channel_id=1, source_target_pairs={{0,8},{1,3},{2,10},{3,5},{4,12},{5,7},{6,14},{7,1},{8,16},{9,11},{... | collective-permute-start | bytes 172040 | tf_op jit(solution)/shard_map/ppermute | solution.py:528
  40.4 5.4 %collective-permute-start.8 = (bf16[2,112,128]{2,1,0:T(8,128)(2,1)S(1)}, bf16[2,112,128]{2,1,0:T(8,128)(2,1)S(1)}, u32[]{:S(2)}, u32[]{:S(2)}) collective-permute-start(bf16[2,112,128]{2,1,0:T(8,128)(2,1)S(1)} %get-tuple-element.133), channel_id=1, source_target_pairs={{0,24},{1,7},{2,26},{3,1},{4,28},{5,3},{6,30},{7,5},{8,0},{9,15},{... | collective-permute-start | bytes 172040 | tf_op jit(solution)/shard_map/ppermute | solution.py:528
  45.8 4.3 %collective-permute-start.9 = (bf16[2,112,128]{2,1,0:T(8,128)(2,1)S(1)}, bf16[2,112,128]{2,1,0:T(8,128)(2,1)S(1)}, u32[]{:S(2)}, u32[]{:S(2)}) collective-permute-start(bf16[2,112,128]{2,1,0:T(8,128)(2,1)S(1)} %shard_map.91.keep_ref), channel_id=1, source_target_pairs={{0,32},{32,0},{64,96},{96,64},{128,160},{160,128},{192,224},{224,1... | collective-permute-start | bytes 172040 | tf_op jit(solution)/shard_map/ppermute | solution.py:544
  50.1 12.2 %collective-permute-start.12 = (bf16[2,112,128]{2,1,0:T(8,128)(2,1)S(1)}, bf16[2,112,128]{2,1,0:T(8,128)(2,1)S(1)}, u32[]{:S(2)}, u32[]{:S(2)}) collective-permute-start(bf16[2,112,128]{2,1,0:T(8,128)(2,1)S(1)} %shard_map.93.refs_0_), channel_id=1, source_target_pairs={{0,160},{32,128},{64,224},{96,192},{128,32},{160,0},{192,96},{224,... | collective-permute-start | bytes 172040 | tf_op jit(solution)/shard_map/ppermute | solution.py:544
  53.5 8.8 %collective-permute-start.11 = (bf16[2,112,128]{2,1,0:T(8,128)(2,1)S(1)}, bf16[2,112,128]{2,1,0:T(8,128)(2,1)S(1)}, u32[]{:S(2)}, u32[]{:S(2)}) collective-permute-start(bf16[2,112,128]{2,1,0:T(8,128)(2,1)S(1)} %shard_map.93.refs_0_), channel_id=1, source_target_pairs={{0,192},{32,96},{64,0},{96,160},{128,64},{160,224},{192,128},{224,... | collective-permute-start | bytes 172040 | tf_op jit(solution)/shard_map/ppermute | solution.py:544
  58.0 5.4 %collective-permute-start.10 = (bf16[2,112,128]{2,1,0:T(8,128)(2,1)S(1)}, bf16[2,112,128]{2,1,0:T(8,128)(2,1)S(1)}, u32[]{:S(2)}, u32[]{:S(2)}) collective-permute-start(bf16[2,112,128]{2,1,0:T(8,128)(2,1)S(1)} %shard_map.93.refs_0_), channel_id=1, source_target_pairs={{0,224},{32,64},{64,32},{96,128},{128,96},{160,192},{192,160},{224... | collective-permute-start | bytes 172040 | tf_op jit(solution)/shard_map/ppermute | solution.py:544

commit v8 on v7

--- a/solution.py
+++ b/solution.py
@@ -593,7 +593,7 @@
             frame_shape(4, F32),
             pltpu.SemaphoreType.DMA((2,)),
         ],
-        flops=CONV_FLOPS * 5 // 2,
+        flops=CONV_FLOPS * 2,
         limit=24,
     )
     tail, head, local = lax.optimization_barrier((tail, head, local))

time: 65 us -> 63 us (0.969)
  waiting for transfers between devices: 7.9 us -> 6.77 us
  starting transfers between devices: 25.1 us -> 24.4 us
    ppermute x6, waiting for transfers between devices: 2.84 us -> 1.73 us  [seq_permute(): lax.ppermute(value, 'seq', [(source, target(source) % 8) for source in ra...]
    ppermute x6, starting transfers between devices: 14.1 us -> 13.3 us  [seq_permute(): lax.ppermute(value, 'seq', [(source, target(source) % 8) for source in ra...]
  transfers between devices with their start and end apart: 13 -> 13, of which waited for: 5 -> 4; matrix products, arithmetic and copies ran while one was open for 0% -> 0% of each run, Pallas kernels for 34% -> 35%
where the time goes in v8:
time: 63 us; the launch traced here: 62.2 us
  Pallas kernels  30.3 us (48%)
  starting transfers between devices  24.4 us (39%)
  waiting for transfers between devices  6.77 us (11%)
  between operations  0.73 us (1%)
    pallas_call x12, Pallas kernels, call(): pl.pallas_call(kernel, out_shape=[jax.ShapeDtypeStruct(shape, dtype) for...  30.3 us
    ppermute x6, starting transfers between devices, seq_permute(): lax.ppermute(value, 'seq', [(source, target(source) % 8) for source in ra...  13.3 us
    ppermute x7, starting transfers between devices, dp_permute(): lax.ppermute(value, 'dp', [(source, target(source)) for source in range(3...  11 us
    ppermute x7, waiting for transfers between devices, dp_permute(): lax.ppermute(value, 'dp', [(source, target(source)) for source in range(3...  5.05 us
    ppermute x6, waiting for transfers between devices, seq_permute(): lax.ppermute(value, 'seq', [(source, target(source) % 8) for source in ra...  1.73 us
  transfers between devices with their start and end apart: 13, of which 4 were waited for; matrix products, arithmetic and copies ran while one was open for 0% of the time, Pallas kernels for 35%

profile of v8, /device:TPU:2, one launch (start us, length us, event | category | flops | bytes accessed | tf_op | source)
XLA Modules:
  0.0 62.2 jit_solution(16678285560249695462)
XLA Ops:
  0.6 1.6 %shard_map.84 = (s32[1,64]{1,0:T(1,128)S(1)}, bf16[4,256,128]{2,1,0:T(8,128)(2,1)S(1)}, bf16[6,256,128]{2,1,0:T(8,128)(2,1)S(1)}, bf16[3456,128]{1,0:T(8,128)(2,1)S(1)}, bf16[9,256,128]{2,1,0:T(8,128)(2,1)S(1)}) custom-call(s32[1,64]{1,0:T(1,128)} %clips.1, bf16[8,256,128]{2,1,0:T(8,128)(2,1)} %bitcast.4, bf16[8,256,128]{2,1,0:T(8,128)(2,1)} %bitcast.5, ...), custom_call_target="tpu_custom_call" | custom-call | bytes 1048576 | tf_op jit(solution)/shard_map/pallas_call | solution.py:502
  2.2 5.9 %collective-permute-start.1 = (bf16[6,256,128]{2,1,0:T(8,128)(2,1)S(1)}, bf16[6,256,128]{2,1,0:T(8,128)(2,1)S(1)}, u32[]{:S(2)}, u32[]{:S(2)}) collective-permute-start(bf16[6,256,128]{2,1,0:T(8,128)(2,1)S(1)} %get-tuple-element.82), channel_id=1, source_target_pairs={{0,224},{32,0},{64,32},{96,64},{128,96},{160,128},{192,160},{224,1... | collective-permute-start | bytes 1179656 | tf_op jit(solution)/shard_map/ppermute | solution.py:544
  8.1 0.0 collective-permute-start
  8.1 9.2 %shard_map.85 = (bf16[9,256,128]{2,1,0:T(8,128)(2,1)S(1)}, bf16[3456,128]{1,0:T(8,128)(2,1)S(1)}, bf16[1152,384]{1,0:T(8,128)(2,1)S(1)}, bf16[1152,384]{1,0:T(8,...) custom-call(s32[1,64]{1,0:T(1,128)S(1)} %get-tuple-element.79.clips,, ...), custom_call_target="tpu_custom_call" | custom-call | flops 3623878656 | bytes 1048576 | tf_op jit(solution)/shard_map/pallas_call | solution.py:502
  17.4 0.0 collective-permute-done.tail
  17.4 0.0 collective-permute-done.1.head
  17.4 5.7 %shard_map.86 = (bf16[8,256,128]{2,1,0:T(8,128)(2,1)S(1)}, bf16[8,256,128]{2,1,0:T(8,128)(2,1)S(1)}, f32[2,16,112,128]{3,2,1,0:T(8,128)S(1)}, bf16[2,16,112,128]{3,2,1,0:T(8,128)(2,1)S(1)}) custom-call(s32[1,64]{1,0:T(1,128)S(1)} %get-tuple-element.79.clips, bf16[9,256,128]{2,1,0:T(8,128)(2,1)S(1)} %get-tuple-element.80.window.frames, ...), custom_call_target="tpu_custom_call" | custom-call | flops 2717908992 | bytes 1048576 | tf_op jit(solution)/shard_map/pallas_call | solution.py:502
  23.1 0.3 collective-permute-start.2
  23.4 2.5 %collective-permute-done.2.part = bf16[2,16,112,128]{3,2,1,0:T(8,128)(2,1)S(1)} collective-permute-done((bf16[2,16,112,128]{3,2,1,0:T(8,128)(2,1)S(1)}, bf16[2,16,112,128]{3,2,1,0:T(8,128)(2,1)S(1)}, u32[]{:S(2)}, u32[]{:S(2)}) %collective-permute-start.2) | collective-permute-done | bytes 917536 | tf_op jit(solution)/shard_map/ppermute | solution.py:528
  25.8 0.2 shard_map.87
  26.0 2.2 %collective-permute-start.3 = (bf16[2,4,112,128]{3,2,1,0:T(8,128)(2,1)S(1)}, bf16[2,4,112,128]{3,2,1,0:T(8,128)(2,1)S(1)}, u32[]{:S(2)}, u32[]{:S(2)}) collective-permute-start(bf16[2,4,112,128]{3,2,1,0:T(8,128)(2,1)S(1)} %get-tuple-element.118), channel_id=1, source_target_pairs={{0,4},{1,17},{2,6},{3,19},{4,0},{5,21},{6,2},{7,23},{8,12},{9,25},... | collective-permute-start | bytes 688136 | tf_op jit(solution)/shard_map/ppermute | solution.py:528
  28.3 0.0 collective-permute-start.4
  28.3 2.0 %collective-permute-start.5 = (bf16[2,4,112,128]{3,2,1,0:T(8,128)(2,1)S(1)}, bf16[2,4,112,128]{3,2,1,0:T(8,128)(2,1)S(1)}, u32[]{:S(2)}, u32[]{:S(2)}) collective-permute-start(bf16[2,4,112,128]{3,2,1,0:T(8,128)(2,1)S(1)} %get-tuple-element.120), channel_id=1, source_target_pairs={{0,6},{1,25},{2,0},{3,27},{4,2},{5,29},{6,4},{7,31},{8,14},{9,1},{... | collective-permute-start | bytes 688136 | tf_op jit(solution)/shard_map/ppermute | solution.py:528
  30.3 3.3 %shard_map.88 = (bf16[4,256,128]{2,1,0:T(8,128)(2,1)S(1)}, bf16[1152,384]{1,0:T(8,128)(2,1)S(1)}) custom-call(s32[1,64]{1,0:T(1,128)S(1)} %get-tuple-element.79.clips, bf16[8,256,128]{2,1,0:T(8,128)(2,1)S(1)} %get-tuple-element.121.hidden_in, bf16[9,256,128]{2,1,0:T(8,128)(2,1)S(1)} %get-tuple-element.80.window.frames, ...), custom_call_target="tpu_custom_call" | custom-call | flops 1358954496 | bytes 1048576 | tf_op jit(solution)/shard_map/pallas_call | solution.py:502
  33.6 0.1 collective-permute-done.3.refs_0_
  33.7 2.4 %collective-permute-done.4.refs_1_ = bf16[2,4,112,128]{3,2,1,0:T(8,128)(2,1)S(1)} collective-permute-done((bf16[2,4,112,128]{3,2,1,0:T(8,128)(2,1)S(1)}, bf16[2,4,112,128]{3,2,1,0:T(8,128)(2,1)S(1)}, u32[]{:S(2)}, u32[]{:S(2)}) %collective-permute-start.4) | collective-permute-done | bytes 229408 | tf_op jit(solution)/shard_map/ppermute | solution.py:528
  36.2 0.0 collective-permute-done.5.refs_2_
  36.2 0.1 shard_map.89
  36.3 3.3 %collective-permute-start.6 = (bf16[2,112,128]{2,1,0:T(8,128)(2,1)S(1)}, bf16[2,112,128]{2,1,0:T(8,128)(2,1)S(1)}, u32[]{:S(2)}, u32[]{:S(2)}) collective-permute-start(bf16[2,112,128]{2,1,0:T(8,128)(2,1)S(1)} %get-tuple-element.131), channel_id=1, source_target_pairs={{0,16},{1,5},{2,18},{3,7},{4,20},{5,1},{6,22},{7,3},{8,24},{9,13},... | collective-permute-start | bytes 172040 | tf_op jit(solution)/shard_map/ppermute | solution.py:528
  39.6 0.7 %collective-permute-start.7 = (bf16[2,112,128]{2,1,0:T(8,128)(2,1)S(1)}, bf16[2,112,128]{2,1,0:T(8,128)(2,1)S(1)}, u32[]{:S(2)}, u32[]{:S(2)}) collective-permute-start(bf16[2,112,128]{2,1,0:T(8,128)(2,1)S(1)} %get-tuple-element.132), channel_id=1, source_target_pairs={{0,8},{1,3},{2,10},{3,5},{4,12},{5,7},{6,14},{7,1},{8,16},{9,11},{... | collective-permute-start | bytes 172040 | tf_op jit(solution)/shard_map/ppermute | solution.py:528
  40.2 2.6 %collective-permute-start.8 = (bf16[2,112,128]{2,1,0:T(8,128)(2,1)S(1)}, bf16[2,112,128]{2,1,0:T(8,128)(2,1)S(1)}, u32[]{:S(2)}, u32[]{:S(2)}) collective-permute-start(bf16[2,112,128]{2,1,0:T(8,128)(2,1)S(1)} %get-tuple-element.133), channel_id=1, source_target_pairs={{0,24},{1,7},{2,26},{3,1},{4,28},{5,3},{6,30},{7,5},{8,0},{9,15},{... | collective-permute-start | bytes 172040 | tf_op jit(solution)/shard_map/ppermute | solution.py:528
  42.8 2.8 %shard_map.90 = bf16[8,256,128]{2,1,0:T(8,128)(2,1)} custom-call(s32[1,64]{1,0:T(1,128)S(1)} %get-tuple-element.79.clips, bf16[8,256,128]{2,1,0:T(8,128)(2,1)S(1)} %get-tuple-element.121.hidden_in, bf16[9,256,128]{2,1,0:T(8,128)(2,1)S(1)} %get-tuple-element.80.window.frames, bf16[1152,384]{1,0:T(8,128)(2,1)S(1)} %get-tuple-element.134.weight, ...), custom_call_target="tpu_custom_call" | custom-call | flops 905969664 | bytes 1048576 | tf_op jit(solution)/shard_map/pallas_call | solution.py:502
  45.6 0.0 collective-permute-done.6.refs_0_
  45.6 0.0 collective-permute-done.7.refs_1_
  45.6 0.0 collective-permute-done.8.refs_2_
  45.7 0.1 collective-permute-start.9
  45.8 2.4 %shard_map.92.next_in = bf16[2,256,128]{2,1,0:T(8,128)(2,1)S(1)} custom-call(s32[1,64]{1,0:T(1,128)S(1)} %get-tuple-element.79.clips, bf16[9,256,128]{2,1,0:T(8,128)(2,1)S(1)} %get-tuple-element.80.window.frames, bf16[6,256,128]{2,1,0:T(8,128)(2,1)S(1)} %collective-permute-done.1.head, bf16[1152,384]{1,0:T(8,128)(2,1)S(1)} %get-tuple-element.100.conv_weight, ...), custom_call_target="tpu_custom_call" | custom-call | flops 905969664 | bytes 1048576 | tf_op jit(solution)/shard_map/pallas_call | solution.py:502
  48.2 1.7 %collective-permute-done.9.refs_0_ = bf16[2,112,128]{2,1,0:T(8,128)(2,1)S(1)} collective-permute-done((bf16[2,112,128]{2,1,0:T(8,128)(2,1)S(1)}, bf16[2,112,128]{2,1,0:T(8,128)(2,1)S(1)}, u32[]{:S(2)}, u32[]{:S(2)}) %collective-permute-start.9) | collective-permute-done | bytes 57376 | tf_op jit(solution)/shard_map/ppermute | solution.py:544
  50.0 3.0 %collective-permute-start.12 = (bf16[2,112,128]{2,1,0:T(8,128)(2,1)S(1)}, bf16[2,112,128]{2,1,0:T(8,128)(2,1)S(1)}, u32[]{:S(2)}, u32[]{:S(2)}) collective-permute-start(bf16[2,112,128]{2,1,0:T(8,128)(2,1)S(1)} %shard_map.93.refs_0_), channel_id=1, source_target_pairs={{0,160},{32,128},{64,224},{96,192},{128,32},{160,0},{192,96},{224,... | collective-permute-start | bytes 172040 | tf_op jit(solution)/shard_map/ppermute | solution.py:544
  53.0 1.8 %collective-permute-start.11 = (bf16[2,112,128]{2,1,0:T(8,128)(2,1)S(1)}, bf16[2,112,128]{2,1,0:T(8,128)(2,1)S(1)}, u32[]{:S(2)}, u32[]{:S(2)}) collective-permute-start(bf16[2,112,128]{2,1,0:T(8,128)(2,1)S(1)} %shard_map.93.refs_0_), channel_id=1, source_target_pairs={{0,192},{32,96},{64,0},{96,160},{128,64},{160,224},{192,128},{224,... | collective-permute-start | bytes 172040 | tf_op jit(solution)/shard_map/ppermute | solution.py:544
  54.8 2.5 %collective-permute-start.10 = (bf16[2,112,128]{2,1,0:T(8,128)(2,1)S(1)}, bf16[2,112,128]{2,1,0:T(8,128)(2,1)S(1)}, u32[]{:S(2)}, u32[]{:S(2)}) collective-permute-start(bf16[2,112,128]{2,1,0:T(8,128)(2,1)S(1)} %shard_map.93.refs_0_), channel_id=1, source_target_pairs={{0,224},{32,64},{64,32},{96,128},{128,96},{160,192},{192,160},{224... | collective-permute-start | bytes 172040 | tf_op jit(solution)/shard_map/ppermute | solution.py:544
  57.3 4.3 %shard_map.94 = bf16[8,256,128]{2,1,0:T(8,128)(2,1)} custom-call(s32[1,64]{1,0:T(1,128)S(1)} %get-tuple-element.79.clips, bf16[8,256,128]{2,1,0:T(8,128)(2,1)S(1)} %get-tuple-element.146.act_grad_in, bf16[2,256,128]{2,1,0:T(8,128)(2,1)S(1)} %shard_map.92.next_in, bf16[9,256,128]{2,1,0:T(8,128)(2,1)S(1)} %get-tuple-element.97.cot, ...), custom_call_target="tpu_custom_call" | custom-call | flops 1811939328 | bytes 1048576 | tf_op jit(solution)/shard_map/pallas_call | solution.py:502
  61.5 0.0 collective-permute-done.12.refs_3_
  61.5 0.0 collective-permute-done.11.refs_2_
  61.6 0.0 collective-permute-done.10.refs_1_
  61.6 0.7 %shard_map.95 = (f32[108,128]{1,0:T(8,128)}, f32[108,128]{1,0:T(8,128)}) custom-call(bf16[2,112,128]{2,1,0:T(8,128)(2,1)S(1)} %shard_map.93.refs_0_, bf16[2,112,128]{2,1,0:T(8,128)(2,1)S(1)} %collective-permute-done.10.refs_1_, bf16[2,112,128]{2,1,0:T(8,128)(2,1)S(1)} %collective-permute-done.11.refs_2_, bf16[2,112,128]{2,1,0:T(8,128)(2,1)S(1)} %collective-permute-done.12.refs_3_), custom_call_target="tpu_custom_call" | custom-call | bytes 1048576 | tf_op jit(solution)/shard_map/pallas_call | solution.py:502
  (2 shorter events, 0.0 us)
Async XLA Ops:
  2.2 15.2 %collective-permute-start.1 = (bf16[6,256,128]{2,1,0:T(8,128)(2,1)S(1)}, bf16[6,256,128]{2,1,0:T(8,128)(2,1)S(1)}, u32[]{:S(2)}, u32[]{:S(2)}) collective-permute-start(bf16[6,256,128]{2,1,0:T(8,128)(2,1)S(1)} %get-tuple-element.82), channel_id=1, source_target_pairs={{0,224},{32,0},{64,32},{96,64},{128,96},{160,128},{192,160},{224,1... | collective-permute-start | bytes 1179656 | tf_op jit(solution)/shard_map/ppermute | solution.py:544
  8.1 9.2 %collective-permute-start = (bf16[4,256,128]{2,1,0:T(8,128)(2,1)S(1)}, bf16[4,256,128]{2,1,0:T(8,128)(2,1)S(1)}, u32[]{:S(2)}, u32[]{:S(2)}) collective-permute-start(bf16[4,256,128]{2,1,0:T(8,128)(2,1)S(1)} %get-tuple-element.81), channel_id=1, source_target_pairs={{0,32},{32,64},{64,96},{96,128},{128,160},{160,192},{192,224},{224... | collective-permute-start | bytes 786440 | tf_op jit(solution)/shard_map/ppermute | solution.py:544
  23.1 2.7 %collective-permute-start.2 = (bf16[2,16,112,128]{3,2,1,0:T(8,128)(2,1)S(1)}, bf16[2,16,112,128]{3,2,1,0:T(8,128)(2,1)S(1)}, u32[]{:S(2)}, u32[]{:S(2)}) collective-permute-start(bf16[2,16,112,128]{3,2,1,0:T(8,128)(2,1)S(1)} %get-tuple-element.112), channel_id=1, source_target_pairs={{0,1},{1,0},{2,3},{3,2},{4,5},{5,4},{6,7},{7,6},{8,9},{9,8},{10,11... | collective-permute-start | bytes 2752520 | tf_op jit(solution)/shard_map/ppermute | solution.py:528
  26.0 7.7 %collective-permute-start.3 = (bf16[2,4,112,128]{3,2,1,0:T(8,128)(2,1)S(1)}, bf16[2,4,112,128]{3,2,1,0:T(8,128)(2,1)S(1)}, u32[]{:S(2)}, u32[]{:S(2)}) collective-permute-start(bf16[2,4,112,128]{3,2,1,0:T(8,128)(2,1)S(1)} %get-tuple-element.118), channel_id=1, source_target_pairs={{0,4},{1,17},{2,6},{3,19},{4,0},{5,21},{6,2},{7,23},{8,12},{9,25},... | collective-permute-start | bytes 688136 | tf_op jit(solution)/shard_map/ppermute | solution.py:528
  28.3 7.9 %collective-permute-start.4 = (bf16[2,4,112,128]{3,2,1,0:T(8,128)(2,1)S(1)}, bf16[2,4,112,128]{3,2,1,0:T(8,128)(2,1)S(1)}, u32[]{:S(2)}, u32[]{:S(2)}) collective-permute-start(bf16[2,4,112,128]{3,2,1,0:T(8,128)(2,1)S(1)} %get-tuple-element.119), channel_id=1, source_target_pairs={{0,2},{1,9},{2,4},{3,11},{4,6},{5,13},{6,0},{7,15},{8,10},{9,17},{... | collective-permute-start | bytes 688136 | tf_op jit(solution)/shard_map/ppermute | solution.py:528
  28.3 7.9 %collective-permute-start.5 = (bf16[2,4,112,128]{3,2,1,0:T(8,128)(2,1)S(1)}, bf16[2,4,112,128]{3,2,1,0:T(8,128)(2,1)S(1)}, u32[]{:S(2)}, u32[]{:S(2)}) collective-permute-start(bf16[2,4,112,128]{3,2,1,0:T(8,128)(2,1)S(1)} %get-tuple-element.120), channel_id=1, source_target_pairs={{0,6},{1,25},{2,0},{3,27},{4,2},{5,29},{6,4},{7,31},{8,14},{9,1},{... | collective-permute-start | bytes 688136 | tf_op jit(solution)/shard_map/ppermute | solution.py:528
  36.3 9.3 %collective-permute-start.6 = (bf16[2,112,128]{2,1,0:T(8,128)(2,1)S(1)}, bf16[2,112,128]{2,1,0:T(8,128)(2,1)S(1)}, u32[]{:S(2)}, u32[]{:S(2)}) collective-permute-start(bf16[2,112,128]{2,1,0:T(8,128)(2,1)S(1)} %get-tuple-element.131), channel_id=1, source_target_pairs={{0,16},{1,5},{2,18},{3,7},{4,20},{5,1},{6,22},{7,3},{8,24},{9,13},... | collective-permute-start | bytes 172040 | tf_op jit(solution)/shard_map/ppermute | solution.py:528
  39.6 6.1 %collective-permute-start.7 = (bf16[2,112,128]{2,1,0:T(8,128)(2,1)S(1)}, bf16[2,112,128]{2,1,0:T(8,128)(2,1)S(1)}, u32[]{:S(2)}, u32[]{:S(2)}) collective-permute-start(bf16[2,112,128]{2,1,0:T(8,128)(2,1)S(1)} %get-tuple-element.132), channel_id=1, source_target_pairs={{0,8},{1,3},{2,10},{3,5},{4,12},{5,7},{6,14},{7,1},{8,16},{9,11},{... | collective-permute-start | bytes 172040 | tf_op jit(solution)/shard_map/ppermute | solution.py:528
  40.2 5.4 %collective-permute-start.8 = (bf16[2,112,128]{2,1,0:T(8,128)(2,1)S(1)}, bf16[2,112,128]{2,1,0:T(8,128)(2,1)S(1)}, u32[]{:S(2)}, u32[]{:S(2)}) collective-permute-start(bf16[2,112,128]{2,1,0:T(8,128)(2,1)S(1)} %get-tuple-element.133), channel_id=1, source_target_pairs={{0,24},{1,7},{2,26},{3,1},{4,28},{5,3},{6,30},{7,5},{8,0},{9,15},{... | collective-permute-start | bytes 172040 | tf_op jit(solution)/shard_map/ppermute | solution.py:528
  45.7 4.3 %collective-permute-start.9 = (bf16[2,112,128]{2,1,0:T(8,128)(2,1)S(1)}, bf16[2,112,128]{2,1,0:T(8,128)(2,1)S(1)}, u32[]{:S(2)}, u32[]{:S(2)}) collective-permute-start(bf16[2,112,128]{2,1,0:T(8,128)(2,1)S(1)} %shard_map.91.keep_ref), channel_id=1, source_target_pairs={{0,32},{32,0},{64,96},{96,64},{128,160},{160,128},{192,224},{224,1... | collective-permute-start | bytes 172040 | tf_op jit(solution)/shard_map/ppermute | solution.py:544
  50.0 11.6 %collective-permute-start.12 = (bf16[2,112,128]{2,1,0:T(8,128)(2,1)S(1)}, bf16[2,112,128]{2,1,0:T(8,128)(2,1)S(1)}, u32[]{:S(2)}, u32[]{:S(2)}) collective-permute-start(bf16[2,112,128]{2,1,0:T(8,128)(2,1)S(1)} %shard_map.93.refs_0_), channel_id=1, source_target_pairs={{0,160},{32,128},{64,224},{96,192},{128,32},{160,0},{192,96},{224,... | collective-permute-start | bytes 172040 | tf_op jit(solution)/shard_map/ppermute | solution.py:544
  53.0 8.6 %collective-permute-start.11 = (bf16[2,112,128]{2,1,0:T(8,128)(2,1)S(1)}, bf16[2,112,128]{2,1,0:T(8,128)(2,1)S(1)}, u32[]{:S(2)}, u32[]{:S(2)}) collective-permute-start(bf16[2,112,128]{2,1,0:T(8,128)(2,1)S(1)} %shard_map.93.refs_0_), channel_id=1, source_target_pairs={{0,192},{32,96},{64,0},{96,160},{128,64},{160,224},{192,128},{224,... | collective-permute-start | bytes 172040 | tf_op jit(solution)/shard_map/ppermute | solution.py:544
  54.8 6.8 %collective-permute-start.10 = (bf16[2,112,128]{2,1,0:T(8,128)(2,1)S(1)}, bf16[2,112,128]{2,1,0:T(8,128)(2,1)S(1)}, u32[]{:S(2)}, u32[]{:S(2)}) collective-permute-start(bf16[2,112,128]{2,1,0:T(8,128)(2,1)S(1)} %shard_map.93.refs_0_), channel_id=1, source_target_pairs={{0,224},{32,64},{64,32},{96,128},{128,96},{160,192},{192,160},{224... | collective-permute-start | bytes 172040 | tf_op jit(solution)/shard_map/ppermute | solution.py:544

commit v9 on v8

--- a/solution.py
+++ b/solution.py
@@ -425,17 +425,25 @@
         out_ref[t] = rounded
 
 
-def backward_kernel(clips, act_grad_in, next_in, cot, weight1, out_ref, act_grad, weight):
+def adjoint_frames(clips, cot, act_grad, weight, out_ref, start):
     first = first_frame()
-    for f in range(F):
-        act_grad[f] = act_grad_in[f]
-    for f in range(2):
-        act_grad[F + f] = next_in[f]
-    act_grad[F + 2] = jnp.zeros((POS, C), BF16)
+    for t in range(HALF):
+        slots = next_slots(clips, first, start + t, -start, HALF + 2)
+        out = conv_frame(act_grad, slots, weight)
+        out_ref[start + t] = (cot[start + t].astype(F32) + out).astype(BF16)
+
+
+def backward_kernel(clips, act_grad_in, cot, weight1, out_ref, weight, act_grad):
+    fill(act_grad, [act_grad_in.at[: HALF + 2]])
     adjoint_weight(weight1, weight)
-    for t in range(F):
-        out = conv_frame(act_grad, next_slots(clips, first, t, 0, F + 2), weight)
-        out_ref[t] = (cot[t].astype(F32) + out).astype(BF16)
+    adjoint_frames(clips, cot, act_grad, weight, out_ref, 0)
+
+
+def last_half_kernel(clips, act_grad_in, next_in, cot, weight, half, out_ref, act_grad):
+    fill(act_grad, [act_grad_in.at[HALF:], next_in])
+    for t in range(HALF):
+        out_ref[t] = half[t]
+    adjoint_frames(clips, cot, act_grad, weight, out_ref, HALF)
 
 
 STEPS = (2, 1, 3)
@@ -622,6 +630,17 @@
         limit=28,
     )
     recv = dp_permute(send, lambda d: d ^ 1)
+    act_grad, keep = lax.optimization_barrier((act_grad, keep))
+    half_grad, wide_adjoint = call(
+        backward_kernel,
+        (clip_ids, act_grad, cot_copy, weight1),
+        [SMEM] + [VMEM] * 3,
+        [frame_shape(HALF), WIDE],
+        [frame_shape(HALF + 3)],
+        flops=CONV_FLOPS // 2,
+        limit=8,
+    )
+    recv, half_grad = lax.optimization_barrier((recv, half_grad))
     keep, *sent = call(
         first_kernel,
         (keep, recv),
@@ -679,12 +698,12 @@
         seq_permute(total, lambda z, s=s: z + s if z % 2 else z - s) for s in (1, 2, 3)
     ]
     (input_grad,) = call(
-        backward_kernel,
-        (clip_ids, act_grad, act_grad_next, cot_copy, weight1),
-        [SMEM] + [VMEM] * 4,
+        last_half_kernel,
+        (clip_ids, act_grad, act_grad_next, cot_copy, wide_adjoint, half_grad),
+        [SMEM] + [VMEM] * 5,
         [frame_shape(F)],
-        [frame_shape(F + 3), WIDE],
-        flops=CONV_FLOPS,
+        [frame_shape(HALF + 3)],
+        flops=CONV_FLOPS // 2,
         limit=8,
     )
     others, input_grad = lax.optimization_barrier((others, input_grad))

time: 63 us -> 61.8 us (0.981)
  waiting for transfers between devices: 6.77 us -> 5.26 us
  Pallas kernels: 30.3 us -> 31 us
    ppermute x7, waiting for transfers between devices: 5.05 us -> 2.9 us  [dp_permute(): lax.ppermute(value, 'dp', [(source, target(source)) for source in range(3...]
    pallas_call x12 -> x13, Pallas kernels: 30.3 us -> 31 us  [call(): pl.pallas_call(kernel, out_shape=[jax.ShapeDtypeStruct(shape, dtype) for...]
    ppermute x6, waiting for transfers between devices: 1.73 us -> 2.36 us  [seq_permute(): lax.ppermute(value, 'seq', [(source, target(source) % 8) for source in ra...]
  transfers between devices with their start and end apart: 13 -> 13, of which waited for: 4 -> 5; matrix products, arithmetic and copies ran while one was open for 0% -> 0% of each run, Pallas kernels for 35% -> 37%
where the time goes in v9:
time: 61.8 us; the launch traced here: 61 us
  Pallas kernels  31 us (50%)
  starting transfers between devices  24 us (39%)
  waiting for transfers between devices  5.26 us (9%)
  between operations  0.74 us (1%)
    pallas_call x13, Pallas kernels, call(): pl.pallas_call(kernel, out_shape=[jax.ShapeDtypeStruct(shape, dtype) for...  31 us
    ppermute x6, starting transfers between devices, seq_permute(): lax.ppermute(value, 'seq', [(source, target(source) % 8) for source in ra...  12.9 us
    ppermute x7, starting transfers between devices, dp_permute(): lax.ppermute(value, 'dp', [(source, target(source)) for source in range(3...  11 us
    ppermute x7, waiting for transfers between devices, dp_permute(): lax.ppermute(value, 'dp', [(source, target(source)) for source in range(3...  2.9 us
    ppermute x6, waiting for transfers between devices, seq_permute(): lax.ppermute(value, 'seq', [(source, target(source) % 8) for source in ra...  2.36 us
  transfers between devices with their start and end apart: 13, of which 5 were waited for; matrix products, arithmetic and copies ran while one was open for 0% of the time, Pallas kernels for 37%

profile of v9, /device:TPU:2, one launch (start us, length us, event | category | flops | bytes accessed | tf_op | source)
XLA Modules:
  0.0 61.0 jit_solution(7359368833947339030)
XLA Ops:
  0.6 1.6 %shard_map.84 = (s32[1,64]{1,0:T(1,128)S(1)}, bf16[4,256,128]{2,1,0:T(8,128)(2,1)S(1)}, bf16[6,256,128]{2,1,0:T(8,128)(2,1)S(1)}, bf16[3456,128]{1,0:T(8,128)(2,1)S(1)}, bf16[9,256,128]{2,1,0:T(8,128)(2,1)S(1)}) custom-call(s32[1,64]{1,0:T(1,128)} %clips.1, bf16[8,256,128]{2,1,0:T(8,128)(2,1)} %bitcast.4, bf16[8,256,128]{2,1,0:T(8,128)(2,1)} %bitcast.5, ...), custom_call_target="tpu_custom_call" | custom-call | bytes 1048576 | tf_op jit(solution)/shard_map/pallas_call | solution.py:510
  2.2 5.9 %collective-permute-start.1 = (bf16[6,256,128]{2,1,0:T(8,128)(2,1)S(1)}, bf16[6,256,128]{2,1,0:T(8,128)(2,1)S(1)}, u32[]{:S(2)}, u32[]{:S(2)}) collective-permute-start(bf16[6,256,128]{2,1,0:T(8,128)(2,1)S(1)} %get-tuple-element.88), channel_id=1, source_target_pairs={{0,224},{32,0},{64,32},{96,64},{128,96},{160,128},{192,160},{224,1... | collective-permute-start | bytes 1179656 | tf_op jit(solution)/shard_map/ppermute | solution.py:552
  8.1 0.0 collective-permute-start
  8.1 9.2 %shard_map.85 = (bf16[9,256,128]{2,1,0:T(8,128)(2,1)S(1)}, bf16[3456,128]{1,0:T(8,128)(2,1)S(1)}, bf16[1152,384]{1,0:T(8,128)(2,1)S(1)}, bf16[1152,384]{1,0:T(8,...) custom-call(s32[1,64]{1,0:T(1,128)S(1)} %get-tuple-element.85.clips,, ...), custom_call_target="tpu_custom_call" | custom-call | flops 3623878656 | bytes 1048576 | tf_op jit(solution)/shard_map/pallas_call | solution.py:510
  17.3 0.0 collective-permute-done.tail
  17.4 0.0 collective-permute-done.1.head
  17.4 5.7 %shard_map.86 = (bf16[8,256,128]{2,1,0:T(8,128)(2,1)S(1)}, bf16[8,256,128]{2,1,0:T(8,128)(2,1)S(1)}, f32[2,16,112,128]{3,2,1,0:T(8,128)S(1)}, bf16[2,16,112,128]{3,2,1,0:T(8,128)(2,1)S(1)}) custom-call(s32[1,64]{1,0:T(1,128)S(1)} %get-tuple-element.85.clips, bf16[9,256,128]{2,1,0:T(8,128)(2,1)S(1)} %get-tuple-element.86.window.frames, ...), custom_call_target="tpu_custom_call" | custom-call | flops 2717908992 | bytes 1048576 | tf_op jit(solution)/shard_map/pallas_call | solution.py:510
  23.1 0.3 collective-permute-start.2
  23.4 2.2 %shard_map.87 = (bf16[4,256,128]{2,1,0:T(8,128)(2,1)S(1)}, bf16[1152,384]{1,0:T(8,128)(2,1)S(1)}) custom-call(s32[1,64]{1,0:T(1,128)S(1)} %get-tuple-element.85.clips, bf16[8,256,128]{2,1,0:T(8,128)(2,1)S(1)} %get-tuple-element.156.act_grad_in, bf16[9,256,128]{2,1,0:T(8,128)(2,1)S(1)} %get-tuple-element.103.cot, bf16[3456,128]{1,0:T(8,128)(2,1)S(1)} %get-tuple-element.89.weight1), custom_call_target="tpu_custom_call" | custom-call | flops 905969664 | bytes 1048576 | tf_op jit(solution)/shard_map/pallas_call | solution.py:510
  25.6 0.3 collective-permute-done.2.part
  25.8 0.2 shard_map.88
  26.0 2.2 %collective-permute-start.3 = (bf16[2,4,112,128]{3,2,1,0:T(8,128)(2,1)S(1)}, bf16[2,4,112,128]{3,2,1,0:T(8,128)(2,1)S(1)}, u32[]{:S(2)}, u32[]{:S(2)}) collective-permute-start(bf16[2,4,112,128]{3,2,1,0:T(8,128)(2,1)S(1)} %get-tuple-element.129), channel_id=1, source_target_pairs={{0,4},{1,17},{2,6},{3,19},{4,0},{5,21},{6,2},{7,23},{8,12},{9,25},... | collective-permute-start | bytes 688136 | tf_op jit(solution)/shard_map/ppermute | solution.py:536
  28.2 0.0 collective-permute-start.4
  28.2 2.0 %collective-permute-start.5 = (bf16[2,4,112,128]{3,2,1,0:T(8,128)(2,1)S(1)}, bf16[2,4,112,128]{3,2,1,0:T(8,128)(2,1)S(1)}, u32[]{:S(2)}, u32[]{:S(2)}) collective-permute-start(bf16[2,4,112,128]{3,2,1,0:T(8,128)(2,1)S(1)} %get-tuple-element.131), channel_id=1, source_target_pairs={{0,6},{1,25},{2,0},{3,27},{4,2},{5,29},{6,4},{7,31},{8,14},{9,1},{... | collective-permute-start | bytes 688136 | tf_op jit(solution)/shard_map/ppermute | solution.py:536
  30.3 3.3 %shard_map.89 = (bf16[4,256,128]{2,1,0:T(8,128)(2,1)S(1)}, bf16[1152,384]{1,0:T(8,128)(2,1)S(1)}) custom-call(s32[1,64]{1,0:T(1,128)S(1)} %get-tuple-element.85.clips, bf16[8,256,128]{2,1,0:T(8,128)(2,1)S(1)} %get-tuple-element.132.hidden_in, bf16[9,256,128]{2,1,0:T(8,128)(2,1)S(1)} %get-tuple-element.86.window.frames, ...), custom_call_target="tpu_custom_call" | custom-call | flops 1358954496 | bytes 1048576 | tf_op jit(solution)/shard_map/pallas_call | solution.py:510
  33.6 0.2 collective-permute-done.3.refs_0_
  33.7 2.5 %collective-permute-done.4.refs_1_ = bf16[2,4,112,128]{3,2,1,0:T(8,128)(2,1)S(1)} collective-permute-done((bf16[2,4,112,128]{3,2,1,0:T(8,128)(2,1)S(1)}, bf16[2,4,112,128]{3,2,1,0:T(8,128)(2,1)S(1)}, u32[]{:S(2)}, u32[]{:S(2)}) %collective-permute-start.4) | collective-permute-done | bytes 229408 | tf_op jit(solution)/shard_map/ppermute | solution.py:536
  36.2 0.0 collective-permute-done.5.refs_2_
  36.2 0.1 shard_map.90
  36.3 3.3 %collective-permute-start.6 = (bf16[2,112,128]{2,1,0:T(8,128)(2,1)S(1)}, bf16[2,112,128]{2,1,0:T(8,128)(2,1)S(1)}, u32[]{:S(2)}, u32[]{:S(2)}) collective-permute-start(bf16[2,112,128]{2,1,0:T(8,128)(2,1)S(1)} %get-tuple-element.142), channel_id=1, source_target_pairs={{0,16},{1,5},{2,18},{3,7},{4,20},{5,1},{6,22},{7,3},{8,24},{9,13},... | collective-permute-start | bytes 172040 | tf_op jit(solution)/shard_map/ppermute | solution.py:536
  39.6 0.7 %collective-permute-start.7 = (bf16[2,112,128]{2,1,0:T(8,128)(2,1)S(1)}, bf16[2,112,128]{2,1,0:T(8,128)(2,1)S(1)}, u32[]{:S(2)}, u32[]{:S(2)}) collective-permute-start(bf16[2,112,128]{2,1,0:T(8,128)(2,1)S(1)} %get-tuple-element.143), channel_id=1, source_target_pairs={{0,8},{1,3},{2,10},{3,5},{4,12},{5,7},{6,14},{7,1},{8,16},{9,11},{... | collective-permute-start | bytes 172040 | tf_op jit(solution)/shard_map/ppermute | solution.py:536
  40.3 2.6 %collective-permute-start.8 = (bf16[2,112,128]{2,1,0:T(8,128)(2,1)S(1)}, bf16[2,112,128]{2,1,0:T(8,128)(2,1)S(1)}, u32[]{:S(2)}, u32[]{:S(2)}) collective-permute-start(bf16[2,112,128]{2,1,0:T(8,128)(2,1)S(1)} %get-tuple-element.144), channel_id=1, source_target_pairs={{0,24},{1,7},{2,26},{3,1},{4,28},{5,3},{6,30},{7,5},{8,0},{9,15},{... | collective-permute-start | bytes 172040 | tf_op jit(solution)/shard_map/ppermute | solution.py:536
  42.8 2.8 %shard_map.91 = bf16[8,256,128]{2,1,0:T(8,128)(2,1)} custom-call(s32[1,64]{1,0:T(1,128)S(1)} %get-tuple-element.85.clips, bf16[8,256,128]{2,1,0:T(8,128)(2,1)S(1)} %get-tuple-element.132.hidden_in, bf16[9,256,128]{2,1,0:T(8,128)(2,1)S(1)} %get-tuple-element.86.window.frames, bf16[1152,384]{1,0:T(8,128)(2,1)S(1)} %get-tuple-element.145.weight, ...), custom_call_target="tpu_custom_call" | custom-call | flops 905969664 | bytes 1048576 | tf_op jit(solution)/shard_map/pallas_call | solution.py:510
  45.6 0.0 collective-permute-done.6.refs_0_
  45.6 0.0 collective-permute-done.7.refs_1_
  45.7 0.0 collective-permute-done.8.refs_2_
  45.7 0.1 collective-permute-start.9
  45.8 2.4 %shard_map.93.next_in = bf16[2,256,128]{2,1,0:T(8,128)(2,1)S(1)} custom-call(s32[1,64]{1,0:T(1,128)S(1)} %get-tuple-element.85.clips, bf16[9,256,128]{2,1,0:T(8,128)(2,1)S(1)} %get-tuple-element.86.window.frames, bf16[6,256,128]{2,1,0:T(8,128)(2,1)S(1)} %collective-permute-done.1.head, bf16[1152,384]{1,0:T(8,128)(2,1)S(1)} %get-tuple-element.106.conv_weight, ...), custom_call_target="tpu_custom_call" | custom-call | flops 905969664 | bytes 1048576 | tf_op jit(solution)/shard_map/pallas_call | solution.py:510
  48.2 1.7 %collective-permute-done.9.refs_0_ = bf16[2,112,128]{2,1,0:T(8,128)(2,1)S(1)} collective-permute-done((bf16[2,112,128]{2,1,0:T(8,128)(2,1)S(1)}, bf16[2,112,128]{2,1,0:T(8,128)(2,1)S(1)}, u32[]{:S(2)}, u32[]{:S(2)}) %collective-permute-start.9) | collective-permute-done | bytes 57376 | tf_op jit(solution)/shard_map/ppermute | solution.py:552
  50.0 3.2 %collective-permute-start.12 = (bf16[2,112,128]{2,1,0:T(8,128)(2,1)S(1)}, bf16[2,112,128]{2,1,0:T(8,128)(2,1)S(1)}, u32[]{:S(2)}, u32[]{:S(2)}) collective-permute-start(bf16[2,112,128]{2,1,0:T(8,128)(2,1)S(1)} %shard_map.94.refs_0_), channel_id=1, source_target_pairs={{0,160},{32,128},{64,224},{96,192},{128,32},{160,0},{192,96},{224,... | collective-permute-start | bytes 172040 | tf_op jit(solution)/shard_map/ppermute | solution.py:552
  53.2 1.8 %collective-permute-start.11 = (bf16[2,112,128]{2,1,0:T(8,128)(2,1)S(1)}, bf16[2,112,128]{2,1,0:T(8,128)(2,1)S(1)}, u32[]{:S(2)}, u32[]{:S(2)}) collective-permute-start(bf16[2,112,128]{2,1,0:T(8,128)(2,1)S(1)} %shard_map.94.refs_0_), channel_id=1, source_target_pairs={{0,192},{32,96},{64,0},{96,160},{128,64},{160,224},{192,128},{224,... | collective-permute-start | bytes 172040 | tf_op jit(solution)/shard_map/ppermute | solution.py:552
  55.0 1.9 %collective-permute-start.10 = (bf16[2,112,128]{2,1,0:T(8,128)(2,1)S(1)}, bf16[2,112,128]{2,1,0:T(8,128)(2,1)S(1)}, u32[]{:S(2)}, u32[]{:S(2)}) collective-permute-start(bf16[2,112,128]{2,1,0:T(8,128)(2,1)S(1)} %shard_map.94.refs_0_), channel_id=1, source_target_pairs={{0,224},{32,64},{64,32},{96,128},{128,96},{160,192},{192,160},{224... | collective-permute-start | bytes 172040 | tf_op jit(solution)/shard_map/ppermute | solution.py:552
  56.9 2.8 %shard_map.95 = bf16[8,256,128]{2,1,0:T(8,128)(2,1)} custom-call(s32[1,64]{1,0:T(1,128)S(1)} %get-tuple-element.85.clips, bf16[8,256,128]{2,1,0:T(8,128)(2,1)S(1)} %get-tuple-element.156.act_grad_in, bf16[2,256,128]{2,1,0:T(8,128)(2,1)S(1)} %shard_map.93.next_in, bf16[9,256,128]{2,1,0:T(8,128)(2,1)S(1)} %get-tuple-element.103.cot, ...), custom_call_target="tpu_custom_call" | custom-call | flops 905969664 | bytes 1048576 | tf_op jit(solution)/shard_map/pallas_call | solution.py:510
  59.7 0.0 collective-permute-done.12.refs_3_
  59.7 0.0 collective-permute-done.11.refs_2_
  59.7 0.6 %collective-permute-done.10.refs_1_ = bf16[2,112,128]{2,1,0:T(8,128)(2,1)S(1)} collective-permute-done((bf16[2,112,128]{2,1,0:T(8,128)(2,1)S(1)}, bf16[2,112,128]{2,1,0:T(8,128)(2,1)S(1)}, u32[]{:S(2)}, u32[]{:S(2)}) %collective-permute-start.10) | collective-permute-done | bytes 57376 | tf_op jit(solution)/shard_map/ppermute | solution.py:552
  60.4 0.7 %shard_map.96 = (f32[108,128]{1,0:T(8,128)}, f32[108,128]{1,0:T(8,128)}) custom-call(bf16[2,112,128]{2,1,0:T(8,128)(2,1)S(1)} %shard_map.94.refs_0_, bf16[2,112,128]{2,1,0:T(8,128)(2,1)S(1)} %collective-permute-done.10.refs_1_, bf16[2,112,128]{2,1,0:T(8,128)(2,1)S(1)} %collective-permute-done.11.refs_2_, bf16[2,112,128]{2,1,0:T(8,128)(2,1)S(1)} %collective-permute-done.12.refs_3_), custom_call_target="tpu_custom_call" | custom-call | bytes 1048576 | tf_op jit(solution)/shard_map/pallas_call | solution.py:510
  (2 shorter events, 0.0 us)
Async XLA Ops:
  2.2 15.2 %collective-permute-start.1 = (bf16[6,256,128]{2,1,0:T(8,128)(2,1)S(1)}, bf16[6,256,128]{2,1,0:T(8,128)(2,1)S(1)}, u32[]{:S(2)}, u32[]{:S(2)}) collective-permute-start(bf16[6,256,128]{2,1,0:T(8,128)(2,1)S(1)} %get-tuple-element.88), channel_id=1, source_target_pairs={{0,224},{32,0},{64,32},{96,64},{128,96},{160,128},{192,160},{224,1... | collective-permute-start | bytes 1179656 | tf_op jit(solution)/shard_map/ppermute | solution.py:552
  8.1 9.2 %collective-permute-start = (bf16[4,256,128]{2,1,0:T(8,128)(2,1)S(1)}, bf16[4,256,128]{2,1,0:T(8,128)(2,1)S(1)}, u32[]{:S(2)}, u32[]{:S(2)}) collective-permute-start(bf16[4,256,128]{2,1,0:T(8,128)(2,1)S(1)} %get-tuple-element.87), channel_id=1, source_target_pairs={{0,32},{32,64},{64,96},{96,128},{128,160},{160,192},{192,224},{224... | collective-permute-start | bytes 786440 | tf_op jit(solution)/shard_map/ppermute | solution.py:552
  23.1 2.7 %collective-permute-start.2 = (bf16[2,16,112,128]{3,2,1,0:T(8,128)(2,1)S(1)}, bf16[2,16,112,128]{3,2,1,0:T(8,128)(2,1)S(1)}, u32[]{:S(2)}, u32[]{:S(2)}) collective-permute-start(bf16[2,16,112,128]{3,2,1,0:T(8,128)(2,1)S(1)} %get-tuple-element.120), channel_id=1, source_target_pairs={{0,1},{1,0},{2,3},{3,2},{4,5},{5,4},{6,7},{7,6},{8,9},{9,8},{10,11... | collective-permute-start | bytes 2752520 | tf_op jit(solution)/shard_map/ppermute | solution.py:536
  26.0 7.7 %collective-permute-start.3 = (bf16[2,4,112,128]{3,2,1,0:T(8,128)(2,1)S(1)}, bf16[2,4,112,128]{3,2,1,0:T(8,128)(2,1)S(1)}, u32[]{:S(2)}, u32[]{:S(2)}) collective-permute-start(bf16[2,4,112,128]{3,2,1,0:T(8,128)(2,1)S(1)} %get-tuple-element.129), channel_id=1, source_target_pairs={{0,4},{1,17},{2,6},{3,19},{4,0},{5,21},{6,2},{7,23},{8,12},{9,25},... | collective-permute-start | bytes 688136 | tf_op jit(solution)/shard_map/ppermute | solution.py:536
  28.2 7.9 %collective-permute-start.4 = (bf16[2,4,112,128]{3,2,1,0:T(8,128)(2,1)S(1)}, bf16[2,4,112,128]{3,2,1,0:T(8,128)(2,1)S(1)}, u32[]{:S(2)}, u32[]{:S(2)}) collective-permute-start(bf16[2,4,112,128]{3,2,1,0:T(8,128)(2,1)S(1)} %get-tuple-element.130), channel_id=1, source_target_pairs={{0,2},{1,9},{2,4},{3,11},{4,6},{5,13},{6,0},{7,15},{8,10},{9,17},{... | collective-permute-start | bytes 688136 | tf_op jit(solution)/shard_map/ppermute | solution.py:536
  28.2 7.9 %collective-permute-start.5 = (bf16[2,4,112,128]{3,2,1,0:T(8,128)(2,1)S(1)}, bf16[2,4,112,128]{3,2,1,0:T(8,128)(2,1)S(1)}, u32[]{:S(2)}, u32[]{:S(2)}) collective-permute-start(bf16[2,4,112,128]{3,2,1,0:T(8,128)(2,1)S(1)} %get-tuple-element.131), channel_id=1, source_target_pairs={{0,6},{1,25},{2,0},{3,27},{4,2},{5,29},{6,4},{7,31},{8,14},{9,1},{... | collective-permute-start | bytes 688136 | tf_op jit(solution)/shard_map/ppermute | solution.py:536
  36.3 9.3 %collective-permute-start.6 = (bf16[2,112,128]{2,1,0:T(8,128)(2,1)S(1)}, bf16[2,112,128]{2,1,0:T(8,128)(2,1)S(1)}, u32[]{:S(2)}, u32[]{:S(2)}) collective-permute-start(bf16[2,112,128]{2,1,0:T(8,128)(2,1)S(1)} %get-tuple-element.142), channel_id=1, source_target_pairs={{0,16},{1,5},{2,18},{3,7},{4,20},{5,1},{6,22},{7,3},{8,24},{9,13},... | collective-permute-start | bytes 172040 | tf_op jit(solution)/shard_map/ppermute | solution.py:536
  39.6 6.1 %collective-permute-start.7 = (bf16[2,112,128]{2,1,0:T(8,128)(2,1)S(1)}, bf16[2,112,128]{2,1,0:T(8,128)(2,1)S(1)}, u32[]{:S(2)}, u32[]{:S(2)}) collective-permute-start(bf16[2,112,128]{2,1,0:T(8,128)(2,1)S(1)} %get-tuple-element.143), channel_id=1, source_target_pairs={{0,8},{1,3},{2,10},{3,5},{4,12},{5,7},{6,14},{7,1},{8,16},{9,11},{... | collective-permute-start | bytes 172040 | tf_op jit(solution)/shard_map/ppermute | solution.py:536
  40.3 5.4 %collective-permute-start.8 = (bf16[2,112,128]{2,1,0:T(8,128)(2,1)S(1)}, bf16[2,112,128]{2,1,0:T(8,128)(2,1)S(1)}, u32[]{:S(2)}, u32[]{:S(2)}) collective-permute-start(bf16[2,112,128]{2,1,0:T(8,128)(2,1)S(1)} %get-tuple-element.144), channel_id=1, source_target_pairs={{0,24},{1,7},{2,26},{3,1},{4,28},{5,3},{6,30},{7,5},{8,0},{9,15},{... | collective-permute-start | bytes 172040 | tf_op jit(solution)/shard_map/ppermute | solution.py:536
  45.7 4.3 %collective-permute-start.9 = (bf16[2,112,128]{2,1,0:T(8,128)(2,1)S(1)}, bf16[2,112,128]{2,1,0:T(8,128)(2,1)S(1)}, u32[]{:S(2)}, u32[]{:S(2)}) collective-permute-start(bf16[2,112,128]{2,1,0:T(8,128)(2,1)S(1)} %shard_map.92.keep_ref), channel_id=1, source_target_pairs={{0,32},{32,0},{64,96},{96,64},{128,160},{160,128},{192,224},{224,1... | collective-permute-start | bytes 172040 | tf_op jit(solution)/shard_map/ppermute | solution.py:552
  50.0 9.7 %collective-permute-start.12 = (bf16[2,112,128]{2,1,0:T(8,128)(2,1)S(1)}, bf16[2,112,128]{2,1,0:T(8,128)(2,1)S(1)}, u32[]{:S(2)}, u32[]{:S(2)}) collective-permute-start(bf16[2,112,128]{2,1,0:T(8,128)(2,1)S(1)} %shard_map.94.refs_0_), channel_id=1, source_target_pairs={{0,160},{32,128},{64,224},{96,192},{128,32},{160,0},{192,96},{224,... | collective-permute-start | bytes 172040 | tf_op jit(solution)/shard_map/ppermute | solution.py:552
  53.2 6.5 %collective-permute-start.11 = (bf16[2,112,128]{2,1,0:T(8,128)(2,1)S(1)}, bf16[2,112,128]{2,1,0:T(8,128)(2,1)S(1)}, u32[]{:S(2)}, u32[]{:S(2)}) collective-permute-start(bf16[2,112,128]{2,1,0:T(8,128)(2,1)S(1)} %shard_map.94.refs_0_), channel_id=1, source_target_pairs={{0,192},{32,96},{64,0},{96,160},{128,64},{160,224},{192,128},{224,... | collective-permute-start | bytes 172040 | tf_op jit(solution)/shard_map/ppermute | solution.py:552
  55.0 5.4 %collective-permute-start.10 = (bf16[2,112,128]{2,1,0:T(8,128)(2,1)S(1)}, bf16[2,112,128]{2,1,0:T(8,128)(2,1)S(1)}, u32[]{:S(2)}, u32[]{:S(2)}) collective-permute-start(bf16[2,112,128]{2,1,0:T(8,128)(2,1)S(1)} %shard_map.94.refs_0_), channel_id=1, source_target_pairs={{0,224},{32,64},{64,32},{96,128},{128,96},{160,192},{192,160},{224... | collective-permute-start | bytes 172040 | tf_op jit(solution)/shard_map/ppermute | solution.py:552
